TPU v7x, 32 devices: a whole 2x2x4 slice. The times are simulated.
32 devices in a mesh: gx: 4 (over x, core), gy: 4 (over z), gz: 2 (over y).
Axes of the slice: x: 2, y: 2, z: 4, core: 2. Of those that a mesh axis runs over, the one named last changes fastest.
Arguments:
- prior_basis: float32 [16, 64, 3072], P('gx', 'gy', 'gz'), may hold values from -6 to 6
- edge_weights: float32 [3, 16, 64, 32], P(None, 'gx', 'gy', 'gz'), may hold values from 0.5 to 1.5
- spectral_shift: float32 [1], replicated, may hold values from 0.5 to 4
Outputs:
- new_basis: float32 [16, 64, 4096], P('gx', 'gy', 'gz')
- projection: float32 [96, 128], replicated
- triangle: float32 [128, 128], replicated
All inputs are finite; a program needn't handle non-finite values.
Results may differ from a plain program's by a relative error of at most 0.002.
Values sent between devices are 32-bit elements; how exact they have to be, the bound alone decides.
No kernel may reach another device: no remote copies, remote signals or barrier semaphores. Data moves between devices by JAX's collectives and lax.ppermute only.
A program may use at most 64 MiB of HBM per device.

v0:
```python
import jax
import jax.numpy as jnp
from jax import lax
from jax.sharding import PartitionSpec as P

BLOCK = 32
POWERS = 4
BASIS = 96


PRECISE = lax.Precision.HIGHEST
OPERATOR_SCALE = 11.0


def with_halo(block, sides, width):
    for axis, dim in sides:
        count = lax.axis_size(axis)
        forward = [(i, i + 1) for i in range(count - 1)]
        backward = [(target, source) for source, target in forward]
        low = lax.ppermute(
            lax.slice_in_dim(block, block.shape[dim] - width, None, axis=dim), axis, forward
        )
        high = lax.ppermute(lax.slice_in_dim(block, 0, width, axis=dim), axis, backward)
        block = jnp.concatenate([low, block, high], axis=dim)
    return block


def crop_margin(values, layers, columns):
    if layers == 0:
        return values
    return values[
        ...,
        layers : values.shape[-3] - layers,
        layers : values.shape[-2] - layers,
        layers * columns : values.shape[-1] - layers * columns,
    ]


def stencil(padded, weight_pad, shift_value, columns):
    centre = crop_margin(padded, 1, columns)
    inner_weights = crop_margin(weight_pad, 1, columns)
    below_x = weight_pad[0, :-2, 1:-1, columns:-columns]
    below_y = weight_pad[1, 1:-1, :-2, columns:-columns]
    below_z = weight_pad[2, 1:-1, 1:-1, : -2 * columns]
    summed = inner_weights[0] * (centre - padded[2:, 1:-1, columns:-columns]) + below_x * (
        centre - padded[:-2, 1:-1, columns:-columns]
    )
    summed = (
        summed
        + inner_weights[1] * (centre - padded[1:-1, 2:, columns:-columns])
        + below_y * (centre - padded[1:-1, :-2, columns:-columns])
    )
    summed = (
        summed
        + inner_weights[2] * (centre - padded[1:-1, 1:-1, 2 * columns :])
        + below_z * (centre - padded[1:-1, 1:-1, : -2 * columns])
    )
    return (summed + shift_value * centre) / OPERATOR_SCALE - centre


def line_inside(local_count, margin, position, device_count):
    positions = (
        jnp.arange(local_count + 2 * margin, dtype=jnp.int32) + position * local_count - margin
    )
    return ((positions >= 0) & (positions < local_count * device_count)).astype(jnp.float32)


def per_device(prior_basis, edge_weights, spectral_shift):
    size_x = prior_basis.shape[0]
    size_y = prior_basis.shape[1]
    size_z = prior_basis.shape[2] // BASIS
    cell_local = size_x * size_y * size_z
    cell_count = cell_local * lax.axis_size("gx") * lax.axis_size("gy") * lax.axis_size("gz")
    shift_value = spectral_shift[0]
    basis_rows = prior_basis.reshape(cell_local, BASIS)
    start_block = prior_basis.reshape(size_x, size_y, size_z, BASIS)[..., BASIS - BLOCK :]
    weight_pad = with_halo(edge_weights, (("gx", 1), ("gy", 2), ("gz", 3)), POWERS)
    weight_pad = jnp.repeat(weight_pad, BLOCK, axis=3)
    padded = with_halo(start_block, (("gx", 0), ("gy", 1), ("gz", 2)), POWERS)
    padded = padded.reshape(size_x + 2 * POWERS, size_y + 2 * POWERS, (size_z + 2 * POWERS) * BLOCK)
    inside_x = line_inside(size_x, POWERS, lax.axis_index("gx"), lax.axis_size("gx"))
    inside_y = line_inside(size_y, POWERS, lax.axis_index("gy"), lax.axis_size("gy"))
    inside_z = jnp.repeat(
        line_inside(size_z, POWERS, lax.axis_index("gz"), lax.axis_size("gz")), BLOCK
    )
    inside = inside_x[:, None, None] * inside_y[None, :, None] * inside_z[None, None, :]
    previous = padded
    current = stencil(padded, weight_pad, shift_value, BLOCK) * crop_margin(inside, 1, BLOCK)
    powers = [crop_margin(current, POWERS - 1, BLOCK).reshape(size_x, size_y, size_z, BLOCK)]
    for degree in range(1, POWERS):
        following = 2.0 * stencil(
            current, crop_margin(weight_pad, degree, BLOCK), shift_value, BLOCK
        ) - crop_margin(previous, 2, BLOCK)
        following = following * crop_margin(inside, degree + 1, BLOCK)
        previous, current = (current, following)
        powers.append(
            crop_margin(following, POWERS - 1 - degree, BLOCK).reshape(
                size_x, size_y, size_z, BLOCK
            )
        )
    krylov = jnp.stack(powers, axis=3).reshape(cell_local, BLOCK * POWERS)
    first_coef = (
        lax.psum(jnp.dot(basis_rows.T, krylov, precision=PRECISE), ("gx", "gy", "gz")) / cell_count
    )
    once = krylov - jnp.dot(basis_rows, first_coef, precision=PRECISE)
    second_coef = (
        lax.psum(jnp.dot(basis_rows.T, once, precision=PRECISE), ("gx", "gy", "gz")) / cell_count
    )
    twice = once - jnp.dot(basis_rows, second_coef, precision=PRECISE)
    gram_matrix = (
        lax.psum(jnp.dot(twice.T, twice, precision=PRECISE), ("gx", "gy", "gz")) / cell_count
    )
    lower_factor = jnp.linalg.cholesky(gram_matrix)
    solved = jax.scipy.linalg.solve_triangular(lower_factor, twice.T, lower=True)
    new_basis = solved.T.reshape(size_x, size_y, size_z * BLOCK * POWERS)
    return (new_basis, first_coef + second_coef, lower_factor.T)


def solution(mesh):
    return jax.shard_map(
        per_device,
        mesh=mesh,
        in_specs=(P("gx", "gy", "gz"), P(None, "gx", "gy", "gz"), P()),
        out_specs=(P("gx", "gy", "gz"), P(), P()),
        check_vma=False,
    )
```

profile of v0, /device:TPU:0, one launch (start us, length us, event | category | flops | bytes accessed | tf_op | source)
XLA Modules:
  0.0 330.9 jit_solution(15191813122158639890)
XLA Ops:
  7.2 1.2 reshape.86
  8.4 0.2 slice.326
  8.6 2.4 collective-permute-start.6
  11.0 1.3 collective-permute-start.7
  12.3 5.1 %collective-permute-start = (f32[3,4,16,16]{3,2,1,0:T(8,128)}, f32[3,4,16,16]{3,2,1,0:T(8,128)S(1)}, u32[]{:S(2)}, u32[]{:S(2)}) collective-permute-start(f32[3,4,16,16]{3,2,1,0:T(8,128)} %param.4), channel_id=1, source_target_pairs={{0,8},{8,16},{16,24},{1,9},{9,17},{17,25},{2,10},{10,18},{18,26},{... | collective-permute-start | bytes 36872 | tf_op jit(solution)/shard_map/ppermute | solution.py:20
  17.4 1.3 collective-permute-start.1
  18.8 0.1 broadcast_multiply_fusion.2
  18.9 0.9 constant_dynamic-update-slice_fusion.1
  19.8 2.3 collective-permute-done.1
  22.1 3.5 %collective-permute-start.2 = (f32[3,12,4,16]{3,2,1,0:T(4,128)S(1)}, f32[3,12,4,16]{3,2,1,0:T(4,128)S(1)}, u32[]{:S(2)}, u32[]{:S(2)}) collective-permute-start(f32[3,12,4,16]{3,2,1,0:T(4,128)S(1)} %get-tuple-element.18), channel_id=1, source_target_pairs={{0,2},{2,4},{4,6},{1,3},{3,5},{5,7},{8,10},{10,12},{12,14},{9,11},... | collective-permute-start | bytes 27656 | tf_op jit(solution)/shard_map/ppermute | solution.py:20
  25.6 1.3 collective-permute-start.3
  27.0 0.1 mul.183
  27.1 0.5 collective-permute-done.2
  27.6 4.3 %collective-permute-done.3 = f32[3,12,4,16]{3,2,1,0:T(4,128)S(1)} collective-permute-done((f32[3,12,4,16]{3,2,1,0:T(4,128)S(1)}, f32[3,12,4,16]{3,2,1,0:T(4,128)S(1)}, u32[]{:S(2)}, u32[]{:S(2)}) %collective-permute-start.3) | collective-permute-done | bytes 9248 | tf_op jit(solution)/shard_map/ppermute | solution.py:23
  31.9 0.1 pad_maximum_fusion.7
  32.1 3.6 %collective-permute-start.8 = (f32[12,4,16,32]{3,2,1,0:T(8,128)S(1)}, f32[12,4,16,32]{3,2,1,0:T(8,128)S(1)}, u32[]{:S(2)}, u32[]{:S(2)}) collective-permute-start(f32[12,4,16,32]{3,2,1,0:T(8,128)S(1)} %get-tuple-element.11), channel_id=1, source_target_pairs={{0,2},{2,4},{4,6},{1,3},{3,5},{5,7},{8,10},{10,12},{12,14},{9,11},... | collective-permute-start | bytes 294920 | tf_op jit(solution)/shard_map/ppermute | solution.py:20
  35.7 1.3 collective-permute-start.9
  37.0 1.0 fusion.73
  38.1 3.4 %collective-permute-start.4 = (f32[3,12,24,4]{3,2,1,0:T(8,128)}, f32[3,12,24,4]{3,2,1,0:T(8,128)S(1)}, u32[]{:S(2)}, u32[]{:S(2)}) collective-permute-start(f32[3,12,24,4]{3,2,1,0:T(8,128)} %get-tuple-element.15), channel_id=1, source_target_pairs={{0,1},{2,3},{4,5},{6,7},{8,9},{10,11},{12,13},{14,15},{16,17},{18,... | collective-permute-start | bytes 41480 | tf_op jit(solution)/shard_map/ppermute | solution.py:20
  41.5 1.3 collective-permute-start.5
  42.8 1.5 collective-permute-done.8
  44.4 4.7 %collective-permute-done.9 = f32[12,4,16,32]{3,2,1,0:T(8,128)S(1)} collective-permute-done((f32[12,4,16,32]{3,2,1,0:T(8,128)S(1)}, f32[12,4,16,32]{3,2,1,0:T(8,128)S(1)}, u32[]{:S(2)}, u32[]{:S(2)}) %collective-permute-start.9) | collective-permute-done | bytes 98336 | tf_op jit(solution)/shard_map/ppermute | solution.py:23
  49.1 1.4 pad_maximum_fusion.6
  50.5 4.3 %collective-permute-start.10 = (f32[12,24,4,32]{3,2,1,0:T(4,128)}, f32[12,24,4,32]{3,2,1,0:T(4,128)}, u32[]{:S(2)}, u32[]{:S(2)}) collective-permute-start(f32[12,24,4,32]{3,2,1,0:T(4,128)} %get-tuple-element.9), channel_id=1, source_target_pairs={{0,1},{2,3},{4,5},{6,7},{8,9},{10,11},{12,13},{14,15},{16,17},{18,... | collective-permute-start | bytes 442376 | tf_op jit(solution)/shard_map/ppermute | solution.py:20
  54.7 1.3 collective-permute-start.11
  56.0 1.1 broadcast_multiply_fusion
  57.1 1.0 reshape.89
  58.7 1.4 pad_maximum_fusion.8
  60.1 5.9 %broadcast_in_dim.10 = f32[3,12,24,24,32]{4,3,2,1,0:T(8,128)} broadcast(f32[3,12,24,24]{3,2,1,0:T(8,128)S(1)} %pad_maximum_fusion.8), dimensions={0,1,2,3} | broadcast | bytes 2737152 | tf_op jit(solution)/shard_map/broadcast_in_dim | solution.py:78
  66.1 6.6 %reshape.85 = f32[3,12,24,768]{3,2,1,0:T(8,128)S(1)} reshape(f32[3,12,24,24,32]{4,3,2,1,0:T(8,128)} %broadcast_in_dim.10) | data formatting | bytes 5308416 | tf_op jit(solution)/shard_map/reshape | solution.py:78
  72.7 4.3 %pad_maximum_fusion = f32[12,24,24,32]{3,2,1,0:T(8,128)} fusion(f32[12,24,4,32]{3,2,1,0:T(4,128)} %collective-permute-done.11, f32[12,4,16,32]{3,2,1,0:T(8,128)} %copy-done.6, f32[4,16,16,32]{3,2,1,0:T(8,128)} %copy-done.3, f32[4,16,16,32]{3,2,1,0:T(8,128)S(1)} %slice.326, f32[4,16,16,32]{3,2,1,0:T(8,128)} %copy-done.2, f32[12,4,16,32]{3,2,1,0:T(8,128)} %copy-done.5, ...), kind=kLoop, calls=%fused_computation | loop fusion | flops 1327104 | bytes 1769472 | tf_op jit(solution)/shard_map/concatenate | solution.py:24
  77.0 2.7 reshape.87
  79.7 3.6 %slice_multiply_fusion = f32[10,22,704]{2,1,0:T(8,128)S(1)} fusion(f32[12,24,768]{2,1,0:T(8,128)} %broadcast_multiply_fusion, f32[12,24,768]{2,1,0:T(8,128)S(1)} %reshape.87, f32[3,12,24,768]{3,2,1,0:T(8,128)S(1)} %reshape.85, f32[]{:T(128)} %bitcast.133), kind=kLoop, calls=%fused_computation.8 | loop fusion | flops 3407360 | bytes 9292804 | tf_op jit(solution)/shard_map/mul | solution.py:88
  83.3 0.8 slice.340
  84.1 1.9 slice_multiply_fusion.1
  86.0 1.4 slice_multiply_fusion.2
  87.4 0.4 fusion.72
  87.8 0.2 stack_reshape.13
  88.0 0.2 stack_reshape.14
  88.1 0.2 stack_reshape.15
  88.3 0.2 stack_reshape.12
  88.5 0.2 pad_maximum_fusion.1
  88.7 1.4 copy.9
  90.1 0.9 reshape.88
  91.0 0.2 copy.10
  91.2 1.0 convolution_bitcast_fusion.3
  92.2 41.5 %psum.21 = f32[96,128]{1,0:T(8,128)S(1)} all-reduce(f32[96,128]{1,0:T(8,128)S(1)} %convolution_bitcast_fusion.3), channel_id=1, replica_groups=mesh['gx'=4,'gy'=4,'gz'=2] {'gx','gy','gz'}, use_global_device_ids=true, to_apply=%region_0.0 | all-reduce | flops 12288 | bytes 98304 | tf_op jit(solution)/shard_map/psum | solution.py:103
  133.7 0.6 fusion
  134.4 1.0 convolution_bitcast_fusion.2
  135.3 40.6 %psum.22 = f32[96,128]{1,0:T(8,128)S(1)} all-reduce(f32[96,128]{1,0:T(8,128)S(1)} %convolution_bitcast_fusion.2), channel_id=1, replica_groups=mesh['gx'=4,'gy'=4,'gz'=2] {'gx','gy','gz'}, use_global_device_ids=true, to_apply=%region_1.0 | all-reduce | flops 12288 | bytes 98304 | tf_op jit(solution)/shard_map/psum | solution.py:107
  175.9 0.6 fusion.1
  176.6 1.2 fusion.75
  177.8 0.6 multiply_add_fusion
  178.5 118.3 %all-reduce.2.cloned.1.call-done = f32[128,128]{0,1:T(8,128)} async-done(((f32[128,128]{0,1:T(8,128)}), f32[128,128]{0,1:T(8,128)}) %all-reduce.2.cloned.1.call-update) | async-done | bytes 65552 | tf_op jit(solution)/shard_map/psum | solution.py:111
  296.7 0.8 broadcast_multiply_fusion.1
  297.6 0.1 copy.12
  297.7 0.9 fusion.64
  298.5 11.7 %cholesky.16 = f32[128,128]{1,0:T(8,128)S(1)} custom-call(f32[128,128]{1,0:T(8,128)S(1)} %fusion.64), custom_call_target="Cholesky" | custom-call | tf_op jit(solution)/shard_map/jit(cholesky)/cholesky | solution.py:113
  310.3 0.6 compare_reduce_fusion
  310.9 0.7 fusion.65
  311.6 9.8 %custom-call.7 = f32[1,128,128]{1,2,0:T(8,128)S(1)} custom-call(f32[1,128,128]{2,1,0:T(8,128)S(1)} %get-tuple-element.21), custom_call_target="InvertDiagBlocksLowerTriangular" | custom-call | tf_op jit(solution)/shard_map/jit(_solve_triangular)/triangular_solve | solution.py:114
  321.4 1.0 fusion.62
  322.4 0.9 reshape.90
  323.3 0.7 copy.13
  (34 shorter events, 0.4 us)
Async XLA Ops:
  7.2 289.6 %all-reduce.2.cloned.1.call-start = ((), (), s32[]{:S(2)}) async-start(), calls=%async_computation | async-start | bytes 131072 | tf_op jit(solution)/shard_map/psum | solution.py:111
  8.6 23.4 %collective-permute-start.6 = (f32[4,16,16,32]{3,2,1,0:T(8,128)S(1)}, f32[4,16,16,32]{3,2,1,0:T(8,128)S(1)}, u32[]{:S(2)}, u32[]{:S(2)}) collective-permute-start(f32[4,16,16,32]{3,2,1,0:T(8,128)S(1)} %slice.326), channel_id=1, source_target_pairs={{0,8},{8,16},{16,24},{1,9},{9,17},{17,25},{2,10},{10,18},{18,26},{... | collective-permute-start | bytes 393224 | tf_op jit(solution)/shard_map/ppermute | solution.py:20
  11.0 20.9 %collective-permute-start.7 = (f32[4,16,16,32]{3,2,1,0:T(8,128)S(1)}, f32[4,16,16,32]{3,2,1,0:T(8,128)S(1)}, u32[]{:S(2)}, u32[]{:S(2)}) collective-permute-start(f32[4,16,16,32]{3,2,1,0:T(8,128)S(1)} %slice.326), channel_id=1, source_target_pairs={{8,0},{16,8},{24,16},{9,1},{17,9},{25,17},{10,2},{18,10},{26,18},{... | collective-permute-start | bytes 393224 | tf_op jit(solution)/shard_map/ppermute | solution.py:23
  12.3 6.5 %collective-permute-start = (f32[3,4,16,16]{3,2,1,0:T(8,128)}, f32[3,4,16,16]{3,2,1,0:T(8,128)S(1)}, u32[]{:S(2)}, u32[]{:S(2)}) collective-permute-start(f32[3,4,16,16]{3,2,1,0:T(8,128)} %param.4), channel_id=1, source_target_pairs={{0,8},{8,16},{16,24},{1,9},{9,17},{17,25},{2,10},{10,18},{18,26},{... | collective-permute-start | bytes 36872 | tf_op jit(solution)/shard_map/ppermute | solution.py:20
  17.4 4.6 %collective-permute-start.1 = (f32[3,4,16,16]{3,2,1,0:T(8,128)}, f32[3,4,16,16]{3,2,1,0:T(8,128)S(1)}, u32[]{:S(2)}, u32[]{:S(2)}) collective-permute-start(f32[3,4,16,16]{3,2,1,0:T(8,128)} %param.4), channel_id=1, source_target_pairs={{8,0},{16,8},{24,16},{9,1},{17,9},{25,17},{10,2},{18,10},{26,18},{... | collective-permute-start | bytes 36872 | tf_op jit(solution)/shard_map/ppermute | solution.py:23
  22.1 5.5 %collective-permute-start.2 = (f32[3,12,4,16]{3,2,1,0:T(4,128)S(1)}, f32[3,12,4,16]{3,2,1,0:T(4,128)S(1)}, u32[]{:S(2)}, u32[]{:S(2)}) collective-permute-start(f32[3,12,4,16]{3,2,1,0:T(4,128)S(1)} %get-tuple-element.18), channel_id=1, source_target_pairs={{0,2},{2,4},{4,6},{1,3},{3,5},{5,7},{8,10},{10,12},{12,14},{9,11},... | collective-permute-start | bytes 27656 | tf_op jit(solution)/shard_map/ppermute | solution.py:20
  25.6 6.2 %collective-permute-start.3 = (f32[3,12,4,16]{3,2,1,0:T(4,128)S(1)}, f32[3,12,4,16]{3,2,1,0:T(4,128)S(1)}, u32[]{:S(2)}, u32[]{:S(2)}) collective-permute-start(f32[3,12,4,16]{3,2,1,0:T(4,128)S(1)} %get-tuple-element.19), channel_id=1, source_target_pairs={{2,0},{4,2},{6,4},{3,1},{5,3},{7,5},{10,8},{12,10},{14,12},{11,9},... | collective-permute-start | bytes 27656 | tf_op jit(solution)/shard_map/ppermute | solution.py:23
  32.0 28.2 %copy-start.2 = (f32[4,16,16,32]{3,2,1,0:T(8,128)}, f32[4,16,16,32]{3,2,1,0:T(8,128)S(1)}, u32[]{:S(2)}) copy-start(f32[4,16,16,32]{3,2,1,0:T(8,128)S(1)} %collective-permute-done.6) | copy-start | bytes 393220
  32.0 18.5 %copy-start.3 = (f32[4,16,16,32]{3,2,1,0:T(8,128)}, f32[4,16,16,32]{3,2,1,0:T(8,128)S(1)}, u32[]{:S(2)}) copy-start(f32[4,16,16,32]{3,2,1,0:T(8,128)S(1)} %collective-permute-done.7) | copy-start | bytes 393220
  32.1 25.0 %copy-start.4 = (f32[4,16,1536]{2,1,0:T(8,128)S(1)}, f32[4,16,1536]{2,1,0:T(8,128)}, u32[]{:S(2)}) copy-start(f32[4,16,1536]{2,1,0:T(8,128)} %param.3) | copy-start | bytes 1179652
  32.1 12.3 %collective-permute-start.8 = (f32[12,4,16,32]{3,2,1,0:T(8,128)S(1)}, f32[12,4,16,32]{3,2,1,0:T(8,128)S(1)}, u32[]{:S(2)}, u32[]{:S(2)}) collective-permute-start(f32[12,4,16,32]{3,2,1,0:T(8,128)S(1)} %get-tuple-element.11), channel_id=1, source_target_pairs={{0,2},{2,4},{4,6},{1,3},{3,5},{5,7},{8,10},{10,12},{12,14},{9,11},... | collective-permute-start | bytes 294920 | tf_op jit(solution)/shard_map/ppermute | solution.py:20
  35.7 13.3 %collective-permute-start.9 = (f32[12,4,16,32]{3,2,1,0:T(8,128)S(1)}, f32[12,4,16,32]{3,2,1,0:T(8,128)S(1)}, u32[]{:S(2)}, u32[]{:S(2)}) collective-permute-start(f32[12,4,16,32]{3,2,1,0:T(8,128)S(1)} %get-tuple-element.12), channel_id=1, source_target_pairs={{2,0},{4,2},{6,4},{3,1},{5,3},{7,5},{10,8},{12,10},{14,12},{11,9},... | collective-permute-start | bytes 294920 | tf_op jit(solution)/shard_map/ppermute | solution.py:23
  38.1 20.6 %collective-permute-start.4 = (f32[3,12,24,4]{3,2,1,0:T(8,128)}, f32[3,12,24,4]{3,2,1,0:T(8,128)S(1)}, u32[]{:S(2)}, u32[]{:S(2)}) collective-permute-start(f32[3,12,24,4]{3,2,1,0:T(8,128)} %get-tuple-element.15), channel_id=1, source_target_pairs={{0,1},{2,3},{4,5},{6,7},{8,9},{10,11},{12,13},{14,15},{16,17},{18,... | collective-permute-start | bytes 41480 | tf_op jit(solution)/shard_map/ppermute | solution.py:20
  41.5 17.2 %collective-permute-start.5 = (f32[3,12,24,4]{3,2,1,0:T(8,128)}, f32[3,12,24,4]{3,2,1,0:T(8,128)}, u32[]{:S(2)}, u32[]{:S(2)}) collective-permute-start(f32[3,12,24,4]{3,2,1,0:T(8,128)} %get-tuple-element.16), channel_id=1, source_target_pairs={{1,0},{3,2},{5,4},{7,6},{9,8},{11,10},{13,12},{15,14},{17,16},{19,... | collective-permute-start | bytes 41480 | tf_op jit(solution)/shard_map/ppermute | solution.py:23
  44.4 14.4 %copy-start.5 = (f32[12,4,16,32]{3,2,1,0:T(8,128)}, f32[12,4,16,32]{3,2,1,0:T(8,128)S(1)}, u32[]{:S(2)}) copy-start(f32[12,4,16,32]{3,2,1,0:T(8,128)S(1)} %collective-permute-done.8) | copy-start | bytes 294916
  49.1 1.4 copy-start.6
  50.5 22.2 %collective-permute-start.10 = (f32[12,24,4,32]{3,2,1,0:T(4,128)}, f32[12,24,4,32]{3,2,1,0:T(4,128)}, u32[]{:S(2)}, u32[]{:S(2)}) collective-permute-start(f32[12,24,4,32]{3,2,1,0:T(4,128)} %get-tuple-element.9), channel_id=1, source_target_pairs={{0,1},{2,3},{4,5},{6,7},{8,9},{10,11},{12,13},{14,15},{16,17},{18,... | collective-permute-start | bytes 442376 | tf_op jit(solution)/shard_map/ppermute | solution.py:20
  54.7 18.0 %collective-permute-start.11 = (f32[12,24,4,32]{3,2,1,0:T(4,128)}, f32[12,24,4,32]{3,2,1,0:T(4,128)}, u32[]{:S(2)}, u32[]{:S(2)}) collective-permute-start(f32[12,24,4,32]{3,2,1,0:T(4,128)} %get-tuple-element.10), channel_id=1, source_target_pairs={{1,0},{3,2},{5,4},{7,6},{9,8},{11,10},{13,12},{15,14},{17,16},{19,... | collective-permute-start | bytes 442376 | tf_op jit(solution)/shard_map/ppermute | solution.py:23
  79.7 4.4 %copy-start.1 = (f32[12,24,768]{2,1,0:T(8,128)S(1)}, f32[12,24,768]{2,1,0:T(8,128)}, u32[]{:S(2)}) copy-start(f32[12,24,768]{2,1,0:T(8,128)} %broadcast_multiply_fusion) | copy-start | bytes 2654212
  87.4 0.9 copy-start.7
  88.7 2.5 copy-start
Sparse Core Ops, SparseCore 0:
  178.0 118.7 all-reduce.1
where the time goes:
time: 333 us; the launch traced here: 331 us
  waiting for transfers between devices  132 us (40%)
  blocking collectives  82.1 us (25%)
  other arithmetic  41.1 us (12%)
  starting transfers between devices  30.1 us (9%)
  local copies, waits for them, and re-layouts  25.3 us (8%)
  between operations  15.1 us (5%)
  matrix products  5.46 us (2%)
    psum x1, waiting for transfers between devices, per_device(): lax.psum(jnp.dot(twice.T, twice, precision=PRECISE), ('gx', 'gy', 'gz'))  118 us
    psum x1, blocking collectives, per_device(): lax.psum(jnp.dot(basis_rows.T, krylov, precision=PRECISE), ('gx', 'gy', '...  41.5 us
    psum x1, blocking collectives, per_device(): lax.psum(jnp.dot(basis_rows.T, once, precision=PRECISE), ('gx', 'gy', 'gz'))  40.6 us
    ppermute x6, starting transfers between devices, with_halo(): lax.ppermute(lax.slice_in_dim(block, block.shape[dim] - width, None, axis...  22.3 us
    another operation x3, other arithmetic, per_device(): lower_factor = jnp.linalg.cholesky(gram_matrix)  12.4 us
    ppermute x6, waiting for transfers between devices, with_halo(): lax.ppermute(lax.slice_in_dim(block, 0, width, axis=dim), axis, backward)  11.3 us
    another operation x1, other arithmetic, per_device(): jax.scipy.linalg.solve_triangular(lower_factor, twice.T, lower=True)  9.81 us
    ppermute x6, starting transfers between devices, with_halo(): lax.ppermute(lax.slice_in_dim(block, 0, width, axis=dim), axis, backward)  7.74 us
  transfers between devices with their start and end apart: 13, of which 6 were waited for; matrix products, arithmetic and copies ran while one was open for 6% of the time, Pallas kernels for 0%

commit v1 on v0

--- a/solution.py
+++ b/solution.py
@@ -10,6 +10,57 @@
 
 PRECISE = lax.Precision.HIGHEST
 OPERATOR_SCALE = 11.0
+
+
+DEGREE = 6.0
+
+
+def precise(left, right):
+    return jnp.dot(left, right, precision=PRECISE)
+
+
+def basis_change(centre, width):
+    zero = jnp.zeros_like(centre)
+    one = zero + 1.0
+
+    def apply_a(c):
+        up = [zero] + [width * v for v in c[:-1]]
+        down = [width * v for v in c[1:]] + [zero]
+        return [centre * v + u + d for v, u, d in zip(c, up, down)]
+
+    def apply_x(c):
+        out = [zero] * len(c)
+        out[1] = out[1] + c[0]
+        for k in range(1, len(c)):
+            if k + 1 < len(c):
+                out[k + 1] = out[k + 1] + 0.5 * c[k]
+            out[k - 1] = out[k - 1] + 0.5 * c[k]
+        return [(o - centre * v) * (1.0 / width) for o, v in zip(out, c)]
+
+    t = [[one] + [zero] * POWERS]
+    t.append(apply_a(t[0]))
+    s = [[one] + [zero] * POWERS]
+    s.append(apply_x(s[0]))
+    for _ in range(1, POWERS):
+        t.append([2.0 * v - w for v, w in zip(apply_a(t[-1]), t[-2])])
+        s.append([v - w for v, w in zip(apply_x(s[-1]), s[-2])])
+    to_power = jnp.stack([jnp.stack([t[k][j] for k in range(1, POWERS + 1)]) for j in range(1, POWERS + 1)])
+    constant = jnp.stack([t[k][0] for k in range(1, POWERS + 1)])[None]
+    removed = -jnp.stack([s[j][0] for j in range(1, POWERS + 1)])[None]
+    return to_power, constant, removed
+
+
+def total(values):
+    for axis in ("gx", "gz", "gy"):
+        count = lax.axis_size(axis)
+        if count & (count - 1):
+            values = lax.psum(values, axis)
+            continue
+        step = 1
+        while step < count:
+            values = values + lax.ppermute(values, axis, [(i, i ^ step) for i in range(count)])
+            step *= 2
+    return values
 
 
 def with_halo(block, sides, width):
@@ -84,13 +135,19 @@
         line_inside(size_z, POWERS, lax.axis_index("gz"), lax.axis_size("gz")), BLOCK
     )
     inside = inside_x[:, None, None] * inside_y[None, :, None] * inside_z[None, None, :]
+    centre_shift, width = (DEGREE + shift_value) / OPERATOR_SCALE - 1.0, DEGREE**0.5 / OPERATOR_SCALE
+    to_power, constant, removed = basis_change(centre_shift, width)
+
+    def centred(values, degree):
+        weights = crop_margin(weight_pad, degree, BLOCK)
+        result = stencil(values, weights, shift_value, BLOCK)
+        return (result - centre_shift * crop_margin(values, 1, BLOCK)) * (1.0 / width)
+
     previous = padded
-    current = stencil(padded, weight_pad, shift_value, BLOCK) * crop_margin(inside, 1, BLOCK)
+    current = centred(padded, 0) * crop_margin(inside, 1, BLOCK)
     powers = [crop_margin(current, POWERS - 1, BLOCK).reshape(size_x, size_y, size_z, BLOCK)]
     for degree in range(1, POWERS):
-        following = 2.0 * stencil(
-            current, crop_margin(weight_pad, degree, BLOCK), shift_value, BLOCK
-        ) - crop_margin(previous, 2, BLOCK)
+        following = centred(current, degree) - crop_margin(previous, 2, BLOCK)
         following = following * crop_margin(inside, degree + 1, BLOCK)
         previous, current = (current, following)
         powers.append(
@@ -98,22 +155,29 @@
                 size_x, size_y, size_z, BLOCK
             )
         )
-    krylov = jnp.stack(powers, axis=3).reshape(cell_local, BLOCK * POWERS)
-    first_coef = (
-        lax.psum(jnp.dot(basis_rows.T, krylov, precision=PRECISE), ("gx", "gy", "gz")) / cell_count
+    columns = jnp.stack(powers, axis=3).reshape(cell_local, BLOCK * POWERS)
+    joined = jnp.concatenate([basis_rows, columns], axis=1)
+    sums = total(precise(joined.T, joined)) / cell_count
+    inner, cross, square = sums[:BASIS, :BASIS], sums[:BASIS, BASIS:], sums[BASIS:, BASIS:]
+    inner, cross, square = lax.optimization_barrier((inner, cross, square))
+    defect = jnp.eye(BASIS, dtype=jnp.float32) - inner
+    eye = jnp.eye(BLOCK, dtype=jnp.float32)
+    start_defect = precise(defect, defect[:, BASIS - BLOCK :])
+    both = cross + precise(defect, cross)
+    both = lax.optimization_barrier(both)
+    moved = lax.optimization_barrier(both - precise(start_defect, jnp.kron(removed, eye)))
+    mix = jnp.kron(to_power, eye)
+    start_unit = jnp.eye(BASIS, BLOCK, BLOCK - BASIS, dtype=jnp.float32)
+    wide = jnp.concatenate([both, start_unit - start_defect], axis=1)
+    projection = precise(wide, jnp.concatenate([mix, jnp.kron(constant, eye)], axis=0))
+    gram = (
+        square - precise(cross.T, moved) - precise(moved.T, cross - precise(inner, moved))
     )
-    once = krylov - jnp.dot(basis_rows, first_coef, precision=PRECISE)
-    second_coef = (
-        lax.psum(jnp.dot(basis_rows.T, once, precision=PRECISE), ("gx", "gy", "gz")) / cell_count
-    )
-    twice = once - jnp.dot(basis_rows, second_coef, precision=PRECISE)
-    gram_matrix = (
-        lax.psum(jnp.dot(twice.T, twice, precision=PRECISE), ("gx", "gy", "gz")) / cell_count
-    )
-    lower_factor = jnp.linalg.cholesky(gram_matrix)
+    lower_factor = jnp.linalg.cholesky(gram)
+    twice = columns - precise(basis_rows, moved)
     solved = jax.scipy.linalg.solve_triangular(lower_factor, twice.T, lower=True)
     new_basis = solved.T.reshape(size_x, size_y, size_z * BLOCK * POWERS)
-    return (new_basis, first_coef + second_coef, lower_factor.T)
+    return (new_basis, projection, precise(lower_factor.T, mix))
 
 
 def solution(mesh):

time: 333 us -> 158 us (0.47)
  waiting for transfers between devices: 132 us -> 40.7 us
  blocking collectives: 82.1 us -> 0 us
  between operations: 15.1 us -> 1.88 us
  starting transfers between devices: 30.1 us -> 35.4 us
  local copies, waits for them, and re-layouts: 25.3 us -> 29.3 us
    psum x1 -> x0, waiting for transfers between devices: 118 us -> none  [per_device(): lax.psum(jnp.dot(twice.T, twice, precision=PRECISE), ('gx', 'gy', 'gz'))]
    psum x2 -> x0, blocking collectives: 82.1 us -> none  [the longest x1 41.5 us: per_device(): lax.psum(jnp.dot(basis_rows.T, krylov, precision=PRECISE), ('gx', 'gy', '...]
    ppermute x0 -> x5, waiting for transfers between devices: none -> 27.8 us  [total(): lax.ppermute(values, axis, [(i, i ^ step) for i in range(count)])]
    ppermute x0 -> x5, starting transfers between devices: none -> 5.34 us  [total(): lax.ppermute(values, axis, [(i, i ^ step) for i in range(count)])]
    another operation x5 -> x4, local copies, waits for them, and re-layouts: 2.02 us -> 6.09 us  [per_device(): columns = jnp.stack(powers, axis=3).reshape(cell_local, BLOCK * POWERS)]
    another operation x4 -> x8, other arithmetic: 12.6 us -> 16.4 us  [the longest x3 12.4 us: per_device(): lower_factor = jnp.linalg.cholesky(gram)]
    dot_general x5 -> x10, matrix products: 4.47 us -> 6.93 us  [precise(): return jnp.dot(left, right, precision=PRECISE)]
    another operation x1 -> x2, other arithmetic: 9.81 us -> 10.5 us  [per_device(): jax.scipy.linalg.solve_triangular(lower_factor, twice.T, lower=True)]
  transfers between devices with their start and end apart: 13 -> 17, of which waited for: 6 -> 10; matrix products, arithmetic and copies ran while one was open for 6% -> 13% of each run, Pallas kernels for 0% -> 0%
where the time goes in v1:
time: 158 us
  other arithmetic  42.8 us (27%)
  waiting for transfers between devices  40.7 us (26%)
  starting transfers between devices  35.4 us (22%)
  local copies, waits for them, and re-layouts  29.3 us (19%)
  matrix products  7.49 us (5%)
  between operations  1.88 us (1%)
    ppermute x5, waiting for transfers between devices, total(): lax.ppermute(values, axis, [(i, i ^ step) for i in range(count)])  27.8 us
    ppermute x6, starting transfers between devices, with_halo(): lax.ppermute(lax.slice_in_dim(block, block.shape[dim] - width, None, axis...  22.4 us
    another operation x3, other arithmetic, per_device(): lower_factor = jnp.linalg.cholesky(gram)  12.4 us
    ppermute x6, waiting for transfers between devices, with_halo(): lax.ppermute(lax.slice_in_dim(block, 0, width, axis=dim), axis, backward)  11.4 us
    another operation x2, other arithmetic, per_device(): jax.scipy.linalg.solve_triangular(lower_factor, twice.T, lower=True)  10.5 us
    ppermute x6, starting transfers between devices, with_halo(): lax.ppermute(lax.slice_in_dim(block, 0, width, axis=dim), axis, backward)  7.74 us
    dot_general x10, matrix products, precise(): return jnp.dot(left, right, precision=PRECISE)  6.93 us
    reshape x1, local copies, waits for them, and re-layouts, per_device(): weight_pad = jnp.repeat(weight_pad, BLOCK, axis=3)  6.62 us
  transfers between devices with their start and end apart: 17, of which 10 were waited for; matrix products, arithmetic and copies ran while one was open for 13% of the time, Pallas kernels for 0%

profile of v1, /device:TPU:0, one launch (start us, length us, event | category | flops | bytes accessed | tf_op | source)
XLA Modules:
  0.0 157.7 jit_solution(16899995667622873441)
XLA Ops:
  0.6 1.2 reshape.154
  1.8 0.2 slice.346
  2.0 2.4 %collective-permute-start.6 = (f32[4,16,16,32]{3,2,1,0:T(8,128)S(1)}, f32[4,16,16,32]{3,2,1,0:T(8,128)S(1)}, u32[]{:S(2)}, u32[]{:S(2)}) collective-permute-start(f32[4,16,16,32]{3,2,1,0:T(8,128)S(1)} %slice.346), channel_id=1, source_target_pairs={{0,8},{8,16},{16,24},{1,9},{9,17},{17,25},{2,10},{10,18},{18,26},{... | collective-permute-start | bytes 393224 | tf_op jit(solution)/shard_map/ppermute | solution.py:71
  4.4 1.3 collective-permute-start.7
  5.7 5.1 %collective-permute-start = (f32[3,4,16,16]{3,2,1,0:T(8,128)}, f32[3,4,16,16]{3,2,1,0:T(8,128)S(1)}, u32[]{:S(2)}, u32[]{:S(2)}) collective-permute-start(f32[3,4,16,16]{3,2,1,0:T(8,128)} %param.4), channel_id=1, source_target_pairs={{0,8},{8,16},{16,24},{1,9},{9,17},{17,25},{2,10},{10,18},{18,26},{... | collective-permute-start | bytes 36872 | tf_op jit(solution)/shard_map/ppermute | solution.py:71
  10.9 1.3 collective-permute-start.1
  12.4 0.9 constant_dynamic-update-slice_fusion.1
  13.3 2.2 %collective-permute-done.1 = f32[3,4,16,16]{3,2,1,0:T(8,128)S(1)} collective-permute-done((f32[3,4,16,16]{3,2,1,0:T(8,128)}, f32[3,4,16,16]{3,2,1,0:T(8,128)S(1)}, u32[]{:S(2)}, u32[]{:S(2)}) %collective-permute-start.1) | collective-permute-done | bytes 12320 | tf_op jit(solution)/shard_map/ppermute | solution.py:74
  15.5 3.5 %collective-permute-start.2 = (f32[3,12,4,16]{3,2,1,0:T(4,128)S(1)}, f32[3,12,4,16]{3,2,1,0:T(4,128)S(1)}, u32[]{:S(2)}, u32[]{:S(2)}) collective-permute-start(f32[3,12,4,16]{3,2,1,0:T(4,128)S(1)} %get-tuple-element.18), channel_id=1, source_target_pairs={{0,2},{2,4},{4,6},{1,3},{3,5},{5,7},{8,10},{10,12},{12,14},{9,11},... | collective-permute-start | bytes 27656 | tf_op jit(solution)/shard_map/ppermute | solution.py:71
  19.0 1.3 collective-permute-start.3
  20.3 1.1 broadcast_multiply_fusion
  22.1 3.2 %collective-permute-done.3 = f32[3,12,4,16]{3,2,1,0:T(4,128)S(1)} collective-permute-done((f32[3,12,4,16]{3,2,1,0:T(4,128)S(1)}, f32[3,12,4,16]{3,2,1,0:T(4,128)S(1)}, u32[]{:S(2)}, u32[]{:S(2)}) %collective-permute-start.3) | collective-permute-done | bytes 9248 | tf_op jit(solution)/shard_map/ppermute | solution.py:74
  25.5 3.6 %collective-permute-start.8 = (f32[12,4,16,32]{3,2,1,0:T(8,128)S(1)}, f32[12,4,16,32]{3,2,1,0:T(8,128)S(1)}, u32[]{:S(2)}, u32[]{:S(2)}) collective-permute-start(f32[12,4,16,32]{3,2,1,0:T(8,128)S(1)} %get-tuple-element.11), channel_id=1, source_target_pairs={{0,2},{2,4},{4,6},{1,3},{3,5},{5,7},{8,10},{10,12},{12,14},{9,11},... | collective-permute-start | bytes 294920 | tf_op jit(solution)/shard_map/ppermute | solution.py:71
  29.1 1.3 collective-permute-start.9
  30.4 1.1 fusion.94
  31.5 3.4 %collective-permute-start.4 = (f32[3,12,24,4]{3,2,1,0:T(8,128)}, f32[3,12,24,4]{3,2,1,0:T(8,128)S(1)}, u32[]{:S(2)}, u32[]{:S(2)}) collective-permute-start(f32[3,12,24,4]{3,2,1,0:T(8,128)} %get-tuple-element.15), channel_id=1, source_target_pairs={{0,1},{2,3},{4,5},{6,7},{8,9},{10,11},{12,13},{14,15},{16,17},{18,... | collective-permute-start | bytes 41480 | tf_op jit(solution)/shard_map/ppermute | solution.py:71
  35.0 1.3 collective-permute-start.5
  36.3 1.5 collective-permute-done.8
  37.8 4.7 %collective-permute-done.9 = f32[12,4,16,32]{3,2,1,0:T(8,128)S(1)} collective-permute-done((f32[12,4,16,32]{3,2,1,0:T(8,128)S(1)}, f32[12,4,16,32]{3,2,1,0:T(8,128)S(1)}, u32[]{:S(2)}, u32[]{:S(2)}) %collective-permute-start.9) | collective-permute-done | bytes 98336 | tf_op jit(solution)/shard_map/ppermute | solution.py:74
  42.5 1.4 pad_maximum_fusion.6
  43.8 4.3 %collective-permute-start.10 = (f32[12,24,4,32]{3,2,1,0:T(4,128)}, f32[12,24,4,32]{3,2,1,0:T(4,128)}, u32[]{:S(2)}, u32[]{:S(2)}) collective-permute-start(f32[12,24,4,32]{3,2,1,0:T(4,128)} %get-tuple-element.9), channel_id=1, source_target_pairs={{0,1},{2,3},{4,5},{6,7},{8,9},{10,11},{12,13},{14,15},{16,17},{18,... | collective-permute-start | bytes 442376 | tf_op jit(solution)/shard_map/ppermute | solution.py:71
  48.1 1.3 collective-permute-start.11
  49.5 1.0 reshape.157
  50.6 1.4 pad_maximum_fusion.8
  52.0 5.9 %broadcast_in_dim.22 = f32[3,12,24,24,32]{4,3,2,1,0:T(8,128)} broadcast(f32[3,12,24,24]{3,2,1,0:T(8,128)S(1)} %pad_maximum_fusion.8), dimensions={0,1,2,3} | broadcast | bytes 2737152 | tf_op jit(solution)/shard_map/broadcast_in_dim | solution.py:129
  58.0 6.6 %reshape.153 = f32[3,12,24,768]{3,2,1,0:T(8,128)S(1)} reshape(f32[3,12,24,24,32]{4,3,2,1,0:T(8,128)} %broadcast_in_dim.22) | data formatting | bytes 5308416 | tf_op jit(solution)/shard_map/reshape | solution.py:129
  64.6 1.3 collective-permute-done.11
  65.9 4.3 %pad_maximum_fusion = f32[12,24,24,32]{3,2,1,0:T(8,128)} fusion(f32[12,24,4,32]{3,2,1,0:T(4,128)} %collective-permute-done.11, f32[12,4,16,32]{3,2,1,0:T(8,128)} %copy-done.6, f32[4,16,16,32]{3,2,1,0:T(8,128)} %copy-done.2, f32[4,16,16,32]{3,2,1,0:T(8,128)S(1)} %slice.346, f32[4,16,16,32]{3,2,1,0:T(8,128)} %copy-done.1, f32[12,4,16,32]{3,2,1,0:T(8,128)} %copy-done.5, ...), kind=kLoop, calls=%fused_computation | loop fusion | flops 1327104 | bytes 1769472 | tf_op jit(solution)/shard_map/concatenate | solution.py:75
  70.2 2.7 %reshape.155 = f32[12,24,768]{2,1,0:T(8,128)S(1)} reshape(f32[12,24,24,32]{3,2,1,0:T(8,128)} %pad_maximum_fusion) | data formatting | bytes 1769472 | tf_op jit(solution)/shard_map/reshape | solution.py:131
  72.9 3.6 %slice_multiply_fusion = f32[10,22,704]{2,1,0:T(8,128)S(1)} fusion(f32[12,24,768]{2,1,0:T(8,128)} %broadcast_multiply_fusion, f32[12,24,768]{2,1,0:T(8,128)S(1)} %reshape.155, f32[3,12,24,768]{3,2,1,0:T(8,128)S(1)} %reshape.153, f32[]{:T(128)} %sub.218, f32[]{:T(128)} %bitcast.157), kind=kLoop, calls=%fused_computation.13 | loop fusion | flops 3872000 | bytes 9292808 | tf_op jit(solution)/shard_map/mul | solution.py:147
  76.5 0.7 slice.360
  77.3 1.9 %slice_multiply_fusion.1 = f32[8,20,640]{2,1,0:T(8,128)S(1)} fusion(f32[12,24,768]{2,1,0:T(8,128)S(1)} %copy-done, f32[12,24,768]{2,1,0:T(8,128)S(1)} %reshape.155, f32[10,22,704]{2,1,0:T(8,128)S(1)} %slice_multiply_fusion, f32[3,12,24,768]{3,2,1,0:T(8,128)S(1)} %reshape.153, f32[]{:T(128)} %sub.218, f32[]{:T(128)} %bitcast.159), kind=kLoop, calls=%fused_computation.47 | loop fusion | flops 2662400 | bytes 6553608 | tf_op jit(solution)/shard_map/mul | solution.py:151
  79.2 1.4 slice_multiply_fusion.2
  80.6 0.4 fusion.93
  81.0 0.9 stack_reshape.13
  81.9 1.7 %stack_reshape.14 = f32[4,16,16,1,32]{4,3,2,1,0:T(1,128)} reshape(f32[4,16,512]{2,1,0:T(8,128)S(1)} %get-tuple-element.17) | data formatting | bytes 262144 | tf_op jit(solution)/shard_map/stack;reshape | solution.py:158
  83.7 1.7 %stack_reshape.15 = f32[4,16,16,1,32]{4,3,2,1,0:T(1,128)} reshape(f32[4,16,512]{2,1,0:T(8,128)S(1)} %get-tuple-element.14) | data formatting | bytes 262144 | tf_op jit(solution)/shard_map/stack;reshape | solution.py:158
  85.4 1.7 %stack_reshape.12 = f32[4,16,16,1,32]{4,3,2,1,0:T(1,128)} reshape(f32[4,16,512]{2,1,0:T(8,128)S(1)} %copy-done.7) | data formatting | bytes 262144 | tf_op jit(solution)/shard_map/stack;reshape | solution.py:158
  87.1 3.7 %pad_maximum_fusion.1 = f32[4,16,16,4,32]{4,3,2,1,0:T(4,128)S(1)} fusion(f32[4,16,16,1,32]{4,3,2,1,0:T(1,128)} %stack_reshape.15, f32[4,16,16,1,32]{4,3,2,1,0:T(1,128)} %stack_reshape.14, f32[4,16,16,1,32]{4,3,2,1,0:T(1,128)S(1)} %stack_reshape.13, f32[4,16,16,1,32]{4,3,2,1,0:T(1,128)} %stack_reshape.12), kind=kLoop, calls=%fused_computation.1 | loop fusion | flops 393216 | bytes 1048576 | tf_op jit(solution)/shard_map/stack | solution.py:158
  90.8 1.1 reshape.156
  91.9 2.4 %fusion.1 = f32[224,224]{0,1:T(8,128)S(1)} fusion(f32[1024,128]{1,0:T(8,128)S(1)} %reshape.156, f32[1024,96]{1,0:T(8,128)S(1)} %copy-done.3), kind=kOutput, calls=%fused_computation.9 | convolution fusion | flops 616792064 | bytes 1118208 | tf_op jit(solution)/shard_map/dot_general | solution.py:19
  94.7 1.2 collective-permute-done.12
  96.1 7.5 %collective-permute-done.13 = f32[224,224]{0,1:T(8,128)S(1)} collective-permute-done((f32[224,224]{0,1:T(8,128)S(1)}, f32[224,224]{0,1:T(8,128)S(1)}, u32[]{:S(2)}, u32[]{:S(2)}) %collective-permute-start.13) | collective-permute-done | bytes 200736 | tf_op jit(solution)/shard_map/ppermute | solution.py:61
  103.7 2.2 %collective-permute-start.14 = (f32[224,224]{0,1:T(8,128)S(1)}, f32[224,224]{0,1:T(8,128)S(1)}, u32[]{:S(2)}, u32[]{:S(2)}) collective-permute-start(f32[224,224]{0,1:T(8,128)S(1)} %add.262), channel_id=1, source_target_pairs={{0,1},{1,0},{2,3},{3,2},{4,5},{5,4},{6,7},{7,6},{8,9},{9,8},{10,11... | collective-permute-start | bytes 602120 | tf_op jit(solution)/shard_map/ppermute | solution.py:61
  106.0 0.2 mul.606
  106.1 4.8 %collective-permute-done.14 = f32[224,224]{0,1:T(8,128)S(1)} collective-permute-done((f32[224,224]{0,1:T(8,128)S(1)}, f32[224,224]{0,1:T(8,128)S(1)}, u32[]{:S(2)}, u32[]{:S(2)}) %collective-permute-start.14) | collective-permute-done | bytes 200736 | tf_op jit(solution)/shard_map/ppermute | solution.py:61
  110.9 1.6 %collective-permute-start.15 = (f32[224,224]{0,1:T(8,128)S(1)}, f32[224,224]{0,1:T(8,128)S(1)}, u32[]{:S(2)}, u32[]{:S(2)}) collective-permute-start(f32[224,224]{0,1:T(8,128)S(1)} %add.263), channel_id=1, source_target_pairs={{0,2},{2,0},{4,6},{6,4},{1,3},{3,1},{5,7},{7,5},{8,10},{10,8},{12,... | collective-permute-start | bytes 602120 | tf_op jit(solution)/shard_map/ppermute | solution.py:61
  112.8 4.4 %collective-permute-done.15 = f32[224,224]{0,1:T(8,128)S(1)} collective-permute-done((f32[224,224]{0,1:T(8,128)S(1)}, f32[224,224]{0,1:T(8,128)S(1)}, u32[]{:S(2)}, u32[]{:S(2)}) %collective-permute-start.15) | collective-permute-done | bytes 200736 | tf_op jit(solution)/shard_map/ppermute | solution.py:61
  117.3 1.4 collective-permute-start.16
  118.6 9.9 %collective-permute-done.16 = f32[224,224]{0,1:T(8,128)S(1)} collective-permute-done((f32[224,224]{0,1:T(8,128)S(1)}, f32[224,224]{0,1:T(8,128)S(1)}, u32[]{:S(2)}, u32[]{:S(2)}) %collective-permute-start.16) | collective-permute-done | bytes 200736 | tf_op jit(solution)/shard_map/ppermute | solution.py:61
  128.7 0.2 convolution_add_fusion
  129.0 0.3 convolution_subtract_fusion.3
  129.3 0.2 convolution_subtract_fusion.1
  129.5 0.6 fusion
  130.1 0.3 convolution_subtract_fusion.2
  130.4 0.3 convolution_subtract_fusion
  130.8 11.7 %cholesky.16 = f32[128,128]{1,0:T(8,128)S(1)} custom-call(f32[128,128]{1,0:T(8,128)S(1)} %fusion.79), custom_call_target="Cholesky" | custom-call | tf_op jit(solution)/shard_map/jit(cholesky)/cholesky | solution.py:176
  142.6 0.6 compare_reduce_fusion
  143.2 0.7 select_bitcast_fusion
  143.9 1.6 fusion.80
  145.4 9.8 %custom-call.7 = f32[1,128,128]{1,2,0:T(8,128)S(1)} custom-call(f32[1,128,128]{2,1,0:T(8,128)S(1)} %select_bitcast_fusion), custom_call_target="InvertDiagBlocksLowerTriangular" | custom-call | tf_op jit(solution)/shard_map/jit(_solve_triangular)/triangular_solve | solution.py:178
  155.2 0.6 fusion.77
  155.8 0.9 reshape.158
  156.7 1.0 fusion.70
  (64 shorter events, 2.0 us)
Async XLA Ops:
  2.0 23.4 %collective-permute-start.6 = (f32[4,16,16,32]{3,2,1,0:T(8,128)S(1)}, f32[4,16,16,32]{3,2,1,0:T(8,128)S(1)}, u32[]{:S(2)}, u32[]{:S(2)}) collective-permute-start(f32[4,16,16,32]{3,2,1,0:T(8,128)S(1)} %slice.346), channel_id=1, source_target_pairs={{0,8},{8,16},{16,24},{1,9},{9,17},{17,25},{2,10},{10,18},{18,26},{... | collective-permute-start | bytes 393224 | tf_op jit(solution)/shard_map/ppermute | solution.py:71
  4.4 21.0 %collective-permute-start.7 = (f32[4,16,16,32]{3,2,1,0:T(8,128)S(1)}, f32[4,16,16,32]{3,2,1,0:T(8,128)S(1)}, u32[]{:S(2)}, u32[]{:S(2)}) collective-permute-start(f32[4,16,16,32]{3,2,1,0:T(8,128)S(1)} %slice.346), channel_id=1, source_target_pairs={{8,0},{16,8},{24,16},{9,1},{17,9},{25,17},{10,2},{18,10},{26,18},{... | collective-permute-start | bytes 393224 | tf_op jit(solution)/shard_map/ppermute | solution.py:74
  5.7 6.7 %collective-permute-start = (f32[3,4,16,16]{3,2,1,0:T(8,128)}, f32[3,4,16,16]{3,2,1,0:T(8,128)S(1)}, u32[]{:S(2)}, u32[]{:S(2)}) collective-permute-start(f32[3,4,16,16]{3,2,1,0:T(8,128)} %param.4), channel_id=1, source_target_pairs={{0,8},{8,16},{16,24},{1,9},{9,17},{17,25},{2,10},{10,18},{18,26},{... | collective-permute-start | bytes 36872 | tf_op jit(solution)/shard_map/ppermute | solution.py:71
  10.9 4.6 %collective-permute-start.1 = (f32[3,4,16,16]{3,2,1,0:T(8,128)}, f32[3,4,16,16]{3,2,1,0:T(8,128)S(1)}, u32[]{:S(2)}, u32[]{:S(2)}) collective-permute-start(f32[3,4,16,16]{3,2,1,0:T(8,128)} %param.4), channel_id=1, source_target_pairs={{8,0},{16,8},{24,16},{9,1},{17,9},{25,17},{10,2},{18,10},{26,18},{... | collective-permute-start | bytes 36872 | tf_op jit(solution)/shard_map/ppermute | solution.py:74
  15.5 6.5 %collective-permute-start.2 = (f32[3,12,4,16]{3,2,1,0:T(4,128)S(1)}, f32[3,12,4,16]{3,2,1,0:T(4,128)S(1)}, u32[]{:S(2)}, u32[]{:S(2)}) collective-permute-start(f32[3,12,4,16]{3,2,1,0:T(4,128)S(1)} %get-tuple-element.18), channel_id=1, source_target_pairs={{0,2},{2,4},{4,6},{1,3},{3,5},{5,7},{8,10},{10,12},{12,14},{9,11},... | collective-permute-start | bytes 27656 | tf_op jit(solution)/shard_map/ppermute | solution.py:71
  19.0 6.2 %collective-permute-start.3 = (f32[3,12,4,16]{3,2,1,0:T(4,128)S(1)}, f32[3,12,4,16]{3,2,1,0:T(4,128)S(1)}, u32[]{:S(2)}, u32[]{:S(2)}) collective-permute-start(f32[3,12,4,16]{3,2,1,0:T(4,128)S(1)} %get-tuple-element.19), channel_id=1, source_target_pairs={{2,0},{4,2},{6,4},{3,1},{5,3},{7,5},{10,8},{12,10},{14,12},{11,9},... | collective-permute-start | bytes 27656 | tf_op jit(solution)/shard_map/ppermute | solution.py:74
  25.4 24.1 %copy-start.4 = (f32[4,16,1536]{2,1,0:T(8,128)S(1)}, f32[4,16,1536]{2,1,0:T(8,128)}, u32[]{:S(2)}) copy-start(f32[4,16,1536]{2,1,0:T(8,128)} %param.3) | copy-start | bytes 1179652
  25.4 26.6 %copy-start.1 = (f32[4,16,16,32]{3,2,1,0:T(8,128)}, f32[4,16,16,32]{3,2,1,0:T(8,128)S(1)}, u32[]{:S(2)}) copy-start(f32[4,16,16,32]{3,2,1,0:T(8,128)S(1)} %collective-permute-done.6) | copy-start | bytes 393220
  25.4 18.4 %copy-start.2 = (f32[4,16,16,32]{3,2,1,0:T(8,128)}, f32[4,16,16,32]{3,2,1,0:T(8,128)S(1)}, u32[]{:S(2)}) copy-start(f32[4,16,16,32]{3,2,1,0:T(8,128)S(1)} %collective-permute-done.7) | copy-start | bytes 393220
  25.5 12.3 %collective-permute-start.8 = (f32[12,4,16,32]{3,2,1,0:T(8,128)S(1)}, f32[12,4,16,32]{3,2,1,0:T(8,128)S(1)}, u32[]{:S(2)}, u32[]{:S(2)}) collective-permute-start(f32[12,4,16,32]{3,2,1,0:T(8,128)S(1)} %get-tuple-element.11), channel_id=1, source_target_pairs={{0,2},{2,4},{4,6},{1,3},{3,5},{5,7},{8,10},{10,12},{12,14},{9,11},... | collective-permute-start | bytes 294920 | tf_op jit(solution)/shard_map/ppermute | solution.py:71
  29.1 13.3 %collective-permute-start.9 = (f32[12,4,16,32]{3,2,1,0:T(8,128)S(1)}, f32[12,4,16,32]{3,2,1,0:T(8,128)S(1)}, u32[]{:S(2)}, u32[]{:S(2)}) collective-permute-start(f32[12,4,16,32]{3,2,1,0:T(8,128)S(1)} %get-tuple-element.12), channel_id=1, source_target_pairs={{2,0},{4,2},{6,4},{3,1},{5,3},{7,5},{10,8},{12,10},{14,12},{11,9},... | collective-permute-start | bytes 294920 | tf_op jit(solution)/shard_map/ppermute | solution.py:74
  31.5 19.1 %collective-permute-start.4 = (f32[3,12,24,4]{3,2,1,0:T(8,128)}, f32[3,12,24,4]{3,2,1,0:T(8,128)S(1)}, u32[]{:S(2)}, u32[]{:S(2)}) collective-permute-start(f32[3,12,24,4]{3,2,1,0:T(8,128)} %get-tuple-element.15), channel_id=1, source_target_pairs={{0,1},{2,3},{4,5},{6,7},{8,9},{10,11},{12,13},{14,15},{16,17},{18,... | collective-permute-start | bytes 41480 | tf_op jit(solution)/shard_map/ppermute | solution.py:71
  35.0 15.7 %collective-permute-start.5 = (f32[3,12,24,4]{3,2,1,0:T(8,128)}, f32[3,12,24,4]{3,2,1,0:T(8,128)}, u32[]{:S(2)}, u32[]{:S(2)}) collective-permute-start(f32[3,12,24,4]{3,2,1,0:T(8,128)} %get-tuple-element.16), channel_id=1, source_target_pairs={{1,0},{3,2},{5,4},{7,6},{9,8},{11,10},{13,12},{15,14},{17,16},{19,... | collective-permute-start | bytes 41480 | tf_op jit(solution)/shard_map/ppermute | solution.py:74
  37.8 12.9 %copy-start.5 = (f32[12,4,16,32]{3,2,1,0:T(8,128)}, f32[12,4,16,32]{3,2,1,0:T(8,128)S(1)}, u32[]{:S(2)}) copy-start(f32[12,4,16,32]{3,2,1,0:T(8,128)S(1)} %collective-permute-done.8) | copy-start | bytes 294916
  42.5 1.4 copy-start.6
  43.8 20.8 %collective-permute-start.10 = (f32[12,24,4,32]{3,2,1,0:T(4,128)}, f32[12,24,4,32]{3,2,1,0:T(4,128)}, u32[]{:S(2)}, u32[]{:S(2)}) collective-permute-start(f32[12,24,4,32]{3,2,1,0:T(4,128)} %get-tuple-element.9), channel_id=1, source_target_pairs={{0,1},{2,3},{4,5},{6,7},{8,9},{10,11},{12,13},{14,15},{16,17},{18,... | collective-permute-start | bytes 442376 | tf_op jit(solution)/shard_map/ppermute | solution.py:71
  48.1 17.8 %collective-permute-start.11 = (f32[12,24,4,32]{3,2,1,0:T(4,128)}, f32[12,24,4,32]{3,2,1,0:T(4,128)}, u32[]{:S(2)}, u32[]{:S(2)}) collective-permute-start(f32[12,24,4,32]{3,2,1,0:T(4,128)} %get-tuple-element.10), channel_id=1, source_target_pairs={{1,0},{3,2},{5,4},{7,6},{9,8},{11,10},{13,12},{15,14},{17,16},{19,... | collective-permute-start | bytes 442376 | tf_op jit(solution)/shard_map/ppermute | solution.py:74
  72.9 4.4 %copy-start = (f32[12,24,768]{2,1,0:T(8,128)S(1)}, f32[12,24,768]{2,1,0:T(8,128)}, u32[]{:S(2)}) copy-start(f32[12,24,768]{2,1,0:T(8,128)} %broadcast_multiply_fusion) | copy-start | bytes 2654212
  80.6 4.8 %copy-start.7 = (f32[4,16,512]{2,1,0:T(8,128)S(1)}, f32[4,16,512]{2,1,0:T(8,128)}, u32[]{:S(2)}) copy-start(f32[4,16,512]{2,1,0:T(8,128)} %slice.360) | copy-start | bytes 393220
  87.1 4.8 %copy-start.3 = (f32[1024,96]{1,0:T(8,128)S(1)}, f32[1024,96]{1,0:T(8,128)}, u32[]{:S(2)}) copy-start(f32[1024,96]{1,0:T(8,128)} %reshape.157) | copy-start | bytes 1179652
  94.3 1.6 collective-permute-start.12
  95.9 7.7 %collective-permute-start.13 = (f32[224,224]{0,1:T(8,128)S(1)}, f32[224,224]{0,1:T(8,128)S(1)}, u32[]{:S(2)}, u32[]{:S(2)}) collective-permute-start(f32[224,224]{0,1:T(8,128)S(1)} %add.261), channel_id=1, source_target_pairs={{0,16},{8,24},{16,0},{24,8},{1,17},{9,25},{17,1},{25,9},{2,18},{10... | collective-permute-start | bytes 602120 | tf_op jit(solution)/shard_map/ppermute | solution.py:61
  103.7 7.3 %collective-permute-start.14 = (f32[224,224]{0,1:T(8,128)S(1)}, f32[224,224]{0,1:T(8,128)S(1)}, u32[]{:S(2)}, u32[]{:S(2)}) collective-permute-start(f32[224,224]{0,1:T(8,128)S(1)} %add.262), channel_id=1, source_target_pairs={{0,1},{1,0},{2,3},{3,2},{4,5},{5,4},{6,7},{7,6},{8,9},{9,8},{10,11... | collective-permute-start | bytes 602120 | tf_op jit(solution)/shard_map/ppermute | solution.py:61
  110.9 6.3 %collective-permute-start.15 = (f32[224,224]{0,1:T(8,128)S(1)}, f32[224,224]{0,1:T(8,128)S(1)}, u32[]{:S(2)}, u32[]{:S(2)}) collective-permute-start(f32[224,224]{0,1:T(8,128)S(1)} %add.263), channel_id=1, source_target_pairs={{0,2},{2,0},{4,6},{6,4},{1,3},{3,1},{5,7},{7,5},{8,10},{10,8},{12,... | collective-permute-start | bytes 602120 | tf_op jit(solution)/shard_map/ppermute | solution.py:61
  117.3 11.2 %collective-permute-start.16 = (f32[224,224]{0,1:T(8,128)S(1)}, f32[224,224]{0,1:T(8,128)S(1)}, u32[]{:S(2)}, u32[]{:S(2)}) collective-permute-start(f32[224,224]{0,1:T(8,128)S(1)} %add.264), channel_id=1, source_target_pairs={{0,4},{2,6},{4,0},{6,2},{1,5},{3,7},{5,1},{7,3},{8,12},{10,14},{12... | collective-permute-start | bytes 602120 | tf_op jit(solution)/shard_map/ppermute | solution.py:61

commit v2 on v0

v2 whole, which is shorter than its diff:
```python
import functools
import math

import jax
import jax.numpy as jnp
from jax import lax
from jax.experimental import pallas as pl
from jax.experimental.pallas import tpu as pltpu
from jax.sharding import PartitionSpec as P

BLOCK = 32
POWERS = 4
BASIS = 96
WIDE = BLOCK * POWERS

PRECISE = lax.Precision.HIGHEST
OPERATOR_SCALE = 11.0
DEGREE = 6.0
LANES = 128
SUBLANES = 8
F32 = jnp.float32
BF16 = jnp.bfloat16
AXES = ("gx", "gy", "gz")


def lane_of(shape):
    return lax.broadcasted_iota(jnp.int32, shape, 1)


def row_of(shape):
    return lax.broadcasted_iota(jnp.int32, shape, 0)


def kernel_call(body, shapes, scratch=()):
    return pl.pallas_call(
        body,
        out_shape=[jax.ShapeDtypeStruct(shape, F32) for shape in shapes],
        scratch_shapes=list(scratch),
        compiler_params=pltpu.CompilerParams(vmem_limit_bytes=24 * 1024 * 1024),
    )


def pack_body(single, prior_ref, weights_ref, field_ref, *face_refs):
    size_x, size_y, width = field_ref.shape
    own = width - LANES
    size_z = own // BLOCK
    shape = (size_y, LANES)
    lane = lane_of(shape)
    first = lax.axis_index("gz") == 0
    for i in range(size_x):
        for q in range(own // LANES):
            tiles = [prior_ref[i, :, (3 * q + m) * LANES : (3 * q + m + 1) * LANES] for m in range(3)]
            low, high = pltpu.roll(tiles[0], 64, 1), pltpu.roll(tiles[2], 64, 1)
            value = jnp.where(lane < 64, jnp.where(lane < 32, low, tiles[1]), jnp.where(lane < 96, high, tiles[2]))
            field_ref[i, :, q * LANES : (q + 1) * LANES] = value
        pieces = [weights_ref[d, i] for d in range(3)]
        pieces.append(jnp.zeros((size_y, LANES - 3 * size_z), F32))
        weights = jnp.concatenate(pieces, axis=1)
        field_ref[i, :, own:] = weights
        low_face, high_face = field_ref[i, :, :LANES], field_ref[i, :, own - LANES : own]
        faces = [jnp.where(first, high_face, low_face)] if single else [high_face, low_face]
        for face_ref, face in zip(face_refs, faces):
            face_ref[i, :, :LANES] = face
            face_ref[i, :, LANES:] = weights


def widen_body(single, field_ref, *refs):
    halo_refs, (wide_ref, low_ref, high_ref) = refs[:-3], refs[-3:]
    size_x, size_y, width = field_ref.shape
    own = width - LANES
    size_z = own // BLOCK
    lane = lane_of((size_y, LANES))
    upper = (lane % size_z) < size_z // 2
    first = lax.axis_index("gz") == 0
    zero = jnp.zeros((size_y, LANES), F32)
    for i in range(size_x):
        if single:
            value, other = halo_refs[0][i, :, :LANES], halo_refs[0][i, :, LANES:]
            above, below = jnp.where(first, value, zero), jnp.where(first, zero, value)
            above_w, below_w = jnp.where(first, other, zero), jnp.where(first, zero, other)
        else:
            above, above_w = halo_refs[0][i, :, :LANES], halo_refs[0][i, :, LANES:]
            below, below_w = halo_refs[1][i, :, :LANES], halo_refs[1][i, :, LANES:]
        other = pltpu.roll(jnp.where(upper, above_w, below_w), 3 * size_z, 1)
        weights = jnp.where(lane < 3 * size_z, field_ref[i, :, own:], jnp.where(lane < 6 * size_z, other, zero))
        row = jnp.concatenate([field_ref[i, :, :own], above, below, weights], axis=1)
        wide_ref[i] = row
        low_ref[i] = row[:POWERS]
        high_ref[i] = row[size_y - POWERS :]


def lengthen_body(wide_ref, above_ref, below_ref, long_ref):
    size_x, size_y, _ = wide_ref.shape
    for i in range(size_x):
        long_ref[i, :size_y] = wide_ref[i]
        long_ref[i, size_y:] = jnp.concatenate([above_ref[i], below_ref[i]], axis=0)


def last_on(axis):
    return lax.axis_index(axis) == lax.axis_size(axis) - 1


def exact_dot(values, selector):
    high = values.astype(BF16)
    rest = values - high.astype(F32)
    middle = rest.astype(BF16)
    low = (rest - middle.astype(F32)).astype(BF16)
    dot = functools.partial(jnp.dot, preferred_element_type=F32)
    return dot(high, selector) + dot(middle, selector) + dot(low, selector)


def columns_body(size_z, own_ref, above_ref, below_ref, prior_ref, q_ref, s_ref, keep_ref, give_ref, coupling, diagonal, levels, sums):
    size_x, rows, width = own_ref.shape
    size_y = rows - 2 * POWERS
    field = width - LANES
    own = size_z * BLOCK
    planes = size_x + 2 * POWERS
    parts = (own_ref, above_ref, below_ref)

    def plane(p):
        if p < size_x:
            return own_ref, p
        return (above_ref, p - size_x) if p < size_x + POWERS else (below_ref, p - size_x - POWERS)

    weights = jnp.concatenate([ref[:, :, field:].reshape(-1, LANES) for ref in parts], axis=0)
    source = row_of((LANES, field))
    position = lane_of((LANES, field)) // BLOCK
    place = jnp.where(
        position < size_z,
        position,
        jnp.where(position < size_z + POWERS, position + 2 * size_z, position + 3 * size_z - 2 * POWERS),
    )
    unit = 1.0 / math.sqrt(DEGREE)
    for d in range(3):
        selector = (source == place + d * size_z).astype(F32).astype(BF16)
        spread = exact_dot(weights, selector) * unit
        coupling[d] = spread.reshape(planes, rows, field)
    row_last = (row_of((rows, field)) == size_y - 1) & last_on("gy")
    lane_last = (lane_of((rows, field)) // BLOCK == size_z - 1) & last_on("gz")

    near = lambda layers: [p for p in range(planes) if p < size_x + layers or p >= planes - layers]
    for p in near(POWERS - 1):
        x, y, z = (coupling[d, p] for d in range(3))
        x_low = coupling[0, (p - 1) % planes]
        diagonal[p] = x + x_low + (y + pltpu.roll(y, 1, 0)) + (z + pltpu.roll(z, BLOCK, 1)) - math.sqrt(DEGREE)
    for p in near(POWERS - 1):
        coupling[1, p] = jnp.where(row_last, 0.0, coupling[1, p])
        coupling[2, p] = jnp.where(lane_last, 0.0, coupling[2, p])
    coupling[0, size_x - 1] = jnp.where(last_on("gx"), 0.0, coupling[0, size_x - 1])

    def level(k, p):
        if k == 0:
            ref, at = plane(p)
            return ref[at, :, :field]
        return levels[k - 1, p]

    for k in range(1, POWERS + 1):
        for p in near(POWERS - k):
            value = level(k - 1, p)
            up, down = (p + 1) % planes, (p - 1) % planes
            x, y, z = (coupling[d, p] for d in range(3))
            total = diagonal[p] * value - x * level(k - 1, up) - coupling[0, down] * level(k - 1, down)
            total = total - y * pltpu.roll(value, rows - 1, 0) - pltpu.roll(y * value, 1, 0)
            total = total - z * pltpu.roll(value, field - BLOCK, 1) - pltpu.roll(z * value, BLOCK, 1)
            if k > 1:
                total = total - level(k - 2, p)
            if k == POWERS:
                levels[k - 1, p, :size_y, :own] = total[:size_y, :own]
            else:
                levels[k - 1, p] = total

    lane = lane_of((size_y, LANES))
    block = lane // BLOCK
    for i in range(size_x):
        for q in range(own // LANES):
            lanes = slice(q * LANES, (q + 1) * LANES)
            tiles = [levels[m, i, :size_y, lanes] for m in range(POWERS)]
            prior = [prior_ref[i, :, (3 * q + m) * LANES : (3 * q + m + 1) * LANES] for m in range(3)]
            prior_rows = [
                prior[0],
                jnp.where(lane < 32, pltpu.roll(prior[0], 32, 1), pltpu.roll(prior[1], 32, 1)),
                jnp.where(lane < 64, pltpu.roll(prior[1], 64, 1), pltpu.roll(prior[2], 64, 1)),
                pltpu.roll(prior[2], 96, 1),
            ]
            for r in range(4):
                moved = [pltpu.roll(tiles[m], (32 * (m - r)) % LANES, 1) if m != r else tiles[m] for m in range(POWERS)]
                row = jnp.where(block < 2, jnp.where(block < 1, moved[0], moved[1]), jnp.where(block < 3, moved[2], moved[3]))
                at = (i * size_z + 4 * q + r) * size_y
                s_ref[at : at + size_y] = row
                q_ref[at : at + size_y] = jnp.where(lane < BASIS, prior_rows[r], 0.0)

    contract = functools.partial(
        lax.dot_general, dimension_numbers=(((0,), (0,)), ((), ())), precision=PRECISE, preferred_element_type=F32
    )
    prior, columns = q_ref[...], s_ref[...]
    sums[:BASIS] = contract(prior, prior)[:BASIS]
    sums[BASIS : 2 * BASIS] = contract(prior, columns)[:BASIS]
    sums[2 * BASIS :] = contract(columns, columns)
    half = sums.shape[0] // 2
    odd = lax.axis_index("gx") % 2 == 1
    keep_ref[...] = jnp.where(odd, sums[half:], sums[:half])
    give_ref[...] = jnp.where(odd, sums[:half], sums[half:])


def split_rows(values):
    high = values.astype(BF16).astype(F32)
    rest = values - high
    middle = rest.astype(BF16).astype(F32)
    low = rest - middle
    left = jnp.concatenate([high, high, middle, high, low, middle], axis=0).astype(BF16)
    right = jnp.concatenate([high, middle, high, low, high, middle], axis=0).astype(BF16)
    return left, right


def factor_panel(left, right, column):
    size, count = left.shape
    entry = lambda i, j: jnp.broadcast_to(left[i : i + 1, column + j : column + j + 1], (size, count))
    a = {(i, j): entry(i, j) for i in range(size) for j in range(i, size)}
    row_a = [jnp.broadcast_to(left[i : i + 1, :], (size, count)) for i in range(size)]
    row_b = [jnp.broadcast_to(right[i : i + 1, :], (size, count)) for i in range(size)]
    for k in range(size):
        inverse = lax.rsqrt(a[k, k])
        row_a[k] = row_a[k] * inverse
        row_b[k] = row_b[k] * inverse
        scaled = {j: a[k, j] * inverse for j in range(k + 1, size)}
        for i in range(k + 1, size):
            for j in range(i, size):
                a[i, j] = a[i, j] - scaled[i] * scaled[j]
            row_a[i] = row_a[i] - scaled[i] * row_a[k]
            row_b[i] = row_b[i] - scaled[i] * row_b[k]
    sub = row_of((size, count))
    out_a, out_b = row_a[0], row_b[0]
    for i in range(1, size):
        out_a, out_b = jnp.where(sub == i, row_a[i], out_a), jnp.where(sub == i, row_b[i], out_b)
    return out_a, out_b


def factor(joined, upper, inverse):
    count = upper.shape[0]
    for start in range(0, count, SUBLANES):
        stop = start + SUBLANES
        out_a, out_b = factor_panel(joined[start:stop, :count], joined[start:stop, count:], start)
        shape = (SUBLANES, count)
        upper[start:stop] = jnp.where(lane_of(shape) >= row_of(shape) + start, out_a, 0.0)
        inverse[start:stop] = out_b
        if stop < count:
            left, right = split_rows(jnp.concatenate([out_a, out_b], axis=1))
            update = lax.dot_general(
                left[:, :count], right, (((0,), (0,)), ((), ())), preferred_element_type=F32
            )
            joined[stop:] = joined[stop:] - update[stop:]


def basis_change(centre, width):
    def apply_a(c):
        up = [0.0] + [width * v for v in c[:-1]]
        down = [width * v for v in c[1:]] + [0.0]
        return [centre * v + u + d for v, u, d in zip(c, up, down)]

    def apply_x(c):
        out = [0.0] * len(c)
        out[1] = out[1] + c[0]
        for k in range(1, len(c)):
            if k + 1 < len(c):
                out[k + 1] = out[k + 1] + 0.5 * c[k]
            out[k - 1] = out[k - 1] + 0.5 * c[k]
        return [(o - centre * v) * (1.0 / width) for o, v in zip(out, c)]

    one = centre * 0.0 + 1.0
    t = [[one] + [0.0] * POWERS]
    s = [[one] + [0.0] * POWERS]
    t.append(apply_a(t[0]))
    s.append(apply_x(s[0]))
    for _ in range(1, POWERS):
        t.append([2.0 * v - w for v, w in zip(apply_a(t[-1]), t[-2])])
        s.append([v - w for v, w in zip(apply_x(s[-1]), s[-2])])
    return t, s


def per_block(values):
    block = lane_of((SUBLANES, WIDE)) // BLOCK
    out = jnp.zeros((SUBLANES, WIDE), F32)
    for k, value in enumerate(values):
        out = jnp.where(block == k, value, out)
    return out[:1]


def finish_body(scale, shift_ref, q_ref, s_ref, mine_ref, other_ref, basis_ref, projection_ref, triangle_ref, sums, joined, upper, inverse):
    size_x, size_y, width = basis_ref.shape
    size_z = width // WIDE
    half = mine_ref.shape[0]
    odd = lax.axis_index("gx") % 2 == 1
    sums[:half] = jnp.where(odd, other_ref[...], mine_ref[...]) * scale
    sums[half:] = jnp.where(odd, mine_ref[...], other_ref[...]) * scale
    dot = functools.partial(jnp.dot, precision=PRECISE, preferred_element_type=F32)

    centre, spread = (DEGREE + shift_ref[0]) * (1.0 / OPERATOR_SCALE) - 1.0, math.sqrt(DEGREE) / OPERATOR_SCALE
    t, s = basis_change(centre, spread)
    constant = per_block([t[k][0] for k in range(1, POWERS + 1)])
    removed = per_block([-s[k][0] for k in range(1, POWERS + 1)])
    mixes = [
        per_block([t[k][k - m] if k > m else 0.0 for k in range(1, POWERS + 1)]) for m in range(POWERS)
    ]

    def to_powers(values):
        total = values * mixes[0]
        for m in range(1, POWERS):
            total = total + pltpu.roll(values, m * BLOCK, 1) * mixes[m]
        return total

    inner, cross = sums[:BASIS], sums[BASIS : 2 * BASIS]
    shape = inner.shape
    row, lane = row_of(shape), lane_of(shape)
    block = lane // BLOCK
    defect = jnp.where(row == lane, 1.0, 0.0) - inner
    first = (BASIS - BLOCK) // BLOCK
    copies = [pltpu.roll(defect, ((k - first) * BLOCK) % WIDE, 1) if k != first else defect for k in range(POWERS)]
    start = jnp.where(block < 2, jnp.where(block < 1, copies[0], copies[1]), jnp.where(block < 3, copies[2], copies[3]))
    start_defect = dot(defect[:, :BASIS], start)
    both = cross + dot(defect[:, :BASIS], cross)
    moved = both - start_defect * removed
    start_unit = jnp.where(row - (BASIS - BLOCK) == lane - block * BLOCK, 1.0, 0.0)
    projection_ref[...] = to_powers(both) + (start_unit - start_defect) * constant
    left = cross - dot(inner[:, :BASIS], moved)
    product = lax.dot_general(
        jnp.concatenate([cross, moved], axis=0),
        jnp.concatenate([moved, left], axis=0),
        (((0,), (0,)), ((), ())),
        precision=PRECISE,
        preferred_element_type=F32,
    )
    joined[:, :WIDE] = sums[2 * BASIS :] - product
    shape = (WIDE, WIDE)
    joined[:, WIDE:] = jnp.where(row_of(shape) == lane_of(shape), 1.0, 0.0)
    padded = jnp.concatenate([moved, jnp.zeros((WIDE - BASIS, WIDE), F32)], axis=0)
    twice = s_ref[...] - dot(q_ref[...], padded)
    factor(joined, upper, inverse)
    triangle_ref[...] = to_powers(upper[...])
    new_basis = lax.dot_general(
        twice, inverse[...], (((1,), (1,)), ((), ())), precision=PRECISE, preferred_element_type=F32
    )
    for i in range(size_x):
        for k in range(size_z):
            at = (i * size_z + k) * size_y
            basis_ref[i, :, k * WIDE : (k + 1) * WIDE] = new_basis[at : at + size_y]


def swap(values, axis, step):
    count = lax.axis_size(axis)
    return lax.ppermute(values, axis, [(i, i ^ step) for i in range(count)])


def to_next(values, axis):
    return lax.ppermute(values, axis, [(i, i + 1) for i in range(lax.axis_size(axis) - 1)])


def to_previous(values, axis):
    return lax.ppermute(values, axis, [(i + 1, i) for i in range(lax.axis_size(axis) - 1)])


def doublings(axis):
    count = lax.axis_size(axis)
    return [1 << k for k in range(count.bit_length() - 1)]


def per_device(prior_basis, edge_weights, spectral_shift):
    size_x, size_y, _ = prior_basis.shape
    size_z = prior_basis.shape[2] // BASIS
    own = size_z * BLOCK
    single = lax.axis_size("gz") == 2
    cell_local = size_x * size_y * size_z
    cell_count = cell_local
    for axis in AXES:
        cell_count = cell_count * lax.axis_size(axis)

    face = (size_x, size_y, 2 * LANES)
    field, *faces = kernel_call(
        functools.partial(pack_body, single), [(size_x, size_y, own + LANES)] + [face] * (1 if single else 2)
    )(prior_basis, edge_weights)
    if single:
        halos = [swap(faces[0], "gz", 1)]
    else:
        halos = [to_previous(faces[1], "gz"), to_next(faces[0], "gz")]
    width = own + 3 * LANES
    wide, low, high = kernel_call(
        functools.partial(widen_body, single),
        [(size_x, size_y, width)] + [(size_x, POWERS, width)] * 2,
    )(field, *halos)
    below, above = to_next(high, "gy"), to_previous(low, "gy")
    (long,) = kernel_call(lengthen_body, [(size_x, size_y + 2 * POWERS, width)])(wide, above, below)
    below, above = to_next(long[-POWERS:], "gx"), to_previous(long[:POWERS], "gx")

    rows, planes, lanes = size_y + 2 * POWERS, size_x + 2 * POWERS, own + 2 * LANES
    sum_rows = 2 * BASIS + WIDE
    half = (sum_rows // 2, WIDE)
    prior_rows, columns, keep, give = kernel_call(
        functools.partial(columns_body, size_z),
        [(cell_local, LANES), (cell_local, WIDE), half, half],
        [
            pltpu.VMEM((3, planes, rows, lanes), F32),
            pltpu.VMEM((planes, rows, lanes), F32),
            pltpu.VMEM((POWERS, planes, rows, lanes), F32),
            pltpu.VMEM((sum_rows, WIDE), F32),
        ],
    )(long, above, below, prior_basis)

    total = keep + swap(give, "gx", 1)
    for axis in ("gx", "gz", "gy"):
        for step in doublings(axis):
            if (axis, step) != ("gx", 1):
                total = total + swap(total, axis, step)
    other = swap(total, "gx", 1)

    new_basis, projection, triangle = pl.pallas_call(
        functools.partial(finish_body, 1.0 / cell_count),
        in_specs=[pl.BlockSpec(memory_space=pltpu.SMEM)] + [pl.BlockSpec(memory_space=pltpu.VMEM)] * 4,
        out_shape=[
            jax.ShapeDtypeStruct((size_x, size_y, size_z * WIDE), F32),
            jax.ShapeDtypeStruct((BASIS, WIDE), F32),
            jax.ShapeDtypeStruct((WIDE, WIDE), F32),
        ],
        scratch_shapes=[
            pltpu.VMEM((sum_rows, WIDE), F32),
            pltpu.VMEM((WIDE, 2 * WIDE), F32),
            pltpu.VMEM((WIDE, WIDE), F32),
            pltpu.VMEM((WIDE, WIDE), F32),
        ],
        compiler_params=pltpu.CompilerParams(vmem_limit_bytes=24 * 1024 * 1024),
    )(spectral_shift, prior_rows, columns, total, other)
    return new_basis, projection, triangle


def solution(mesh):
    return jax.shard_map(
        per_device,
        mesh=mesh,
        in_specs=(P("gx", "gy", "gz"), P(None, "gx", "gy", "gz"), P()),
        out_specs=(P("gx", "gy", "gz"), P(), P()),
        check_vma=False,
    )
```

time: 333 us -> 62 us (0.19)
  waiting for transfers between devices: 132 us -> 17.4 us
  blocking collectives: 82.1 us -> 0 us
  other arithmetic: 41.1 us -> 0.05 us
  local copies, waits for them, and re-layouts: 25.3 us -> 1.89 us
  between operations: 15.1 us -> 1.39 us
  Pallas kernels: 0 us -> 12.8 us
  matrix products: 5.46 us -> 0 us
    psum x1 -> x0, waiting for transfers between devices: 118 us -> none  [per_device(): lax.psum(jnp.dot(twice.T, twice, precision=PRECISE), ('gx', 'gy', 'gz'))]
    psum x2 -> x0, blocking collectives: 82.1 us -> none  [the longest x1 41.5 us: per_device(): lax.psum(jnp.dot(basis_rows.T, krylov, precision=PRECISE), ('gx', 'gy', '...]
    another operation x5 -> x0, other arithmetic: 22.4 us -> none  [the longest x3 12.4 us: per_device(): lower_factor = jnp.linalg.cholesky(gram_matrix)]
    reshape x7 -> x0, local copies, waits for them, and re-layouts: 13.4 us -> none  [the longest x1 6.62 us: per_device(): weight_pad = jnp.repeat(weight_pad, BLOCK, axis=3)]
    pallas_call x0 -> x5, Pallas kernels: none -> 12.8 us  [the longest x1 8.17 us: per_device(): pl.pallas_call(functools.partial(finish_body, 1.0 / cell_count), in_specs...]
    mul x5 -> x0, other arithmetic: 8.07 us -> none  [the longest x1 3.61 us: per_device(): stencil(padded, weight_pad, shift_value, BLOCK)]
    broadcast_in_dim x2 -> x0, local copies, waits for them, and re-layouts: 5.98 us -> none  [the longest x1 5.91 us: per_device(): weight_pad = jnp.repeat(weight_pad, BLOCK, axis=3)]
    concatenate x3 -> x0, other arithmetic: 5.77 us -> none  [with_halo(): block = jnp.concatenate([low, block, high], axis=dim)]
  transfers between devices with their start and end apart: 13 -> 11, of which waited for: 6 -> 10; matrix products, arithmetic and copies ran while one was open for 6% -> 0% of each run, Pallas kernels for 0% -> 0%
where the time goes in v2:
time: 62 us; the launch traced here: 61.6 us
  starting transfers between devices  28.1 us (45%)
  waiting for transfers between devices  17.4 us (28%)
  Pallas kernels  12.8 us (21%)
  local copies, waits for them, and re-layouts  1.89 us (3%)
  between operations  1.39 us (2%)
    ppermute x7, starting transfers between devices, swap(): return lax.ppermute(values, axis, [(i, i ^ step) for i in range(count)])  17.7 us
    ppermute x7, waiting for transfers between devices, swap(): return lax.ppermute(values, axis, [(i, i ^ step) for i in range(count)])  14.3 us
    pallas_call x1, Pallas kernels, per_device(): pl.pallas_call(functools.partial(finish_body, 1.0 / cell_count), in_specs...  8.17 us
    ppermute x2, starting transfers between devices, to_next(): lax.ppermute(values, axis, [(i, i + 1) for i in range(lax.axis_size(axis)...  7.66 us
    pallas_call x1, Pallas kernels, per_device(): kernel_call(functools.partial(columns_body, size_z), [(cell_local, LANES)...  4.4 us
    ppermute x2, waiting for transfers between devices, to_next(): lax.ppermute(values, axis, [(i, i + 1) for i in range(lax.axis_size(axis)...  2.82 us
    ppermute x2, starting transfers between devices, to_previous(): lax.ppermute(values, axis, [(i + 1, i) for i in range(lax.axis_size(axis)...  2.72 us
    unnamed x6, local copies, waits for them, and re-layouts  1.89 us
  transfers between devices with their start and end apart: 11, of which 10 were waited for; matrix products, arithmetic and copies ran while one was open for 0% of the time, Pallas kernels for 0%

profile of v2, /device:TPU:0, one launch (start us, length us, event | category | flops | bytes accessed | tf_op | source)
XLA Modules:
  0.0 61.6 jit_solution(7685926801570274942)
XLA Ops:
  0.6 0.0 copy-start
  0.6 1.0 %copy-done = f32[4,16,1536]{2,1,0:T(8,128)S(1)} copy-done((f32[4,16,1536]{2,1,0:T(8,128)S(1)}, f32[4,16,1536]{2,1,0:T(8,128)}, u32[]{:S(2)}) %copy-start) | copy-done | bytes 393240
  1.6 0.0 copy-start.2
  1.6 0.9 %copy-done.2 = f32[3,4,16,16]{3,2,1,0:T(8,128)S(1)} copy-done((f32[3,4,16,16]{3,2,1,0:T(8,128)S(1)}, f32[3,4,16,16]{3,2,1,0:T(8,128)}, u32[]{:S(2)}) %copy-start.2) | copy-done | bytes 12312
  2.5 0.1 shard_map.58
  2.7 3.1 %collective-permute-start = (f32[4,16,256]{2,1,0:T(8,128)S(1)}, f32[4,16,256]{2,1,0:T(8,128)S(1)}, u32[]{:S(2)}, u32[]{:S(2)}) collective-permute-start(f32[4,16,256]{2,1,0:T(8,128)S(1)} %get-tuple-element.13), channel_id=1, source_target_pairs={{0,1},{1,0},{2,3},{3,2},{4,5},{5,4},{6,7},{7,6},{8,9},{9,8},{10,11... | collective-permute-start | bytes 196616 | tf_op jit(solution)/shard_map/ppermute | solution.py:350
  5.7 2.2 %collective-permute-done.refs_0_ = f32[4,16,256]{2,1,0:T(8,128)S(1)} collective-permute-done((f32[4,16,256]{2,1,0:T(8,128)S(1)}, f32[4,16,256]{2,1,0:T(8,128)S(1)}, u32[]{:S(2)}, u32[]{:S(2)}) %collective-permute-start) | collective-permute-done | bytes 65568 | tf_op jit(solution)/shard_map/ppermute | solution.py:350
  8.0 0.1 shard_map.59
  8.1 0.0 copy-start.1
  8.1 1.4 %collective-permute-start.1 = (f32[4,4,896]{2,1,0:T(4,128)S(1)}, f32[4,4,896]{2,1,0:T(4,128)S(1)}, u32[]{:S(2)}, u32[]{:S(2)}) collective-permute-start(f32[4,4,896]{2,1,0:T(4,128)S(1)} %get-tuple-element.15), channel_id=1, source_target_pairs={{2,0},{4,2},{6,4},{3,1},{5,3},{7,5},{10,8},{12,10},{14,12},{11,9},... | collective-permute-start | bytes 172040 | tf_op jit(solution)/shard_map/ppermute | solution.py:358
  9.5 4.6 %collective-permute-start.2 = (f32[4,4,896]{2,1,0:T(4,128)S(1)}, f32[4,4,896]{2,1,0:T(4,128)S(1)}, u32[]{:S(2)}, u32[]{:S(2)}) collective-permute-start(f32[4,4,896]{2,1,0:T(4,128)S(1)} %get-tuple-element.16), channel_id=1, source_target_pairs={{0,2},{2,4},{4,6},{1,3},{3,5},{5,7},{8,10},{10,12},{12,14},{9,11},... | collective-permute-start | bytes 172040 | tf_op jit(solution)/shard_map/ppermute | solution.py:354
  14.1 0.2 collective-permute-done.1.above_ref
  14.4 1.6 %collective-permute-done.2.below_ref = f32[4,4,896]{2,1,0:T(4,128)S(1)} collective-permute-done((f32[4,4,896]{2,1,0:T(4,128)S(1)}, f32[4,4,896]{2,1,0:T(4,128)S(1)}, u32[]{:S(2)}, u32[]{:S(2)}) %collective-permute-start.2) | collective-permute-done | bytes 57376 | tf_op jit(solution)/shard_map/ppermute | solution.py:354
  16.0 1.3 %collective-permute-start.3 = (f32[4,24,896]{2,1,0:T(8,128)S(1)}, f32[4,24,896]{2,1,0:T(8,128)S(1)}, u32[]{:S(2)}, u32[]{:S(2)}) collective-permute-start(f32[4,24,896]{2,1,0:T(8,128)S(1)} %shard_map.60.own_ref), channel_id=1, source_target_pairs={{8,0},{16,8},{24,16},{9,1},{17,9},{25,17},{10,2},{18,10},{26,18},{... | collective-permute-start | bytes 1032200 | tf_op jit(solution)/shard_map/ppermute | solution.py:358
  17.3 3.1 %collective-permute-start.4 = (f32[4,24,896]{2,1,0:T(8,128)S(1)}, f32[4,24,896]{2,1,0:T(8,128)S(1)}, u32[]{:S(2)}, u32[]{:S(2)}) collective-permute-start(f32[4,24,896]{2,1,0:T(8,128)S(1)} %shard_map.60.own_ref), channel_id=1, source_target_pairs={{0,8},{8,16},{16,24},{1,9},{9,17},{17,25},{2,10},{10,18},{18,26},{... | collective-permute-start | bytes 1032200 | tf_op jit(solution)/shard_map/ppermute | solution.py:354
  20.3 0.0 collective-permute-done.3.above_ref
  20.3 1.2 %collective-permute-done.4.below_ref = f32[4,24,896]{2,1,0:T(8,128)S(1)} collective-permute-done((f32[4,24,896]{2,1,0:T(8,128)S(1)}, f32[4,24,896]{2,1,0:T(8,128)S(1)}, u32[]{:S(2)}, u32[]{:S(2)}) %collective-permute-start.4) | collective-permute-done | bytes 344096 | tf_op jit(solution)/shard_map/ppermute | solution.py:354
  21.6 0.0 copy-done.1
  21.6 4.4 %shard_map.61 = (f32[1024,128]{1,0:T(8,128)S(1)}, f32[1024,128]{1,0:T(8,128)S(1)}, f32[160,128]{1,0:T(8,128)S(1)}, f32[160,128]{1,0:T(8,128)S(1)}) custom-call(f32[4,24,896]{2,1,0:T(8,128)S(1)} %shard_map.60.own_ref, f32[4,24,896]{2,1,0:T(8,128)S(1)} %collective-permute-done.3.above_ref, f32[4,24,896]{2,1,0:T(8,128)S(1)} %collective-permute-done.4.below_ref, ...), custom_call_target="tpu_custom_call" | custom-call | tf_op jit(solution)/shard_map/pallas_call | solution.py:396
  26.0 4.5 %collective-permute-start.5 = (f32[160,128]{1,0:T(8,128)S(1)}, f32[160,128]{1,0:T(8,128)S(1)}, u32[]{:S(2)}, u32[]{:S(2)}) collective-permute-start(f32[160,128]{1,0:T(8,128)S(1)} %get-tuple-element.20), channel_id=1, source_target_pairs={{0,8},{8,0},{16,24},{24,16},{1,9},{9,1},{17,25},{25,17},{2,10},{10... | collective-permute-start | bytes 245768 | tf_op jit(solution)/shard_map/ppermute | solution.py:350
  30.5 0.9 %collective-permute-done.5 = f32[160,128]{1,0:T(8,128)S(1)} collective-permute-done((f32[160,128]{1,0:T(8,128)S(1)}, f32[160,128]{1,0:T(8,128)S(1)}, u32[]{:S(2)}, u32[]{:S(2)}) %collective-permute-start.5) | collective-permute-done | bytes 81952 | tf_op jit(solution)/shard_map/ppermute | solution.py:350
  31.5 2.8 %collective-permute-start.6 = (f32[160,128]{1,0:T(8,128)S(1)}, f32[160,128]{1,0:T(8,128)S(1)}, u32[]{:S(2)}, u32[]{:S(2)}) collective-permute-start(f32[160,128]{1,0:T(8,128)S(1)} %add.15), channel_id=1, source_target_pairs={{0,16},{8,24},{16,0},{24,8},{1,17},{9,25},{17,1},{25,9},{2,18},{10... | collective-permute-start | bytes 245768 | tf_op jit(solution)/shard_map/ppermute | solution.py:350
  34.2 2.8 %collective-permute-done.6 = f32[160,128]{1,0:T(8,128)S(1)} collective-permute-done((f32[160,128]{1,0:T(8,128)S(1)}, f32[160,128]{1,0:T(8,128)S(1)}, u32[]{:S(2)}, u32[]{:S(2)}) %collective-permute-start.6) | collective-permute-done | bytes 81952 | tf_op jit(solution)/shard_map/ppermute | solution.py:350
  37.0 1.6 %collective-permute-start.7 = (f32[160,128]{1,0:T(8,128)S(1)}, f32[160,128]{1,0:T(8,128)S(1)}, u32[]{:S(2)}, u32[]{:S(2)}) collective-permute-start(f32[160,128]{1,0:T(8,128)S(1)} %add.16), channel_id=1, source_target_pairs={{0,1},{1,0},{2,3},{3,2},{4,5},{5,4},{6,7},{7,6},{8,9},{9,8},{10,11... | collective-permute-start | bytes 245768 | tf_op jit(solution)/shard_map/ppermute | solution.py:350
  38.6 2.9 %collective-permute-done.7 = f32[160,128]{1,0:T(8,128)S(1)} collective-permute-done((f32[160,128]{1,0:T(8,128)S(1)}, f32[160,128]{1,0:T(8,128)S(1)}, u32[]{:S(2)}, u32[]{:S(2)}) %collective-permute-start.7) | collective-permute-done | bytes 81952 | tf_op jit(solution)/shard_map/ppermute | solution.py:350
  41.5 2.4 %collective-permute-start.8 = (f32[160,128]{1,0:T(8,128)S(1)}, f32[160,128]{1,0:T(8,128)S(1)}, u32[]{:S(2)}, u32[]{:S(2)}) collective-permute-start(f32[160,128]{1,0:T(8,128)S(1)} %add.17), channel_id=1, source_target_pairs={{0,2},{2,0},{4,6},{6,4},{1,3},{3,1},{5,7},{7,5},{8,10},{10,8},{12,... | collective-permute-start | bytes 245768 | tf_op jit(solution)/shard_map/ppermute | solution.py:350
  44.0 2.4 %collective-permute-done.8 = f32[160,128]{1,0:T(8,128)S(1)} collective-permute-done((f32[160,128]{1,0:T(8,128)S(1)}, f32[160,128]{1,0:T(8,128)S(1)}, u32[]{:S(2)}, u32[]{:S(2)}) %collective-permute-start.8) | collective-permute-done | bytes 81952 | tf_op jit(solution)/shard_map/ppermute | solution.py:350
  46.4 3.3 %collective-permute-start.9 = (f32[160,128]{1,0:T(8,128)S(1)}, f32[160,128]{1,0:T(8,128)S(1)}, u32[]{:S(2)}, u32[]{:S(2)}) collective-permute-start(f32[160,128]{1,0:T(8,128)S(1)} %add.18), channel_id=1, source_target_pairs={{0,4},{2,6},{4,0},{6,2},{1,5},{3,7},{5,1},{7,3},{8,12},{10,14},{12... | collective-permute-start | bytes 245768 | tf_op jit(solution)/shard_map/ppermute | solution.py:350
  49.6 2.4 %collective-permute-done.9 = f32[160,128]{1,0:T(8,128)S(1)} collective-permute-done((f32[160,128]{1,0:T(8,128)S(1)}, f32[160,128]{1,0:T(8,128)S(1)}, u32[]{:S(2)}, u32[]{:S(2)}) %collective-permute-start.9) | collective-permute-done | bytes 81952 | tf_op jit(solution)/shard_map/ppermute | solution.py:350
  52.1 0.1 collective-permute-start.10
  52.8 0.6 %collective-permute-done.10.other_ref = f32[160,128]{1,0:T(8,128)S(1)} collective-permute-done((f32[160,128]{1,0:T(8,128)S(1)}, f32[160,128]{1,0:T(8,128)S(1)}, u32[]{:S(2)}, u32[]{:S(2)}) %collective-permute-start.10) | collective-permute-done | bytes 81952 | tf_op jit(solution)/shard_map/ppermute | solution.py:350
  53.4 8.2 %shard_map.62 = (f32[4,16,2048]{2,1,0:T(8,128)}, f32[96,128]{1,0:T(8,128)}, f32[128,128]{1,0:T(8,128)}) custom-call(f32[1]{0:T(128)S(6)} %copy.6.shift_ref, f32[1024,128]{1,0:T(8,128)S(1)} %get-tuple-element.17.q_ref, f32[1024,128]{1,0:T(8,128)S(1)} %get-tuple-element.18.s_ref, f32[160,128]{1,0:T(8,128)S(1)} %add.19.mine_ref, ...), custom_call_target="tpu_custom_call" | custom-call | tf_op jit(solution)/shard_map/pallas_call | solution.py:414
  (6 shorter events, 0.1 us)
Async XLA Ops:
  0.6 1.0 %copy-start = (f32[4,16,1536]{2,1,0:T(8,128)S(1)}, f32[4,16,1536]{2,1,0:T(8,128)}, u32[]{:S(2)}) copy-start(f32[4,16,1536]{2,1,0:T(8,128)} %prior_ref.3) | copy-start | bytes 1179652
  1.6 0.9 %copy-start.2 = (f32[3,4,16,16]{3,2,1,0:T(8,128)S(1)}, f32[3,4,16,16]{3,2,1,0:T(8,128)}, u32[]{:S(2)}) copy-start(f32[3,4,16,16]{3,2,1,0:T(8,128)} %weights_ref.1) | copy-start | bytes 36868
  2.7 5.3 %collective-permute-start = (f32[4,16,256]{2,1,0:T(8,128)S(1)}, f32[4,16,256]{2,1,0:T(8,128)S(1)}, u32[]{:S(2)}, u32[]{:S(2)}) collective-permute-start(f32[4,16,256]{2,1,0:T(8,128)S(1)} %get-tuple-element.13), channel_id=1, source_target_pairs={{0,1},{1,0},{2,3},{3,2},{4,5},{5,4},{6,7},{7,6},{8,9},{9,8},{10,11... | collective-permute-start | bytes 196616 | tf_op jit(solution)/shard_map/ppermute | solution.py:350
  8.1 13.5 %copy-start.1 = (f32[4,16,1536]{2,1,0:T(8,128)S(1)}, f32[4,16,1536]{2,1,0:T(8,128)}, u32[]{:S(2)}) copy-start(f32[4,16,1536]{2,1,0:T(8,128)} %prior_ref.3) | copy-start | bytes 1179652
  8.1 6.3 %collective-permute-start.1 = (f32[4,4,896]{2,1,0:T(4,128)S(1)}, f32[4,4,896]{2,1,0:T(4,128)S(1)}, u32[]{:S(2)}, u32[]{:S(2)}) collective-permute-start(f32[4,4,896]{2,1,0:T(4,128)S(1)} %get-tuple-element.15), channel_id=1, source_target_pairs={{2,0},{4,2},{6,4},{3,1},{5,3},{7,5},{10,8},{12,10},{14,12},{11,9},... | collective-permute-start | bytes 172040 | tf_op jit(solution)/shard_map/ppermute | solution.py:358
  9.5 6.4 %collective-permute-start.2 = (f32[4,4,896]{2,1,0:T(4,128)S(1)}, f32[4,4,896]{2,1,0:T(4,128)S(1)}, u32[]{:S(2)}, u32[]{:S(2)}) collective-permute-start(f32[4,4,896]{2,1,0:T(4,128)S(1)} %get-tuple-element.16), channel_id=1, source_target_pairs={{0,2},{2,4},{4,6},{1,3},{3,5},{5,7},{8,10},{10,12},{12,14},{9,11},... | collective-permute-start | bytes 172040 | tf_op jit(solution)/shard_map/ppermute | solution.py:354
  16.0 4.4 %collective-permute-start.3 = (f32[4,24,896]{2,1,0:T(8,128)S(1)}, f32[4,24,896]{2,1,0:T(8,128)S(1)}, u32[]{:S(2)}, u32[]{:S(2)}) collective-permute-start(f32[4,24,896]{2,1,0:T(8,128)S(1)} %shard_map.60.own_ref), channel_id=1, source_target_pairs={{8,0},{16,8},{24,16},{9,1},{17,9},{25,17},{10,2},{18,10},{26,18},{... | collective-permute-start | bytes 1032200 | tf_op jit(solution)/shard_map/ppermute | solution.py:358
  17.3 4.3 %collective-permute-start.4 = (f32[4,24,896]{2,1,0:T(8,128)S(1)}, f32[4,24,896]{2,1,0:T(8,128)S(1)}, u32[]{:S(2)}, u32[]{:S(2)}) collective-permute-start(f32[4,24,896]{2,1,0:T(8,128)S(1)} %shard_map.60.own_ref), channel_id=1, source_target_pairs={{0,8},{8,16},{16,24},{1,9},{9,17},{17,25},{2,10},{10,18},{18,26},{... | collective-permute-start | bytes 1032200 | tf_op jit(solution)/shard_map/ppermute | solution.py:354
  26.0 5.5 %collective-permute-start.5 = (f32[160,128]{1,0:T(8,128)S(1)}, f32[160,128]{1,0:T(8,128)S(1)}, u32[]{:S(2)}, u32[]{:S(2)}) collective-permute-start(f32[160,128]{1,0:T(8,128)S(1)} %get-tuple-element.20), channel_id=1, source_target_pairs={{0,8},{8,0},{16,24},{24,16},{1,9},{9,1},{17,25},{25,17},{2,10},{10... | collective-permute-start | bytes 245768 | tf_op jit(solution)/shard_map/ppermute | solution.py:350
  31.5 5.5 %collective-permute-start.6 = (f32[160,128]{1,0:T(8,128)S(1)}, f32[160,128]{1,0:T(8,128)S(1)}, u32[]{:S(2)}, u32[]{:S(2)}) collective-permute-start(f32[160,128]{1,0:T(8,128)S(1)} %add.15), channel_id=1, source_target_pairs={{0,16},{8,24},{16,0},{24,8},{1,17},{9,25},{17,1},{25,9},{2,18},{10... | collective-permute-start | bytes 245768 | tf_op jit(solution)/shard_map/ppermute | solution.py:350
  37.0 4.5 %collective-permute-start.7 = (f32[160,128]{1,0:T(8,128)S(1)}, f32[160,128]{1,0:T(8,128)S(1)}, u32[]{:S(2)}, u32[]{:S(2)}) collective-permute-start(f32[160,128]{1,0:T(8,128)S(1)} %add.16), channel_id=1, source_target_pairs={{0,1},{1,0},{2,3},{3,2},{4,5},{5,4},{6,7},{7,6},{8,9},{9,8},{10,11... | collective-permute-start | bytes 245768 | tf_op jit(solution)/shard_map/ppermute | solution.py:350
  41.5 4.8 %collective-permute-start.8 = (f32[160,128]{1,0:T(8,128)S(1)}, f32[160,128]{1,0:T(8,128)S(1)}, u32[]{:S(2)}, u32[]{:S(2)}) collective-permute-start(f32[160,128]{1,0:T(8,128)S(1)} %add.17), channel_id=1, source_target_pairs={{0,2},{2,0},{4,6},{6,4},{1,3},{3,1},{5,7},{7,5},{8,10},{10,8},{12,... | collective-permute-start | bytes 245768 | tf_op jit(solution)/shard_map/ppermute | solution.py:350
  46.4 5.7 %collective-permute-start.9 = (f32[160,128]{1,0:T(8,128)S(1)}, f32[160,128]{1,0:T(8,128)S(1)}, u32[]{:S(2)}, u32[]{:S(2)}) collective-permute-start(f32[160,128]{1,0:T(8,128)S(1)} %add.18), channel_id=1, source_target_pairs={{0,4},{2,6},{4,0},{6,2},{1,5},{3,7},{5,1},{7,3},{8,12},{10,14},{12... | collective-permute-start | bytes 245768 | tf_op jit(solution)/shard_map/ppermute | solution.py:350
  52.1 1.3 %collective-permute-start.10 = (f32[160,128]{1,0:T(8,128)S(1)}, f32[160,128]{1,0:T(8,128)S(1)}, u32[]{:S(2)}, u32[]{:S(2)}) collective-permute-start(f32[160,128]{1,0:T(8,128)S(1)} %add.19.mine_ref), channel_id=1, source_target_pairs={{0,8},{8,0},{16,24},{24,16},{1,9},{9,1},{17,25},{25,17},{2,10},{10... | collective-permute-start | bytes 245768 | tf_op jit(solution)/shard_map/ppermute | solution.py:350

commit v3 on v2

--- a/solution.py
+++ b/solution.py
@@ -31,69 +31,127 @@
     return lax.broadcasted_iota(jnp.int32, shape, 0)
 
 
-def kernel_call(body, shapes, scratch=()):
+def kernel_call(body, shapes, scratch=(), in_specs=None, cost=None, limit=24 * 1024 * 1024):
+    options = {} if in_specs is None else {"in_specs": in_specs}
     return pl.pallas_call(
         body,
         out_shape=[jax.ShapeDtypeStruct(shape, F32) for shape in shapes],
         scratch_shapes=list(scratch),
-        compiler_params=pltpu.CompilerParams(vmem_limit_bytes=24 * 1024 * 1024),
-    )
-
-
-def pack_body(single, prior_ref, weights_ref, field_ref, *face_refs):
+        compiler_params=pltpu.CompilerParams(vmem_limit_bytes=limit),
+        cost_estimate=cost,
+        **options,
+    )
+
+
+def even_on(axis):
+    return lax.axis_index(axis) % 2 == 0
+
+
+def pick(even, first, second):
+    return jnp.where(even, first, second)
+
+
+def pack_body(prior_hbm, weights_hbm, field_ref, *refs):
+    face_refs, (prior_ref, weights_ref, prior_sem, weights_sem) = refs[:-4], refs[-4:]
     size_x, size_y, width = field_ref.shape
+    weights_copy = pltpu.make_async_copy(weights_hbm, weights_ref, weights_sem)
+    copies = [pltpu.make_async_copy(prior_hbm.at[i], prior_ref.at[i], prior_sem.at[i]) for i in range(size_x)]
+    weights_copy.start()
+    for copy in copies:
+        copy.start()
     own = width - LANES
     size_z = own // BLOCK
     shape = (size_y, LANES)
     lane = lane_of(shape)
-    first = lax.axis_index("gz") == 0
-    for i in range(size_x):
+    even = even_on("gz")
+    weights_copy.wait()
+    for i in range(size_x):
+        pieces = [weights_ref[d, i] for d in range(3)]
+        pieces.append(jnp.zeros((size_y, LANES - 3 * size_z), F32))
+        weights = jnp.concatenate(pieces, axis=1)
+        field_ref[i, :, own:] = weights
+        for face_ref in face_refs:
+            face_ref[i, :, LANES:] = weights
+    for i in range(size_x):
+        copies[i].wait()
+        values = []
         for q in range(own // LANES):
             tiles = [prior_ref[i, :, (3 * q + m) * LANES : (3 * q + m + 1) * LANES] for m in range(3)]
             low, high = pltpu.roll(tiles[0], 64, 1), pltpu.roll(tiles[2], 64, 1)
             value = jnp.where(lane < 64, jnp.where(lane < 32, low, tiles[1]), jnp.where(lane < 96, high, tiles[2]))
             field_ref[i, :, q * LANES : (q + 1) * LANES] = value
-        pieces = [weights_ref[d, i] for d in range(3)]
-        pieces.append(jnp.zeros((size_y, LANES - 3 * size_z), F32))
-        weights = jnp.concatenate(pieces, axis=1)
-        field_ref[i, :, own:] = weights
-        low_face, high_face = field_ref[i, :, :LANES], field_ref[i, :, own - LANES : own]
-        faces = [jnp.where(first, high_face, low_face)] if single else [high_face, low_face]
+            values.append(value)
+        faces = [pick(even, values[-1], values[0]), pick(even, values[0], values[-1])]
         for face_ref, face in zip(face_refs, faces):
             face_ref[i, :, :LANES] = face
-            face_ref[i, :, LANES:] = weights
-
-
-def widen_body(single, field_ref, *refs):
-    halo_refs, (wide_ref, low_ref, high_ref) = refs[:-3], refs[-3:]
+
+
+def widen_body(field_ref, *refs):
+    halo_refs, (wide_ref, *face_refs) = refs[:-3], refs[-3:]
     size_x, size_y, width = field_ref.shape
     own = width - LANES
     size_z = own // BLOCK
     lane = lane_of((size_y, LANES))
     upper = (lane % size_z) < size_z // 2
-    first = lax.axis_index("gz") == 0
+    even, even_y = even_on("gz"), even_on("gy")
     zero = jnp.zeros((size_y, LANES), F32)
     for i in range(size_x):
-        if single:
-            value, other = halo_refs[0][i, :, :LANES], halo_refs[0][i, :, LANES:]
-            above, below = jnp.where(first, value, zero), jnp.where(first, zero, value)
-            above_w, below_w = jnp.where(first, other, zero), jnp.where(first, zero, other)
-        else:
-            above, above_w = halo_refs[0][i, :, :LANES], halo_refs[0][i, :, LANES:]
-            below, below_w = halo_refs[1][i, :, :LANES], halo_refs[1][i, :, LANES:]
+        values = [ref[i, :, :LANES] for ref in halo_refs] + [zero, zero]
+        others = [ref[i, :, LANES:] for ref in halo_refs] + [zero, zero]
+        above, below = pick(even, values[0], values[1]), pick(even, values[1], values[0])
+        above_w, below_w = pick(even, others[0], others[1]), pick(even, others[1], others[0])
         other = pltpu.roll(jnp.where(upper, above_w, below_w), 3 * size_z, 1)
         weights = jnp.where(lane < 3 * size_z, field_ref[i, :, own:], jnp.where(lane < 6 * size_z, other, zero))
         row = jnp.concatenate([field_ref[i, :, :own], above, below, weights], axis=1)
         wide_ref[i] = row
-        low_ref[i] = row[:POWERS]
-        high_ref[i] = row[size_y - POWERS :]
-
-
-def lengthen_body(wide_ref, above_ref, below_ref, long_ref):
-    size_x, size_y, _ = wide_ref.shape
-    for i in range(size_x):
-        long_ref[i, :size_y] = wide_ref[i]
-        long_ref[i, size_y:] = jnp.concatenate([above_ref[i], below_ref[i]], axis=0)
+        low, high = row[:POWERS], row[size_y - POWERS :]
+        face_refs[0][i] = pick(even_y, high, low)
+        face_refs[1][i] = pick(even_y, low, high)
+
+
+def lengthen_body(wide_ref, first_ref, second_ref, long_ref, *rest_refs):
+    size_x, size_y, width = wide_ref.shape
+    even, even_x = even_on("gy"), even_on("gx")
+    rest = []
+    for i in range(size_x):
+        wide = wide_ref[i]
+        long_ref[i, :size_y] = wide
+        first, second = first_ref[i], second_ref[i]
+        halo = jnp.concatenate([pick(even, first, second), pick(even, second, first)], axis=0)
+        long_ref[i, size_y:] = halo
+        side = wide[:, width - 3 * LANES :]
+        pieces = [side[row : row + SUBLANES] for row in range(0, size_y, SUBLANES)]
+        rest.append(jnp.concatenate(pieces + [halo], axis=1))
+    for at in range(POWERS - 1):
+        low, high = rest[at], rest[size_x - POWERS + 1 + at]
+        rest_refs[0][at] = pick(even_x, high, low)
+        rest_refs[1][at] = pick(even_x, low, high)
+
+
+def contract(left, right):
+    return lax.dot_general(
+        left, right, (((0,), (0,)), ((), ())), precision=PRECISE, preferred_element_type=F32
+    )
+
+
+def prior_body(prior_ref, q_ref, inner_ref):
+    size_x, size_y, width = prior_ref.shape
+    size_z = width // BASIS
+    lane = lane_of((size_y, LANES))
+    for i in range(size_x):
+        for q in range(width // (3 * LANES)):
+            prior = [prior_ref[i, :, (3 * q + m) * LANES : (3 * q + m + 1) * LANES] for m in range(3)]
+            rows = [
+                prior[0],
+                jnp.where(lane < 32, pltpu.roll(prior[0], 32, 1), pltpu.roll(prior[1], 32, 1)),
+                jnp.where(lane < 64, pltpu.roll(prior[1], 64, 1), pltpu.roll(prior[2], 64, 1)),
+                pltpu.roll(prior[2], 96, 1),
+            ]
+            for r in range(4):
+                at = (i * size_z + 4 * q + r) * size_y
+                q_ref[at : at + size_y] = jnp.where(lane < BASIS, rows[r], 0.0)
+    rows = q_ref[...]
+    inner_ref[...] = contract(rows, rows)[:BASIS]
 
 
 def last_on(axis):
@@ -109,20 +167,34 @@
     return dot(high, selector) + dot(middle, selector) + dot(low, selector)
 
 
-def columns_body(size_z, own_ref, above_ref, below_ref, prior_ref, q_ref, s_ref, keep_ref, give_ref, coupling, diagonal, levels, sums):
+def columns_body(size_z, own_ref, near_ref, far_ref, near_rest_ref, far_rest_ref, q_ref, inner_ref, s_ref, keep_ref, give_ref, joined, coupling, diagonal, levels, sums):
     size_x, rows, width = own_ref.shape
     size_y = rows - 2 * POWERS
     field = width - LANES
     own = size_z * BLOCK
     planes = size_x + 2 * POWERS
-    parts = (own_ref, above_ref, below_ref)
-
-    def plane(p):
-        if p < size_x:
-            return own_ref, p
-        return (above_ref, p - size_x) if p < size_x + POWERS else (below_ref, p - size_x - POWERS)
-
-    weights = jnp.concatenate([ref[:, :, field:].reshape(-1, LANES) for ref in parts], axis=0)
+    even = even_on("gx")
+    joined[:size_x] = own_ref[...]
+    for at in range(POWERS):
+        near, far = near_ref[at], far_ref[at]
+        above, below = size_x + at, size_x + POWERS + at
+        near_high, far_high = near_ref[near_ref.shape[0] - POWERS + at], far_ref[near_ref.shape[0] - POWERS + at]
+        for p, value in ((above, pick(even, near, far)), (below, pick(even, far_high, near_high))):
+            joined[p, :size_y, :own] = value[:, :own]
+            joined[p, :size_y, field:] = value[:, own:]
+    zero = jnp.zeros((size_y, 2 * LANES), F32)
+    for p in (size_x + POWERS - 1, size_x + POWERS):
+        joined[p, :size_y, own:field] = zero
+        joined[p, size_y:] = jnp.zeros((2 * POWERS, width), F32)
+    for at in range(POWERS - 1):
+        near, far = near_rest_ref[at], far_rest_ref[at]
+        for p, value in ((size_x + at, pick(even, near, far)), (size_x + POWERS + 1 + at, pick(even, far, near))):
+            for part in range(size_y // SUBLANES):
+                lanes = slice(3 * part * LANES, 3 * (part + 1) * LANES)
+                joined[p, part * SUBLANES : (part + 1) * SUBLANES, own:] = value[:, lanes]
+            joined[p, size_y:] = value[:, 3 * (size_y // SUBLANES) * LANES :]
+
+    weights = joined[:, :, field:].reshape(-1, LANES)
     source = row_of((LANES, field))
     position = lane_of((LANES, field)) // BLOCK
     place = jnp.where(
@@ -149,10 +221,7 @@
     coupling[0, size_x - 1] = jnp.where(last_on("gx"), 0.0, coupling[0, size_x - 1])
 
     def level(k, p):
-        if k == 0:
-            ref, at = plane(p)
-            return ref[at, :, :field]
-        return levels[k - 1, p]
+        return joined[p, :, :field] if k == 0 else levels[k - 1, p]
 
     for k in range(1, POWERS + 1):
         for p in near(POWERS - k):
@@ -173,33 +242,56 @@
     block = lane // BLOCK
     for i in range(size_x):
         for q in range(own // LANES):
-            lanes = slice(q * LANES, (q + 1) * LANES)
-            tiles = [levels[m, i, :size_y, lanes] for m in range(POWERS)]
-            prior = [prior_ref[i, :, (3 * q + m) * LANES : (3 * q + m + 1) * LANES] for m in range(3)]
-            prior_rows = [
-                prior[0],
-                jnp.where(lane < 32, pltpu.roll(prior[0], 32, 1), pltpu.roll(prior[1], 32, 1)),
-                jnp.where(lane < 64, pltpu.roll(prior[1], 64, 1), pltpu.roll(prior[2], 64, 1)),
-                pltpu.roll(prior[2], 96, 1),
-            ]
+            tiles = [levels[m, i, :size_y, q * LANES : (q + 1) * LANES] for m in range(POWERS)]
             for r in range(4):
                 moved = [pltpu.roll(tiles[m], (32 * (m - r)) % LANES, 1) if m != r else tiles[m] for m in range(POWERS)]
-                row = jnp.where(block < 2, jnp.where(block < 1, moved[0], moved[1]), jnp.where(block < 3, moved[2], moved[3]))
                 at = (i * size_z + 4 * q + r) * size_y
-                s_ref[at : at + size_y] = row
-                q_ref[at : at + size_y] = jnp.where(lane < BASIS, prior_rows[r], 0.0)
-
-    contract = functools.partial(
-        lax.dot_general, dimension_numbers=(((0,), (0,)), ((), ())), precision=PRECISE, preferred_element_type=F32
-    )
-    prior, columns = q_ref[...], s_ref[...]
-    sums[:BASIS] = contract(prior, prior)[:BASIS]
-    sums[BASIS : 2 * BASIS] = contract(prior, columns)[:BASIS]
-    sums[2 * BASIS :] = contract(columns, columns)
+                s_ref[at : at + size_y] = by_block(block, moved)
+
+    columns = s_ref[...]
+    sums[:BASIS] = contract(q_ref[...], columns)[:BASIS]
+    last = contract(columns[:, WIDE - BLOCK :], columns)
+    inner = inner_ref[...]
+    block = lane_of((BLOCK, LANES)) // BLOCK
+    turned = pltpu.roll(last, 96, 1)
+    sums[BASIS : BASIS + 32] = jnp.where(block < 3, inner[:32], turned)
+    sums[BASIS + 32 : BASIS + 64] = by_block(block, [turned, inner[32:64], inner[32:64], pltpu.roll(last, 32, 1)])
+    block = block[:16]
+    sums[BASIS + 64 :] = by_block(
+        block,
+        [pltpu.roll(inner[64:80], 64, 1), pltpu.roll(inner[80:96], 96, 1), pltpu.roll(last[:16], 96, 1), last[16:]],
+    )
     half = sums.shape[0] // 2
-    odd = lax.axis_index("gx") % 2 == 1
-    keep_ref[...] = jnp.where(odd, sums[half:], sums[:half])
-    give_ref[...] = jnp.where(odd, sums[:half], sums[half:])
+    even = even_on("gx")
+    keep_ref[...] = pick(even, sums[:half], sums[half:])
+    give_ref[...] = pick(even, sums[half:], sums[:half])
+
+
+def by_block(block, values):
+    return jnp.where(
+        block < 2, jnp.where(block < 1, values[0], values[1]), jnp.where(block < 3, values[2], values[3])
+    )
+
+
+def unpack(sums):
+    cross = sums[:BASIS]
+    top, middle, tail = sums[BASIS : BASIS + 32], sums[BASIS + 32 : BASIS + 64], sums[BASIS + 64 : BASIS + 80]
+    block = lane_of((BLOCK, LANES)) // BLOCK
+    corner = jnp.concatenate([pltpu.roll(tail, 64, 1), pltpu.roll(tail, 32, 1)], axis=0)
+    moment = jnp.concatenate([tail, pltpu.roll(tail, 96, 1)], axis=0)
+    last = jnp.concatenate([pltpu.roll(tail, 32, 1), tail], axis=0)
+    upper = jnp.concatenate([top, middle, corner, jnp.zeros((BLOCK, LANES), F32)], axis=0)
+    row, lane = row_of((BASIS, LANES)) // BLOCK, lane_of((BASIS, LANES)) // BLOCK
+    inner = jnp.where(row <= lane, upper[:BASIS], jnp.transpose(upper)[:BASIS])
+    inner = jnp.where(lane < BASIS // BLOCK, inner, 0.0)
+    moments = cross[BASIS - BLOCK :]
+    half = pltpu.roll(moments, 64, 1)
+    first = jnp.where(block == 0, moment, pltpu.roll(moments, 32, 1)) + pltpu.roll(moments, 96, 1)
+    first = jnp.where(block == 3, top, first)
+    second = jnp.where(block == 2, half + pltpu.roll(top, 96, 1), pltpu.roll(moment, 32, 1) + moments + half)
+    second = jnp.where(block == 3, pltpu.roll(middle, 96, 1), second)
+    third = jnp.where(block == 3, middle, corner + pltpu.roll(middle, 64, 1))
+    return inner, cross, jnp.concatenate([first, second, third, last], axis=0)
 
 
 def split_rows(values):
@@ -241,7 +333,8 @@
         stop = start + SUBLANES
         out_a, out_b = factor_panel(joined[start:stop, :count], joined[start:stop, count:], start)
         shape = (SUBLANES, count)
-        upper[start:stop] = jnp.where(lane_of(shape) >= row_of(shape) + start, out_a, 0.0)
+        out_a = jnp.where(lane_of(shape) >= row_of(shape) + start, out_a, 0.0)
+        upper[start:stop] = out_a
         inverse[start:stop] = out_b
         if stop < count:
             left, right = split_rows(jnp.concatenate([out_a, out_b], axis=1))
@@ -285,13 +378,12 @@
     return out[:1]
 
 
-def finish_body(scale, shift_ref, q_ref, s_ref, mine_ref, other_ref, basis_ref, projection_ref, triangle_ref, sums, joined, upper, inverse):
+def finish_body(scale, shift_ref, q_ref, s_ref, mine_ref, other_ref, basis_ref, projection_ref, triangle_ref, joined, upper, inverse):
     size_x, size_y, width = basis_ref.shape
     size_z = width // WIDE
-    half = mine_ref.shape[0]
-    odd = lax.axis_index("gx") % 2 == 1
-    sums[:half] = jnp.where(odd, other_ref[...], mine_ref[...]) * scale
-    sums[half:] = jnp.where(odd, mine_ref[...], other_ref[...]) * scale
+    even = even_on("gx")
+    mine, other = mine_ref[...] * scale, other_ref[...] * scale
+    sums = jnp.concatenate([pick(even, mine, other), pick(even, other, mine)], axis=0)
     dot = functools.partial(jnp.dot, precision=PRECISE, preferred_element_type=F32)
 
     centre, spread = (DEGREE + shift_ref[0]) * (1.0 / OPERATOR_SCALE) - 1.0, math.sqrt(DEGREE) / OPERATOR_SCALE
@@ -308,7 +400,7 @@
             total = total + pltpu.roll(values, m * BLOCK, 1) * mixes[m]
         return total
 
-    inner, cross = sums[:BASIS], sums[BASIS : 2 * BASIS]
+    inner, cross, square = unpack(sums)
     shape = inner.shape
     row, lane = row_of(shape), lane_of(shape)
     block = lane // BLOCK
@@ -322,14 +414,8 @@
     start_unit = jnp.where(row - (BASIS - BLOCK) == lane - block * BLOCK, 1.0, 0.0)
     projection_ref[...] = to_powers(both) + (start_unit - start_defect) * constant
     left = cross - dot(inner[:, :BASIS], moved)
-    product = lax.dot_general(
-        jnp.concatenate([cross, moved], axis=0),
-        jnp.concatenate([moved, left], axis=0),
-        (((0,), (0,)), ((), ())),
-        precision=PRECISE,
-        preferred_element_type=F32,
-    )
-    joined[:, :WIDE] = sums[2 * BASIS :] - product
+    product = contract(jnp.concatenate([cross, moved], axis=0), jnp.concatenate([moved, left], axis=0))
+    joined[:, :WIDE] = square - product
     shape = (WIDE, WIDE)
     joined[:, WIDE:] = jnp.where(row_of(shape) == lane_of(shape), 1.0, 0.0)
     padded = jnp.concatenate([moved, jnp.zeros((WIDE - BASIS, WIDE), F32)], axis=0)
@@ -350,12 +436,16 @@
     return lax.ppermute(values, axis, [(i, i ^ step) for i in range(count)])
 
 
-def to_next(values, axis):
-    return lax.ppermute(values, axis, [(i, i + 1) for i in range(lax.axis_size(axis) - 1)])
-
-
-def to_previous(values, axis):
-    return lax.ppermute(values, axis, [(i + 1, i) for i in range(lax.axis_size(axis) - 1)])
+def exchange(first, second, axis):
+    count = lax.axis_size(axis)
+    pairs = [(i, i ^ 1) for i in range(count) if i ^ 1 < count]
+    across = [(i, j) for k in range(1, count - 1, 2) for i, j in ((k, k + 1), (k + 1, k))]
+    got = [lax.ppermute(first, axis, pairs)] if pairs else []
+    return got + ([lax.ppermute(second, axis, across)] if across else [])
+
+
+def filled(halos, like):
+    return halos + [jnp.zeros_like(like)] * (2 - len(halos))
 
 
 def doublings(axis):
@@ -367,42 +457,54 @@
     size_x, size_y, _ = prior_basis.shape
     size_z = prior_basis.shape[2] // BASIS
     own = size_z * BLOCK
-    single = lax.axis_size("gz") == 2
     cell_local = size_x * size_y * size_z
     cell_count = cell_local
     for axis in AXES:
         cell_count = cell_count * lax.axis_size(axis)
 
-    face = (size_x, size_y, 2 * LANES)
+    hbm = pl.BlockSpec(memory_space=pltpu.HBM)
+    faces = min(lax.axis_size("gz") - 1, 2)
     field, *faces = kernel_call(
-        functools.partial(pack_body, single), [(size_x, size_y, own + LANES)] + [face] * (1 if single else 2)
-    )(prior_basis, edge_weights)
-    if single:
-        halos = [swap(faces[0], "gz", 1)]
-    else:
-        halos = [to_previous(faces[1], "gz"), to_next(faces[0], "gz")]
+        pack_body,
+        [(size_x, size_y, own + LANES)] + [(size_x, size_y, 2 * LANES)] * faces,
+        [
+            pltpu.VMEM(prior_basis.shape, F32),
+            pltpu.VMEM(edge_weights.shape, F32),
+            pltpu.SemaphoreType.DMA((size_x,)),
+            pltpu.SemaphoreType.DMA(()),
+        ],
+        [hbm, hbm],
+    )(*(pltpu.with_memory_space_constraint(array, pltpu.HBM) for array in (prior_basis, edge_weights)))
+    halos = exchange(faces[0], faces[-1], "gz") if faces else []
+    planes_x = filled(exchange(field, field, "gx"), field)
+    prior_rows, inner = kernel_call(
+        prior_body,
+        [(cell_local, LANES), (BASIS, LANES)],
+        cost=pl.CostEstimate(flops=6 * 2 * cell_local * LANES * LANES, bytes_accessed=4 * prior_basis.size, transcendentals=0),
+    )(prior_basis)
     width = own + 3 * LANES
-    wide, low, high = kernel_call(
-        functools.partial(widen_body, single),
-        [(size_x, size_y, width)] + [(size_x, POWERS, width)] * 2,
+    wide, first, second = kernel_call(
+        widen_body, [(size_x, size_y, width)] + [(size_x, POWERS, width)] * 2
     )(field, *halos)
-    below, above = to_next(high, "gy"), to_previous(low, "gy")
-    (long,) = kernel_call(lengthen_body, [(size_x, size_y + 2 * POWERS, width)])(wide, above, below)
-    below, above = to_next(long[-POWERS:], "gx"), to_previous(long[:POWERS], "gx")
+    halos = filled(exchange(first, second, "gy"), first)
+    rest = (POWERS - 1, SUBLANES, 3 * LANES * (size_y // SUBLANES) + width)
+    long, first, second = kernel_call(lengthen_body, [(size_x, size_y + 2 * POWERS, width), rest, rest])(wide, *halos)
+    rests = filled(exchange(first, second, "gx"), first)
 
     rows, planes, lanes = size_y + 2 * POWERS, size_x + 2 * POWERS, own + 2 * LANES
-    sum_rows = 2 * BASIS + WIDE
+    sum_rows = BASIS + 80
     half = (sum_rows // 2, WIDE)
-    prior_rows, columns, keep, give = kernel_call(
+    columns, keep, give = kernel_call(
         functools.partial(columns_body, size_z),
-        [(cell_local, LANES), (cell_local, WIDE), half, half],
+        [(cell_local, WIDE), half, half],
         [
+            pltpu.VMEM((planes, rows, width), F32),
             pltpu.VMEM((3, planes, rows, lanes), F32),
             pltpu.VMEM((planes, rows, lanes), F32),
             pltpu.VMEM((POWERS, planes, rows, lanes), F32),
             pltpu.VMEM((sum_rows, WIDE), F32),
         ],
-    )(long, above, below, prior_basis)
+    )(long, *planes_x, *rests, prior_rows, inner)
 
     total = keep + swap(give, "gx", 1)
     for axis in ("gx", "gz", "gy"):
@@ -420,7 +522,6 @@
             jax.ShapeDtypeStruct((WIDE, WIDE), F32),
         ],
         scratch_shapes=[
-            pltpu.VMEM((sum_rows, WIDE), F32),
             pltpu.VMEM((WIDE, 2 * WIDE), F32),
             pltpu.VMEM((WIDE, WIDE), F32),
             pltpu.VMEM((WIDE, WIDE), F32),

time: 62 us -> 55.2 us (0.89)
  starting transfers between devices: 28.1 us -> 24.1 us
  waiting for transfers between devices: 17.4 us -> 14.6 us
  Pallas kernels: 12.8 us -> 14.9 us
  local copies, waits for them, and re-layouts: 1.89 us -> 0.01 us
    ppermute x7 -> x6, starting transfers between devices: 17.7 us -> 14.6 us  [swap(): return lax.ppermute(values, axis, [(i, i ^ step) for i in range(count)])]
    ppermute x7 -> x6, waiting for transfers between devices: 14.3 us -> 11.6 us  [swap(): return lax.ppermute(values, axis, [(i, i ^ step) for i in range(count)])]
    pallas_call x4 -> x5, Pallas kernels: 4.66 us -> 6.61 us  [the longest x1 4.09 us: per_device(): kernel_call(functools.partial(columns_body, size_z), [(cell_local, WIDE),...]
    unnamed x6 -> x2, local copies, waits for them, and re-layouts: 1.89 us -> 0.01 us
    ppermute x4 -> x7, starting transfers between devices: 10.4 us -> 9.45 us  [the longest x4 7.46 us: exchange(): got = [lax.ppermute(first, axis, pairs)] if pairs else []]
    ppermute x4 -> x7, waiting for transfers between devices: 3.04 us -> 3 us  [the longest x4 2.99 us: exchange(): got = [lax.ppermute(first, axis, pairs)] if pairs else []]
  transfers between devices with their start and end apart: 11 -> 13, of which waited for: 10 -> 8; matrix products, arithmetic and copies ran while one was open for 0% -> 0% of each run, Pallas kernels for 0% -> 2%
where the time goes in v3:
time: 55.2 us; the launch traced here: 55 us
  starting transfers between devices  24.1 us (44%)
  Pallas kernels  14.9 us (27%)
  waiting for transfers between devices  14.6 us (26%)
  between operations  1.41 us (3%)
    ppermute x6, starting transfers between devices, swap(): return lax.ppermute(values, axis, [(i, i ^ step) for i in range(count)])  14.6 us
    ppermute x6, waiting for transfers between devices, swap(): return lax.ppermute(values, axis, [(i, i ^ step) for i in range(count)])  11.6 us
    pallas_call x1, Pallas kernels, per_device(): pl.pallas_call(functools.partial(finish_body, 1.0 / cell_count), in_specs...  8.31 us
    ppermute x4, starting transfers between devices, exchange(): got = [lax.ppermute(first, axis, pairs)] if pairs else []  7.46 us
    pallas_call x1, Pallas kernels, per_device(): kernel_call(functools.partial(columns_body, size_z), [(cell_local, WIDE),...  4.09 us
    ppermute x4, waiting for transfers between devices, exchange(): got = [lax.ppermute(first, axis, pairs)] if pairs else []  2.99 us
    ppermute x3, starting transfers between devices, exchange(): return got + ([lax.ppermute(second, axis, across)] if across else [])  1.98 us
    pallas_call x1, Pallas kernels, per_device(): kernel_call(pack_body, [(size_x, size_y, own + LANES)] + [(size_x, size_y...  1.51 us
  transfers between devices with their start and end apart: 13, of which 8 were waited for; matrix products, arithmetic and copies ran while one was open for 0% of the time, Pallas kernels for 2%

profile of v3, /device:TPU:0, one launch (start us, length us, event | category | flops | bytes accessed | tf_op | source)
XLA Modules:
  0.0 55.0 jit_solution(15298019185592174172)
XLA Ops:
  0.6 1.5 %shard_map.59 = (f32[4,16,640]{2,1,0:T(8,128)S(1)}, f32[4,16,256]{2,1,0:T(8,128)S(1)}) custom-call(f32[4,16,1536]{2,1,0:T(8,128)} %prior_hbm.1, f32[3,4,16,16]{3,2,1,0:T(8,128)} %weights_hbm.1), custom_call_target="tpu_custom_call" | custom-call | tf_op jit(solution)/shard_map/pallas_call | solution.py:467
  2.1 0.0 copy-start
  2.2 3.1 %collective-permute-start = (f32[4,16,256]{2,1,0:T(8,128)S(1)}, f32[4,16,256]{2,1,0:T(8,128)S(1)}, u32[]{:S(2)}, u32[]{:S(2)}) collective-permute-start(f32[4,16,256]{2,1,0:T(8,128)S(1)} %get-tuple-element.18), channel_id=1, source_target_pairs={{0,1},{1,0},{2,3},{3,2},{4,5},{5,4},{6,7},{7,6},{8,9},{9,8},{10,11... | collective-permute-start | bytes 196616 | tf_op jit(solution)/shard_map/ppermute | solution.py:443
  5.2 2.2 %collective-permute-done.refs_0_ = f32[4,16,256]{2,1,0:T(8,128)S(1)} collective-permute-done((f32[4,16,256]{2,1,0:T(8,128)S(1)}, f32[4,16,256]{2,1,0:T(8,128)S(1)}, u32[]{:S(2)}, u32[]{:S(2)}) %collective-permute-start) | collective-permute-done | bytes 65568 | tf_op jit(solution)/shard_map/ppermute | solution.py:443
  7.5 0.1 shard_map.60
  7.6 2.1 %collective-permute-start.1 = (f32[4,4,896]{2,1,0:T(4,128)S(1)}, f32[4,4,896]{2,1,0:T(4,128)S(1)}, u32[]{:S(2)}, u32[]{:S(2)}) collective-permute-start(f32[4,4,896]{2,1,0:T(4,128)S(1)} %get-tuple-element.20), channel_id=1, source_target_pairs={{0,2},{2,0},{4,6},{6,4},{1,3},{3,1},{5,7},{7,5},{8,10},{10,8},{12,... | collective-permute-start | bytes 172040 | tf_op jit(solution)/shard_map/ppermute | solution.py:443
  9.7 0.7 %collective-permute-start.2 = (f32[4,4,896]{2,1,0:T(4,128)S(1)}, f32[4,4,896]{2,1,0:T(4,128)S(1)}, u32[]{:S(2)}, u32[]{:S(2)}) collective-permute-start(f32[4,4,896]{2,1,0:T(4,128)S(1)} %get-tuple-element.21), channel_id=1, source_target_pairs={{2,4},{4,2},{3,5},{5,3},{10,12},{12,10},{11,13},{13,11},{18,20},{2... | collective-permute-start | bytes 172040 | tf_op jit(solution)/shard_map/ppermute | solution.py:444
  10.4 0.1 collective-permute-start.3
  10.4 0.7 %collective-permute-start.4 = (f32[4,16,640]{2,1,0:T(8,128)S(1)}, f32[4,16,640]{2,1,0:T(8,128)S(1)}, u32[]{:S(2)}, u32[]{:S(2)}) collective-permute-start(f32[4,16,640]{2,1,0:T(8,128)S(1)} %get-tuple-element.17.field_ref), channel_id=1, source_target_pairs={{8,16},{16,8},{9,17},{17,9},{10,18},{18,10},{11,19},{19,11},{12,20... | collective-permute-start | bytes 491528 | tf_op jit(solution)/shard_map/ppermute | solution.py:444
  11.1 0.7 %collective-permute-done.1.first_ref = f32[4,4,896]{2,1,0:T(4,128)S(1)} collective-permute-done((f32[4,4,896]{2,1,0:T(4,128)S(1)}, f32[4,4,896]{2,1,0:T(4,128)S(1)}, u32[]{:S(2)}, u32[]{:S(2)}) %collective-permute-start.1) | collective-permute-done | bytes 57376 | tf_op jit(solution)/shard_map/ppermute | solution.py:443
  11.9 0.0 collective-permute-done.2.second_ref
  11.9 0.1 shard_map.61
  11.9 2.2 %collective-permute-start.5 = (f32[3,8,1664]{2,1,0:T(8,128)S(1)}, f32[3,8,1664]{2,1,0:T(8,128)S(1)}, u32[]{:S(2)}, u32[]{:S(2)}) collective-permute-start(f32[3,8,1664]{2,1,0:T(8,128)S(1)} %get-tuple-element.23), channel_id=1, source_target_pairs={{0,8},{8,0},{16,24},{24,16},{1,9},{9,1},{17,25},{25,17},{2,10},{10... | collective-permute-start | bytes 479240 | tf_op jit(solution)/shard_map/ppermute | solution.py:443
  14.1 0.7 %collective-permute-start.6 = (f32[3,8,1664]{2,1,0:T(8,128)S(1)}, f32[3,8,1664]{2,1,0:T(8,128)S(1)}, u32[]{:S(2)}, u32[]{:S(2)}) collective-permute-start(f32[3,8,1664]{2,1,0:T(8,128)S(1)} %get-tuple-element.24), channel_id=1, source_target_pairs={{8,16},{16,8},{9,17},{17,9},{10,18},{18,10},{11,19},{19,11},{12,20... | collective-permute-start | bytes 479240 | tf_op jit(solution)/shard_map/ppermute | solution.py:444
  14.8 0.0 copy-done
  14.8 0.9 %shard_map.58 = (f32[1024,128]{1,0:T(8,128)S(1)}, f32[96,128]{1,0:T(8,128)S(1)}) custom-call(f32[4,16,1536]{2,1,0:T(8,128)S(1)} %copy-done), custom_call_target="tpu_custom_call" | custom-call | flops 201326592 | bytes 393216 | tf_op jit(solution)/shard_map/pallas_call | solution.py:480
  15.7 0.0 collective-permute-done.3.near_ref
  15.7 0.0 collective-permute-done.4.far_ref
  15.7 0.0 collective-permute-done.5.near_rest_ref
  15.7 0.0 collective-permute-done.6.far_rest_ref
  15.7 4.1 %shard_map.62 = (f32[1024,128]{1,0:T(8,128)S(1)}, f32[88,128]{1,0:T(8,128)S(1)}, f32[88,128]{1,0:T(8,128)S(1)}) custom-call(f32[4,24,896]{2,1,0:T(8,128)S(1)} %get-tuple-element.22.own_ref, f32[4,16,640]{2,1,0:T(8,128)S(1)} %collective-permute-done.3.near_ref, f32[4,16,640]{2,1,0:T(8,128)S(1)} %collective-permute-done.4.far_ref, ...), custom_call_target="tpu_custom_call" | custom-call | tf_op jit(solution)/shard_map/pallas_call | solution.py:497
  19.8 5.1 %collective-permute-start.7 = (f32[88,128]{1,0:T(8,128)S(1)}, f32[88,128]{1,0:T(8,128)S(1)}, u32[]{:S(2)}, u32[]{:S(2)}) collective-permute-start(f32[88,128]{1,0:T(8,128)S(1)} %get-tuple-element.28), channel_id=1, source_target_pairs={{0,8},{8,0},{16,24},{24,16},{1,9},{9,1},{17,25},{25,17},{2,10},{10... | collective-permute-start | bytes 135176 | tf_op jit(solution)/shard_map/ppermute | solution.py:436
  24.9 0.9 %collective-permute-done.7 = f32[88,128]{1,0:T(8,128)S(1)} collective-permute-done((f32[88,128]{1,0:T(8,128)S(1)}, f32[88,128]{1,0:T(8,128)S(1)}, u32[]{:S(2)}, u32[]{:S(2)}) %collective-permute-start.7) | collective-permute-done | bytes 45088 | tf_op jit(solution)/shard_map/ppermute | solution.py:436
  25.8 0.9 %collective-permute-start.8 = (f32[88,128]{1,0:T(8,128)S(1)}, f32[88,128]{1,0:T(8,128)S(1)}, u32[]{:S(2)}, u32[]{:S(2)}) collective-permute-start(f32[88,128]{1,0:T(8,128)S(1)} %add.15), channel_id=1, source_target_pairs={{0,16},{8,24},{16,0},{24,8},{1,17},{9,25},{17,1},{25,9},{2,18},{10... | collective-permute-start | bytes 135176 | tf_op jit(solution)/shard_map/ppermute | solution.py:436
  26.7 3.1 %collective-permute-done.8 = f32[88,128]{1,0:T(8,128)S(1)} collective-permute-done((f32[88,128]{1,0:T(8,128)S(1)}, f32[88,128]{1,0:T(8,128)S(1)}, u32[]{:S(2)}, u32[]{:S(2)}) %collective-permute-start.8) | collective-permute-done | bytes 45088 | tf_op jit(solution)/shard_map/ppermute | solution.py:436
  29.8 1.6 %collective-permute-start.9 = (f32[88,128]{1,0:T(8,128)S(1)}, f32[88,128]{1,0:T(8,128)S(1)}, u32[]{:S(2)}, u32[]{:S(2)}) collective-permute-start(f32[88,128]{1,0:T(8,128)S(1)} %add.16), channel_id=1, source_target_pairs={{0,1},{1,0},{2,3},{3,2},{4,5},{5,4},{6,7},{7,6},{8,9},{9,8},{10,11... | collective-permute-start | bytes 135176 | tf_op jit(solution)/shard_map/ppermute | solution.py:436
  31.4 2.5 %collective-permute-done.9 = f32[88,128]{1,0:T(8,128)S(1)} collective-permute-done((f32[88,128]{1,0:T(8,128)S(1)}, f32[88,128]{1,0:T(8,128)S(1)}, u32[]{:S(2)}, u32[]{:S(2)}) %collective-permute-start.9) | collective-permute-done | bytes 45088 | tf_op jit(solution)/shard_map/ppermute | solution.py:436
  33.9 4.5 %collective-permute-start.10 = (f32[88,128]{1,0:T(8,128)S(1)}, f32[88,128]{1,0:T(8,128)S(1)}, u32[]{:S(2)}, u32[]{:S(2)}) collective-permute-start(f32[88,128]{1,0:T(8,128)S(1)} %add.17), channel_id=1, source_target_pairs={{0,2},{2,0},{4,6},{6,4},{1,3},{3,1},{5,7},{7,5},{8,10},{10,8},{12,... | collective-permute-start | bytes 135176 | tf_op jit(solution)/shard_map/ppermute | solution.py:436
  38.4 2.0 %collective-permute-done.10 = f32[88,128]{1,0:T(8,128)S(1)} collective-permute-done((f32[88,128]{1,0:T(8,128)S(1)}, f32[88,128]{1,0:T(8,128)S(1)}, u32[]{:S(2)}, u32[]{:S(2)}) %collective-permute-start.10) | collective-permute-done | bytes 45088 | tf_op jit(solution)/shard_map/ppermute | solution.py:436
  40.4 2.5 %collective-permute-start.11 = (f32[88,128]{1,0:T(8,128)S(1)}, f32[88,128]{1,0:T(8,128)S(1)}, u32[]{:S(2)}, u32[]{:S(2)}) collective-permute-start(f32[88,128]{1,0:T(8,128)S(1)} %add.18), channel_id=1, source_target_pairs={{0,4},{2,6},{4,0},{6,2},{1,5},{3,7},{5,1},{7,3},{8,12},{10,14},{12... | collective-permute-start | bytes 135176 | tf_op jit(solution)/shard_map/ppermute | solution.py:436
  43.0 2.5 %collective-permute-done.11 = f32[88,128]{1,0:T(8,128)S(1)} collective-permute-done((f32[88,128]{1,0:T(8,128)S(1)}, f32[88,128]{1,0:T(8,128)S(1)}, u32[]{:S(2)}, u32[]{:S(2)}) %collective-permute-start.11) | collective-permute-done | bytes 45088 | tf_op jit(solution)/shard_map/ppermute | solution.py:436
  45.4 0.1 collective-permute-start.12
  46.2 0.6 %collective-permute-done.12.other_ref = f32[88,128]{1,0:T(8,128)S(1)} collective-permute-done((f32[88,128]{1,0:T(8,128)S(1)}, f32[88,128]{1,0:T(8,128)S(1)}, u32[]{:S(2)}, u32[]{:S(2)}) %collective-permute-start.12) | collective-permute-done | bytes 45088 | tf_op jit(solution)/shard_map/ppermute | solution.py:436
  46.7 8.3 %shard_map.63 = (f32[4,16,2048]{2,1,0:T(8,128)}, f32[96,128]{1,0:T(8,128)}, f32[128,128]{1,0:T(8,128)}) custom-call(f32[1]{0:T(128)S(6)} %copy.6.shift_ref, f32[1024,128]{1,0:T(8,128)S(1)} %get-tuple-element.16.q_ref, f32[1024,128]{1,0:T(8,128)S(1)} %get-tuple-element.26.s_ref, f32[88,128]{1,0:T(8,128)S(1)} %add.19.mine_ref, ...), custom_call_target="tpu_custom_call" | custom-call | tf_op jit(solution)/shard_map/pallas_call | solution.py:516
  (5 shorter events, 0.0 us)
Async XLA Ops:
  2.1 12.6 %copy-start = (f32[4,16,1536]{2,1,0:T(8,128)S(1)}, f32[4,16,1536]{2,1,0:T(8,128)}, u32[]{:S(2)}) copy-start(f32[4,16,1536]{2,1,0:T(8,128)} %prior_hbm.1) | copy-start | bytes 1179652
  2.2 5.3 %collective-permute-start = (f32[4,16,256]{2,1,0:T(8,128)S(1)}, f32[4,16,256]{2,1,0:T(8,128)S(1)}, u32[]{:S(2)}, u32[]{:S(2)}) collective-permute-start(f32[4,16,256]{2,1,0:T(8,128)S(1)} %get-tuple-element.18), channel_id=1, source_target_pairs={{0,1},{1,0},{2,3},{3,2},{4,5},{5,4},{6,7},{7,6},{8,9},{9,8},{10,11... | collective-permute-start | bytes 196616 | tf_op jit(solution)/shard_map/ppermute | solution.py:443
  7.6 4.3 %collective-permute-start.1 = (f32[4,4,896]{2,1,0:T(4,128)S(1)}, f32[4,4,896]{2,1,0:T(4,128)S(1)}, u32[]{:S(2)}, u32[]{:S(2)}) collective-permute-start(f32[4,4,896]{2,1,0:T(4,128)S(1)} %get-tuple-element.20), channel_id=1, source_target_pairs={{0,2},{2,0},{4,6},{6,4},{1,3},{3,1},{5,7},{7,5},{8,10},{10,8},{12,... | collective-permute-start | bytes 172040 | tf_op jit(solution)/shard_map/ppermute | solution.py:443
  9.7 2.2 %collective-permute-start.2 = (f32[4,4,896]{2,1,0:T(4,128)S(1)}, f32[4,4,896]{2,1,0:T(4,128)S(1)}, u32[]{:S(2)}, u32[]{:S(2)}) collective-permute-start(f32[4,4,896]{2,1,0:T(4,128)S(1)} %get-tuple-element.21), channel_id=1, source_target_pairs={{2,4},{4,2},{3,5},{5,3},{10,12},{12,10},{11,13},{13,11},{18,20},{2... | collective-permute-start | bytes 172040 | tf_op jit(solution)/shard_map/ppermute | solution.py:444
  10.4 5.3 %collective-permute-start.3 = (f32[4,16,640]{2,1,0:T(8,128)S(1)}, f32[4,16,640]{2,1,0:T(8,128)S(1)}, u32[]{:S(2)}, u32[]{:S(2)}) collective-permute-start(f32[4,16,640]{2,1,0:T(8,128)S(1)} %get-tuple-element.17.field_ref), channel_id=1, source_target_pairs={{0,8},{8,0},{16,24},{24,16},{1,9},{9,1},{17,25},{25,17},{2,10},{10... | collective-permute-start | bytes 491528 | tf_op jit(solution)/shard_map/ppermute | solution.py:443
  10.4 5.2 %collective-permute-start.4 = (f32[4,16,640]{2,1,0:T(8,128)S(1)}, f32[4,16,640]{2,1,0:T(8,128)S(1)}, u32[]{:S(2)}, u32[]{:S(2)}) collective-permute-start(f32[4,16,640]{2,1,0:T(8,128)S(1)} %get-tuple-element.17.field_ref), channel_id=1, source_target_pairs={{8,16},{16,8},{9,17},{17,9},{10,18},{18,10},{11,19},{19,11},{12,20... | collective-permute-start | bytes 491528 | tf_op jit(solution)/shard_map/ppermute | solution.py:444
  11.9 3.8 %collective-permute-start.5 = (f32[3,8,1664]{2,1,0:T(8,128)S(1)}, f32[3,8,1664]{2,1,0:T(8,128)S(1)}, u32[]{:S(2)}, u32[]{:S(2)}) collective-permute-start(f32[3,8,1664]{2,1,0:T(8,128)S(1)} %get-tuple-element.23), channel_id=1, source_target_pairs={{0,8},{8,0},{16,24},{24,16},{1,9},{9,1},{17,25},{25,17},{2,10},{10... | collective-permute-start | bytes 479240 | tf_op jit(solution)/shard_map/ppermute | solution.py:443
  14.1 1.6 %collective-permute-start.6 = (f32[3,8,1664]{2,1,0:T(8,128)S(1)}, f32[3,8,1664]{2,1,0:T(8,128)S(1)}, u32[]{:S(2)}, u32[]{:S(2)}) collective-permute-start(f32[3,8,1664]{2,1,0:T(8,128)S(1)} %get-tuple-element.24), channel_id=1, source_target_pairs={{8,16},{16,8},{9,17},{17,9},{10,18},{18,10},{11,19},{19,11},{12,20... | collective-permute-start | bytes 479240 | tf_op jit(solution)/shard_map/ppermute | solution.py:444
  19.8 5.9 %collective-permute-start.7 = (f32[88,128]{1,0:T(8,128)S(1)}, f32[88,128]{1,0:T(8,128)S(1)}, u32[]{:S(2)}, u32[]{:S(2)}) collective-permute-start(f32[88,128]{1,0:T(8,128)S(1)} %get-tuple-element.28), channel_id=1, source_target_pairs={{0,8},{8,0},{16,24},{24,16},{1,9},{9,1},{17,25},{25,17},{2,10},{10... | collective-permute-start | bytes 135176 | tf_op jit(solution)/shard_map/ppermute | solution.py:436
  25.8 4.0 %collective-permute-start.8 = (f32[88,128]{1,0:T(8,128)S(1)}, f32[88,128]{1,0:T(8,128)S(1)}, u32[]{:S(2)}, u32[]{:S(2)}) collective-permute-start(f32[88,128]{1,0:T(8,128)S(1)} %add.15), channel_id=1, source_target_pairs={{0,16},{8,24},{16,0},{24,8},{1,17},{9,25},{17,1},{25,9},{2,18},{10... | collective-permute-start | bytes 135176 | tf_op jit(solution)/shard_map/ppermute | solution.py:436
  29.8 4.1 %collective-permute-start.9 = (f32[88,128]{1,0:T(8,128)S(1)}, f32[88,128]{1,0:T(8,128)S(1)}, u32[]{:S(2)}, u32[]{:S(2)}) collective-permute-start(f32[88,128]{1,0:T(8,128)S(1)} %add.16), channel_id=1, source_target_pairs={{0,1},{1,0},{2,3},{3,2},{4,5},{5,4},{6,7},{7,6},{8,9},{9,8},{10,11... | collective-permute-start | bytes 135176 | tf_op jit(solution)/shard_map/ppermute | solution.py:436
  33.9 6.5 %collective-permute-start.10 = (f32[88,128]{1,0:T(8,128)S(1)}, f32[88,128]{1,0:T(8,128)S(1)}, u32[]{:S(2)}, u32[]{:S(2)}) collective-permute-start(f32[88,128]{1,0:T(8,128)S(1)} %add.17), channel_id=1, source_target_pairs={{0,2},{2,0},{4,6},{6,4},{1,3},{3,1},{5,7},{7,5},{8,10},{10,8},{12,... | collective-permute-start | bytes 135176 | tf_op jit(solution)/shard_map/ppermute | solution.py:436
  40.4 5.0 %collective-permute-start.11 = (f32[88,128]{1,0:T(8,128)S(1)}, f32[88,128]{1,0:T(8,128)S(1)}, u32[]{:S(2)}, u32[]{:S(2)}) collective-permute-start(f32[88,128]{1,0:T(8,128)S(1)} %add.18), channel_id=1, source_target_pairs={{0,4},{2,6},{4,0},{6,2},{1,5},{3,7},{5,1},{7,3},{8,12},{10,14},{12... | collective-permute-start | bytes 135176 | tf_op jit(solution)/shard_map/ppermute | solution.py:436
  45.4 1.3 %collective-permute-start.12 = (f32[88,128]{1,0:T(8,128)S(1)}, f32[88,128]{1,0:T(8,128)S(1)}, u32[]{:S(2)}, u32[]{:S(2)}) collective-permute-start(f32[88,128]{1,0:T(8,128)S(1)} %add.19.mine_ref), channel_id=1, source_target_pairs={{0,8},{8,0},{16,24},{24,16},{1,9},{9,1},{17,25},{25,17},{2,10},{10... | collective-permute-start | bytes 135176 | tf_op jit(solution)/shard_map/ppermute | solution.py:436

commit v4 on v3

--- a/solution.py
+++ b/solution.py
@@ -7,6 +7,7 @@
 from jax.experimental import pallas as pl
 from jax.experimental.pallas import tpu as pltpu
 from jax.sharding import PartitionSpec as P
+
 
 BLOCK = 32
 POWERS = 4
@@ -45,6 +46,17 @@
 
 def even_on(axis):
     return lax.axis_index(axis) % 2 == 0
+
+
+def last_on(axis):
+    return lax.axis_index(axis) == lax.axis_size(axis) - 1
+
+
+def sides(axis, first, second):
+    even = even_on(axis)
+    above = jnp.where(last_on(axis), 0.0, jnp.where(even, first, second))
+    below = jnp.where(lax.axis_index(axis) == 0, 0.0, jnp.where(even, second, first))
+    return above, below
 
 
 def pick(even, first, second):
@@ -93,13 +105,13 @@
     size_z = own // BLOCK
     lane = lane_of((size_y, LANES))
     upper = (lane % size_z) < size_z // 2
-    even, even_y = even_on("gz"), even_on("gy")
+    even_y = even_on("gy")
     zero = jnp.zeros((size_y, LANES), F32)
     for i in range(size_x):
         values = [ref[i, :, :LANES] for ref in halo_refs] + [zero, zero]
         others = [ref[i, :, LANES:] for ref in halo_refs] + [zero, zero]
-        above, below = pick(even, values[0], values[1]), pick(even, values[1], values[0])
-        above_w, below_w = pick(even, others[0], others[1]), pick(even, others[1], others[0])
+        above, below = sides("gz", values[0], values[1])
+        above_w, below_w = sides("gz", others[0], others[1])
         other = pltpu.roll(jnp.where(upper, above_w, below_w), 3 * size_z, 1)
         weights = jnp.where(lane < 3 * size_z, field_ref[i, :, own:], jnp.where(lane < 6 * size_z, other, zero))
         row = jnp.concatenate([field_ref[i, :, :own], above, below, weights], axis=1)
@@ -111,13 +123,12 @@
 
 def lengthen_body(wide_ref, first_ref, second_ref, long_ref, *rest_refs):
     size_x, size_y, width = wide_ref.shape
-    even, even_x = even_on("gy"), even_on("gx")
+    even_x = even_on("gx")
     rest = []
     for i in range(size_x):
         wide = wide_ref[i]
         long_ref[i, :size_y] = wide
-        first, second = first_ref[i], second_ref[i]
-        halo = jnp.concatenate([pick(even, first, second), pick(even, second, first)], axis=0)
+        halo = jnp.concatenate(sides("gy", first_ref[i], second_ref[i]), axis=0)
         long_ref[i, size_y:] = halo
         side = wide[:, width - 3 * LANES :]
         pieces = [side[row : row + SUBLANES] for row in range(0, size_y, SUBLANES)]
@@ -154,10 +165,6 @@
     inner_ref[...] = contract(rows, rows)[:BASIS]
 
 
-def last_on(axis):
-    return lax.axis_index(axis) == lax.axis_size(axis) - 1
-
-
 def exact_dot(values, selector):
     high = values.astype(BF16)
     rest = values - high.astype(F32)
@@ -173,13 +180,12 @@
     field = width - LANES
     own = size_z * BLOCK
     planes = size_x + 2 * POWERS
-    even = even_on("gx")
     joined[:size_x] = own_ref[...]
     for at in range(POWERS):
-        near, far = near_ref[at], far_ref[at]
-        above, below = size_x + at, size_x + POWERS + at
-        near_high, far_high = near_ref[near_ref.shape[0] - POWERS + at], far_ref[near_ref.shape[0] - POWERS + at]
-        for p, value in ((above, pick(even, near, far)), (below, pick(even, far_high, near_high))):
+        high = near_ref.shape[0] - POWERS + at
+        above, _ = sides("gx", near_ref[at], far_ref[at])
+        _, below = sides("gx", near_ref[high], far_ref[high])
+        for p, value in ((size_x + at, above), (size_x + POWERS + at, below)):
             joined[p, :size_y, :own] = value[:, :own]
             joined[p, :size_y, field:] = value[:, own:]
     zero = jnp.zeros((size_y, 2 * LANES), F32)
@@ -187,8 +193,8 @@
         joined[p, :size_y, own:field] = zero
         joined[p, size_y:] = jnp.zeros((2 * POWERS, width), F32)
     for at in range(POWERS - 1):
-        near, far = near_rest_ref[at], far_rest_ref[at]
-        for p, value in ((size_x + at, pick(even, near, far)), (size_x + POWERS + 1 + at, pick(even, far, near))):
+        above, below = sides("gx", near_rest_ref[at], far_rest_ref[at])
+        for p, value in ((size_x + at, above), (size_x + POWERS + 1 + at, below)):
             for part in range(size_y // SUBLANES):
                 lanes = slice(3 * part * LANES, 3 * (part + 1) * LANES)
                 joined[p, part * SUBLANES : (part + 1) * SUBLANES, own:] = value[:, lanes]
@@ -386,7 +392,7 @@
     sums = jnp.concatenate([pick(even, mine, other), pick(even, other, mine)], axis=0)
     dot = functools.partial(jnp.dot, precision=PRECISE, preferred_element_type=F32)
 
-    centre, spread = (DEGREE + shift_ref[0]) * (1.0 / OPERATOR_SCALE) - 1.0, math.sqrt(DEGREE) / OPERATOR_SCALE
+    centre, spread = shift_ref[0] * (1.0 / OPERATOR_SCALE) - 1.0, math.sqrt(DEGREE) / OPERATOR_SCALE
     t, s = basis_change(centre, spread)
     constant = per_block([t[k][0] for k in range(1, POWERS + 1)])
     removed = per_block([-s[k][0] for k in range(1, POWERS + 1)])
@@ -436,12 +442,22 @@
     return lax.ppermute(values, axis, [(i, i ^ step) for i in range(count)])
 
 
-def exchange(first, second, axis):
-    count = lax.axis_size(axis)
-    pairs = [(i, i ^ 1) for i in range(count) if i ^ 1 < count]
-    across = [(i, j) for k in range(1, count - 1, 2) for i, j in ((k, k + 1), (k + 1, k))]
-    got = [lax.ppermute(first, axis, pairs)] if pairs else []
-    return got + ([lax.ppermute(second, axis, across)] if across else [])
+def exchange(first, second, axis, helper):
+    count, others = lax.axis_size(axis), lax.axis_size(helper)
+    near = [(i, i + 1) for i in range(0, count - 1, 2)]
+    far = [(i, i + 1) for i in range(1, count - 1, 2)]
+    axes = tuple(name for name in AXES if name in (axis, helper))
+    place = lambda at: at[0] * others + at[1] if axes[0] == axis else at[1] * count + at[0]
+    got = []
+    for value, pairs in ((first, near), (second, far)):
+        if not pairs:
+            continue
+        links = [((i, k), (j, k)) for pair in pairs for i, j in (pair, pair[::-1]) for k in range(others)]
+        if others % 2 == 0:
+            alone = [i for i in range(count) if not any(i in pair for pair in pairs)]
+            links += [((i, k), (i, k ^ 1)) for i in alone for k in range(others)]
+        got.append(lax.ppermute(value, axes, [(place(source), place(target)) for source, target in links]))
+    return got
 
 
 def filled(halos, like):
@@ -453,7 +469,7 @@
     return [1 << k for k in range(count.bit_length() - 1)]
 
 
-def per_device(prior_basis, edge_weights, spectral_shift):
+def cycle(prior_basis, edge_weights, spectral_shift):
     size_x, size_y, _ = prior_basis.shape
     size_z = prior_basis.shape[2] // BASIS
     own = size_z * BLOCK
@@ -475,8 +491,9 @@
         ],
         [hbm, hbm],
     )(*(pltpu.with_memory_space_constraint(array, pltpu.HBM) for array in (prior_basis, edge_weights)))
-    halos = exchange(faces[0], faces[-1], "gz") if faces else []
-    planes_x = filled(exchange(field, field, "gx"), field)
+    halos = exchange(faces[0], faces[-1], "gz", "gx") if faces else []
+    planes_x = filled(exchange(field, field, "gx", "gz"), field)
+    degree_shift = spectral_shift + DEGREE
     prior_rows, inner = kernel_call(
         prior_body,
         [(cell_local, LANES), (BASIS, LANES)],
@@ -486,10 +503,10 @@
     wide, first, second = kernel_call(
         widen_body, [(size_x, size_y, width)] + [(size_x, POWERS, width)] * 2
     )(field, *halos)
-    halos = filled(exchange(first, second, "gy"), first)
+    halos = filled(exchange(first, second, "gy", "gx"), first)
     rest = (POWERS - 1, SUBLANES, 3 * LANES * (size_y // SUBLANES) + width)
     long, first, second = kernel_call(lengthen_body, [(size_x, size_y + 2 * POWERS, width), rest, rest])(wide, *halos)
-    rests = filled(exchange(first, second, "gx"), first)
+    rests = filled(exchange(first, second, "gx", "gz"), first)
 
     rows, planes, lanes = size_y + 2 * POWERS, size_x + 2 * POWERS, own + 2 * LANES
     sum_rows = BASIS + 80
@@ -527,13 +544,13 @@
             pltpu.VMEM((WIDE, WIDE), F32),
         ],
         compiler_params=pltpu.CompilerParams(vmem_limit_bytes=24 * 1024 * 1024),
-    )(spectral_shift, prior_rows, columns, total, other)
+    )(degree_shift, prior_rows, columns, total, other)
     return new_basis, projection, triangle
 
 
 def solution(mesh):
     return jax.shard_map(
-        per_device,
+        cycle,
         mesh=mesh,
         in_specs=(P("gx", "gy", "gz"), P(None, "gx", "gy", "gz"), P()),
         out_specs=(P("gx", "gy", "gz"), P(), P()),

time: 55.2 us -> 51.6 us (0.935)
  starting transfers between devices: 24.1 us -> 19.8 us
  waiting for transfers between devices: 14.6 us -> 15.3 us
    ppermute x6, starting transfers between devices: 14.6 us -> 10.4 us  [swap(): return lax.ppermute(values, axis, [(i, i ^ step) for i in range(count)])]
    ppermute x7, waiting for transfers between devices: 3 us -> 4.79 us  [exchange(): lax.ppermute(value, axes, [(place(source), place(target)) for source, tar...]
    ppermute x6, waiting for transfers between devices: 11.6 us -> 10.5 us  [swap(): return lax.ppermute(values, axis, [(i, i ^ step) for i in range(count)])]
  transfers between devices with their start and end apart: 13 -> 13, of which waited for: 8 -> 10; matrix products, arithmetic and copies ran while one was open for 0% -> 0% of each run, Pallas kernels for 2% -> 2%
where the time goes in v4:
time: 51.6 us; the launch traced here: 51.4 us
  starting transfers between devices  19.8 us (38%)
  waiting for transfers between devices  15.3 us (30%)
  Pallas kernels  15 us (29%)
  between operations  1.36 us (3%)
    ppermute x6, waiting for transfers between devices, swap(): return lax.ppermute(values, axis, [(i, i ^ step) for i in range(count)])  10.5 us
    ppermute x6, starting transfers between devices, swap(): return lax.ppermute(values, axis, [(i, i ^ step) for i in range(count)])  10.4 us
    ppermute x7, starting transfers between devices, exchange(): lax.ppermute(value, axes, [(place(source), place(target)) for source, tar...  9.33 us
    pallas_call x1, Pallas kernels, cycle(): pl.pallas_call(functools.partial(finish_body, 1.0 / cell_count), in_specs...  8.32 us
    ppermute x7, waiting for transfers between devices, exchange(): lax.ppermute(value, axes, [(place(source), place(target)) for source, tar...  4.79 us
    pallas_call x1, Pallas kernels, cycle(): kernel_call(functools.partial(columns_body, size_z), [(cell_local, WIDE),...  4.12 us
    pallas_call x1, Pallas kernels, cycle(): kernel_call(pack_body, [(size_x, size_y, own + LANES)] + [(size_x, size_y...  1.51 us
  transfers between devices with their start and end apart: 13, of which 10 were waited for; matrix products, arithmetic and copies ran while one was open for 0% of the time, Pallas kernels for 2%

profile of v4, /device:TPU:0, one launch (start us, length us, event | category | flops | bytes accessed | tf_op | source)
XLA Modules:
  0.0 51.4 jit_solution(8791052463523212136)
XLA Ops:
  0.6 1.5 %shard_map.59 = (f32[4,16,640]{2,1,0:T(8,128)S(1)}, f32[4,16,256]{2,1,0:T(8,128)S(1)}) custom-call(f32[4,16,1536]{2,1,0:T(8,128)} %prior_hbm.1, f32[3,4,16,16]{3,2,1,0:T(8,128)} %weights_hbm.1), custom_call_target="tpu_custom_call" | custom-call | tf_op jit(solution)/shard_map/pallas_call | solution.py:483
  2.1 0.0 copy-start
  2.2 3.1 %collective-permute-start = (f32[4,16,256]{2,1,0:T(8,128)S(1)}, f32[4,16,256]{2,1,0:T(8,128)S(1)}, u32[]{:S(2)}, u32[]{:S(2)}) collective-permute-start(f32[4,16,256]{2,1,0:T(8,128)S(1)} %get-tuple-element.18), channel_id=1, source_target_pairs={{0,1},{8,9},{16,17},{24,25},{1,0},{9,8},{17,16},{25,24},{2,3},{10,... | collective-permute-start | bytes 196616 | tf_op jit(solution)/shard_map/ppermute | solution.py:459
  5.2 2.2 %collective-permute-done.refs_0_ = f32[4,16,256]{2,1,0:T(8,128)S(1)} collective-permute-done((f32[4,16,256]{2,1,0:T(8,128)S(1)}, f32[4,16,256]{2,1,0:T(8,128)S(1)}, u32[]{:S(2)}, u32[]{:S(2)}) %collective-permute-start) | collective-permute-done | bytes 65568 | tf_op jit(solution)/shard_map/ppermute | solution.py:459
  7.5 0.1 shard_map.60
  7.6 2.1 %collective-permute-start.1 = (f32[4,4,896]{2,1,0:T(4,128)S(1)}, f32[4,4,896]{2,1,0:T(4,128)S(1)}, u32[]{:S(2)}, u32[]{:S(2)}) collective-permute-start(f32[4,4,896]{2,1,0:T(4,128)S(1)} %get-tuple-element.20), channel_id=1, source_target_pairs={{0,2},{8,10},{16,18},{24,26},{2,0},{10,8},{18,16},{26,24},{4,6},{1... | collective-permute-start | bytes 172040 | tf_op jit(solution)/shard_map/ppermute | solution.py:459
  9.7 0.0 collective-permute-start.2
  9.7 0.5 collective-permute-start.3
  10.2 1.5 %collective-permute-start.4 = (f32[4,16,640]{2,1,0:T(8,128)S(1)}, f32[4,16,640]{2,1,0:T(8,128)S(1)}, u32[]{:S(2)}, u32[]{:S(2)}) collective-permute-start(f32[4,16,640]{2,1,0:T(8,128)S(1)} %get-tuple-element.17.field_ref), channel_id=1, source_target_pairs={{8,16},{9,17},{16,8},{17,9},{0,1},{1,0},{24,25},{25,24},{10,18},{1... | collective-permute-start | bytes 491528 | tf_op jit(solution)/shard_map/ppermute | solution.py:459
  11.7 0.1 collective-permute-done.1.first_ref
  11.9 0.0 collective-permute-done.2.second_ref
  11.9 0.1 shard_map.61
  11.9 0.1 collective-permute-start.5
  12.0 2.0 %collective-permute-start.6 = (f32[3,8,1664]{2,1,0:T(8,128)S(1)}, f32[3,8,1664]{2,1,0:T(8,128)S(1)}, u32[]{:S(2)}, u32[]{:S(2)}) collective-permute-start(f32[3,8,1664]{2,1,0:T(8,128)S(1)} %get-tuple-element.24), channel_id=1, source_target_pairs={{8,16},{9,17},{16,8},{17,9},{0,1},{1,0},{24,25},{25,24},{10,18},{1... | collective-permute-start | bytes 479240 | tf_op jit(solution)/shard_map/ppermute | solution.py:459
  14.0 0.0 copy-done
  14.0 0.9 %shard_map.58 = (f32[1024,128]{1,0:T(8,128)S(1)}, f32[96,128]{1,0:T(8,128)S(1)}) custom-call(f32[4,16,1536]{2,1,0:T(8,128)S(1)} %copy-done), custom_call_target="tpu_custom_call" | custom-call | flops 201326592 | bytes 393216 | tf_op jit(solution)/shard_map/pallas_call | solution.py:497
  14.9 0.0 collective-permute-done.3.near_ref
  14.9 0.6 %collective-permute-done.4.far_ref = f32[4,16,640]{2,1,0:T(8,128)S(1)} collective-permute-done((f32[4,16,640]{2,1,0:T(8,128)S(1)}, f32[4,16,640]{2,1,0:T(8,128)S(1)}, u32[]{:S(2)}, u32[]{:S(2)}) %collective-permute-start.4) | collective-permute-done | bytes 163872 | tf_op jit(solution)/shard_map/ppermute | solution.py:459
  15.5 0.0 collective-permute-done.5.near_rest_ref
  15.5 1.8 %collective-permute-done.6.far_rest_ref = f32[3,8,1664]{2,1,0:T(8,128)S(1)} collective-permute-done((f32[3,8,1664]{2,1,0:T(8,128)S(1)}, f32[3,8,1664]{2,1,0:T(8,128)S(1)}, u32[]{:S(2)}, u32[]{:S(2)}) %collective-permute-start.6) | collective-permute-done | bytes 159776 | tf_op jit(solution)/shard_map/ppermute | solution.py:459
  17.3 4.1 %shard_map.62 = (f32[1024,128]{1,0:T(8,128)S(1)}, f32[88,128]{1,0:T(8,128)S(1)}, f32[88,128]{1,0:T(8,128)S(1)}) custom-call(f32[4,24,896]{2,1,0:T(8,128)S(1)} %get-tuple-element.22.own_ref, f32[4,16,640]{2,1,0:T(8,128)S(1)} %collective-permute-done.3.near_ref, f32[4,16,640]{2,1,0:T(8,128)S(1)} %collective-permute-done.4.far_ref, ...), custom_call_target="tpu_custom_call" | custom-call | tf_op jit(solution)/shard_map/pallas_call | solution.py:514
  21.5 0.2 collective-permute-start.7
  21.7 1.1 %collective-permute-done.7 = f32[88,128]{1,0:T(8,128)S(1)} collective-permute-done((f32[88,128]{1,0:T(8,128)S(1)}, f32[88,128]{1,0:T(8,128)S(1)}, u32[]{:S(2)}, u32[]{:S(2)}) %collective-permute-start.7) | collective-permute-done | bytes 45088 | tf_op jit(solution)/shard_map/ppermute | solution.py:442
  22.8 1.4 %collective-permute-start.8 = (f32[88,128]{1,0:T(8,128)S(1)}, f32[88,128]{1,0:T(8,128)S(1)}, u32[]{:S(2)}, u32[]{:S(2)}) collective-permute-start(f32[88,128]{1,0:T(8,128)S(1)} %add.19), channel_id=1, source_target_pairs={{0,16},{8,24},{16,0},{24,8},{1,17},{9,25},{17,1},{25,9},{2,18},{10... | collective-permute-start | bytes 135176 | tf_op jit(solution)/shard_map/ppermute | solution.py:442
  24.2 2.7 %collective-permute-done.8 = f32[88,128]{1,0:T(8,128)S(1)} collective-permute-done((f32[88,128]{1,0:T(8,128)S(1)}, f32[88,128]{1,0:T(8,128)S(1)}, u32[]{:S(2)}, u32[]{:S(2)}) %collective-permute-start.8) | collective-permute-done | bytes 45088 | tf_op jit(solution)/shard_map/ppermute | solution.py:442
  26.9 2.0 %collective-permute-start.9 = (f32[88,128]{1,0:T(8,128)S(1)}, f32[88,128]{1,0:T(8,128)S(1)}, u32[]{:S(2)}, u32[]{:S(2)}) collective-permute-start(f32[88,128]{1,0:T(8,128)S(1)} %add.20), channel_id=1, source_target_pairs={{0,1},{1,0},{2,3},{3,2},{4,5},{5,4},{6,7},{7,6},{8,9},{9,8},{10,11... | collective-permute-start | bytes 135176 | tf_op jit(solution)/shard_map/ppermute | solution.py:442
  28.9 2.1 %collective-permute-done.9 = f32[88,128]{1,0:T(8,128)S(1)} collective-permute-done((f32[88,128]{1,0:T(8,128)S(1)}, f32[88,128]{1,0:T(8,128)S(1)}, u32[]{:S(2)}, u32[]{:S(2)}) %collective-permute-start.9) | collective-permute-done | bytes 45088 | tf_op jit(solution)/shard_map/ppermute | solution.py:442
  31.0 3.2 %collective-permute-start.10 = (f32[88,128]{1,0:T(8,128)S(1)}, f32[88,128]{1,0:T(8,128)S(1)}, u32[]{:S(2)}, u32[]{:S(2)}) collective-permute-start(f32[88,128]{1,0:T(8,128)S(1)} %add.21), channel_id=1, source_target_pairs={{0,2},{2,0},{4,6},{6,4},{1,3},{3,1},{5,7},{7,5},{8,10},{10,8},{12,... | collective-permute-start | bytes 135176 | tf_op jit(solution)/shard_map/ppermute | solution.py:442
  34.2 2.0 %collective-permute-done.10 = f32[88,128]{1,0:T(8,128)S(1)} collective-permute-done((f32[88,128]{1,0:T(8,128)S(1)}, f32[88,128]{1,0:T(8,128)S(1)}, u32[]{:S(2)}, u32[]{:S(2)}) %collective-permute-start.10) | collective-permute-done | bytes 45088 | tf_op jit(solution)/shard_map/ppermute | solution.py:442
  36.2 3.5 %collective-permute-start.11 = (f32[88,128]{1,0:T(8,128)S(1)}, f32[88,128]{1,0:T(8,128)S(1)}, u32[]{:S(2)}, u32[]{:S(2)}) collective-permute-start(f32[88,128]{1,0:T(8,128)S(1)} %add.22), channel_id=1, source_target_pairs={{0,4},{2,6},{4,0},{6,2},{1,5},{3,7},{5,1},{7,3},{8,12},{10,14},{12... | collective-permute-start | bytes 135176 | tf_op jit(solution)/shard_map/ppermute | solution.py:442
  39.8 2.0 %collective-permute-done.11 = f32[88,128]{1,0:T(8,128)S(1)} collective-permute-done((f32[88,128]{1,0:T(8,128)S(1)}, f32[88,128]{1,0:T(8,128)S(1)}, u32[]{:S(2)}, u32[]{:S(2)}) %collective-permute-start.11) | collective-permute-done | bytes 45088 | tf_op jit(solution)/shard_map/ppermute | solution.py:442
  41.8 0.1 collective-permute-start.12
  42.5 0.6 %collective-permute-done.12.other_ref = f32[88,128]{1,0:T(8,128)S(1)} collective-permute-done((f32[88,128]{1,0:T(8,128)S(1)}, f32[88,128]{1,0:T(8,128)S(1)}, u32[]{:S(2)}, u32[]{:S(2)}) %collective-permute-start.12) | collective-permute-done | bytes 45088 | tf_op jit(solution)/shard_map/ppermute | solution.py:442
  43.1 8.3 %shard_map.63 = (f32[4,16,2048]{2,1,0:T(8,128)}, f32[96,128]{1,0:T(8,128)}, f32[128,128]{1,0:T(8,128)}) custom-call(f32[1]{0:T(128)S(6)} %add.18.shift_ref, f32[1024,128]{1,0:T(8,128)S(1)} %get-tuple-element.16.q_ref, f32[1024,128]{1,0:T(8,128)S(1)} %get-tuple-element.26.s_ref, f32[88,128]{1,0:T(8,128)S(1)} %add.23.mine_ref, ...), custom_call_target="tpu_custom_call" | custom-call | tf_op jit(solution)/shard_map/pallas_call | solution.py:533
  (5 shorter events, 0.0 us)
Async XLA Ops:
  2.1 11.9 %copy-start = (f32[4,16,1536]{2,1,0:T(8,128)S(1)}, f32[4,16,1536]{2,1,0:T(8,128)}, u32[]{:S(2)}) copy-start(f32[4,16,1536]{2,1,0:T(8,128)} %prior_hbm.1) | copy-start | bytes 1179652
  2.2 5.3 %collective-permute-start = (f32[4,16,256]{2,1,0:T(8,128)S(1)}, f32[4,16,256]{2,1,0:T(8,128)S(1)}, u32[]{:S(2)}, u32[]{:S(2)}) collective-permute-start(f32[4,16,256]{2,1,0:T(8,128)S(1)} %get-tuple-element.18), channel_id=1, source_target_pairs={{0,1},{8,9},{16,17},{24,25},{1,0},{9,8},{17,16},{25,24},{2,3},{10,... | collective-permute-start | bytes 196616 | tf_op jit(solution)/shard_map/ppermute | solution.py:459
  7.6 4.3 %collective-permute-start.1 = (f32[4,4,896]{2,1,0:T(4,128)S(1)}, f32[4,4,896]{2,1,0:T(4,128)S(1)}, u32[]{:S(2)}, u32[]{:S(2)}) collective-permute-start(f32[4,4,896]{2,1,0:T(4,128)S(1)} %get-tuple-element.20), channel_id=1, source_target_pairs={{0,2},{8,10},{16,18},{24,26},{2,0},{10,8},{18,16},{26,24},{4,6},{1... | collective-permute-start | bytes 172040 | tf_op jit(solution)/shard_map/ppermute | solution.py:459
  9.7 2.2 %collective-permute-start.2 = (f32[4,4,896]{2,1,0:T(4,128)S(1)}, f32[4,4,896]{2,1,0:T(4,128)S(1)}, u32[]{:S(2)}, u32[]{:S(2)}) collective-permute-start(f32[4,4,896]{2,1,0:T(4,128)S(1)} %get-tuple-element.21), channel_id=1, source_target_pairs={{2,4},{10,12},{18,20},{26,28},{4,2},{12,10},{20,18},{28,26},{0,8},... | collective-permute-start | bytes 172040 | tf_op jit(solution)/shard_map/ppermute | solution.py:459
  9.7 5.2 %collective-permute-start.3 = (f32[4,16,640]{2,1,0:T(8,128)S(1)}, f32[4,16,640]{2,1,0:T(8,128)S(1)}, u32[]{:S(2)}, u32[]{:S(2)}) collective-permute-start(f32[4,16,640]{2,1,0:T(8,128)S(1)} %get-tuple-element.17.field_ref), channel_id=1, source_target_pairs={{0,8},{1,9},{8,0},{9,1},{16,24},{17,25},{24,16},{25,17},{2,10},{3,... | collective-permute-start | bytes 491528 | tf_op jit(solution)/shard_map/ppermute | solution.py:459
  10.2 5.3 %collective-permute-start.4 = (f32[4,16,640]{2,1,0:T(8,128)S(1)}, f32[4,16,640]{2,1,0:T(8,128)S(1)}, u32[]{:S(2)}, u32[]{:S(2)}) collective-permute-start(f32[4,16,640]{2,1,0:T(8,128)S(1)} %get-tuple-element.17.field_ref), channel_id=1, source_target_pairs={{8,16},{9,17},{16,8},{17,9},{0,1},{1,0},{24,25},{25,24},{10,18},{1... | collective-permute-start | bytes 491528 | tf_op jit(solution)/shard_map/ppermute | solution.py:459
  11.9 3.6 %collective-permute-start.5 = (f32[3,8,1664]{2,1,0:T(8,128)S(1)}, f32[3,8,1664]{2,1,0:T(8,128)S(1)}, u32[]{:S(2)}, u32[]{:S(2)}) collective-permute-start(f32[3,8,1664]{2,1,0:T(8,128)S(1)} %get-tuple-element.23), channel_id=1, source_target_pairs={{0,8},{1,9},{8,0},{9,1},{16,24},{17,25},{24,16},{25,17},{2,10},{3,... | collective-permute-start | bytes 479240 | tf_op jit(solution)/shard_map/ppermute | solution.py:459
  12.0 5.3 %collective-permute-start.6 = (f32[3,8,1664]{2,1,0:T(8,128)S(1)}, f32[3,8,1664]{2,1,0:T(8,128)S(1)}, u32[]{:S(2)}, u32[]{:S(2)}) collective-permute-start(f32[3,8,1664]{2,1,0:T(8,128)S(1)} %get-tuple-element.24), channel_id=1, source_target_pairs={{8,16},{9,17},{16,8},{17,9},{0,1},{1,0},{24,25},{25,24},{10,18},{1... | collective-permute-start | bytes 479240 | tf_op jit(solution)/shard_map/ppermute | solution.py:459
  21.5 1.3 %collective-permute-start.7 = (f32[88,128]{1,0:T(8,128)S(1)}, f32[88,128]{1,0:T(8,128)S(1)}, u32[]{:S(2)}, u32[]{:S(2)}) collective-permute-start(f32[88,128]{1,0:T(8,128)S(1)} %get-tuple-element.28), channel_id=1, source_target_pairs={{0,8},{8,0},{16,24},{24,16},{1,9},{9,1},{17,25},{25,17},{2,10},{10... | collective-permute-start | bytes 135176 | tf_op jit(solution)/shard_map/ppermute | solution.py:442
  22.8 4.1 %collective-permute-start.8 = (f32[88,128]{1,0:T(8,128)S(1)}, f32[88,128]{1,0:T(8,128)S(1)}, u32[]{:S(2)}, u32[]{:S(2)}) collective-permute-start(f32[88,128]{1,0:T(8,128)S(1)} %add.19), channel_id=1, source_target_pairs={{0,16},{8,24},{16,0},{24,8},{1,17},{9,25},{17,1},{25,9},{2,18},{10... | collective-permute-start | bytes 135176 | tf_op jit(solution)/shard_map/ppermute | solution.py:442
  26.9 4.1 %collective-permute-start.9 = (f32[88,128]{1,0:T(8,128)S(1)}, f32[88,128]{1,0:T(8,128)S(1)}, u32[]{:S(2)}, u32[]{:S(2)}) collective-permute-start(f32[88,128]{1,0:T(8,128)S(1)} %add.20), channel_id=1, source_target_pairs={{0,1},{1,0},{2,3},{3,2},{4,5},{5,4},{6,7},{7,6},{8,9},{9,8},{10,11... | collective-permute-start | bytes 135176 | tf_op jit(solution)/shard_map/ppermute | solution.py:442
  31.0 5.2 %collective-permute-start.10 = (f32[88,128]{1,0:T(8,128)S(1)}, f32[88,128]{1,0:T(8,128)S(1)}, u32[]{:S(2)}, u32[]{:S(2)}) collective-permute-start(f32[88,128]{1,0:T(8,128)S(1)} %add.21), channel_id=1, source_target_pairs={{0,2},{2,0},{4,6},{6,4},{1,3},{3,1},{5,7},{7,5},{8,10},{10,8},{12,... | collective-permute-start | bytes 135176 | tf_op jit(solution)/shard_map/ppermute | solution.py:442
  36.2 5.6 %collective-permute-start.11 = (f32[88,128]{1,0:T(8,128)S(1)}, f32[88,128]{1,0:T(8,128)S(1)}, u32[]{:S(2)}, u32[]{:S(2)}) collective-permute-start(f32[88,128]{1,0:T(8,128)S(1)} %add.22), channel_id=1, source_target_pairs={{0,4},{2,6},{4,0},{6,2},{1,5},{3,7},{5,1},{7,3},{8,12},{10,14},{12... | collective-permute-start | bytes 135176 | tf_op jit(solution)/shard_map/ppermute | solution.py:442
  41.8 1.3 %collective-permute-start.12 = (f32[88,128]{1,0:T(8,128)S(1)}, f32[88,128]{1,0:T(8,128)S(1)}, u32[]{:S(2)}, u32[]{:S(2)}) collective-permute-start(f32[88,128]{1,0:T(8,128)S(1)} %add.23.mine_ref), channel_id=1, source_target_pairs={{0,8},{8,0},{16,24},{24,16},{1,9},{9,1},{17,25},{25,17},{2,10},{10... | collective-permute-start | bytes 135176 | tf_op jit(solution)/shard_map/ppermute | solution.py:442

commit v5 on v4

--- a/solution.py
+++ b/solution.py
@@ -36,7 +36,7 @@
     options = {} if in_specs is None else {"in_specs": in_specs}
     return pl.pallas_call(
         body,
-        out_shape=[jax.ShapeDtypeStruct(shape, F32) for shape in shapes],
+        out_shape=[shape if isinstance(shape, jax.ShapeDtypeStruct) else jax.ShapeDtypeStruct(shape, F32) for shape in shapes],
         scratch_shapes=list(scratch),
         compiler_params=pltpu.CompilerParams(vmem_limit_bytes=limit),
         cost_estimate=cost,
@@ -98,8 +98,16 @@
             face_ref[i, :, :LANES] = face
 
 
+def nearest(planes, refs):
+    even = even_on("gx")
+    for at in range(POWERS - 1):
+        low, high = planes[at], planes[len(planes) - POWERS + 1 + at]
+        refs[0][at] = pick(even, high, low)
+        refs[1][at] = pick(even, low, high)
+
+
 def widen_body(field_ref, *refs):
-    halo_refs, (wide_ref, *face_refs) = refs[:-3], refs[-3:]
+    halo_refs, (wide_ref, *face_refs) = refs[:-5], refs[-5:]
     size_x, size_y, width = field_ref.shape
     own = width - LANES
     size_z = own // BLOCK
@@ -107,6 +115,7 @@
     upper = (lane % size_z) < size_z // 2
     even_y = even_on("gy")
     zero = jnp.zeros((size_y, LANES), F32)
+    side = []
     for i in range(size_x):
         values = [ref[i, :, :LANES] for ref in halo_refs] + [zero, zero]
         others = [ref[i, :, LANES:] for ref in halo_refs] + [zero, zero]
@@ -119,24 +128,19 @@
         low, high = row[:POWERS], row[size_y - POWERS :]
         face_refs[0][i] = pick(even_y, high, low)
         face_refs[1][i] = pick(even_y, low, high)
+        side.append(row[:, own:])
+    nearest(side, face_refs[2:])
 
 
 def lengthen_body(wide_ref, first_ref, second_ref, long_ref, *rest_refs):
-    size_x, size_y, width = wide_ref.shape
-    even_x = even_on("gx")
+    size_x, size_y, _ = wide_ref.shape
     rest = []
     for i in range(size_x):
-        wide = wide_ref[i]
-        long_ref[i, :size_y] = wide
+        long_ref[i, :size_y] = wide_ref[i]
         halo = jnp.concatenate(sides("gy", first_ref[i], second_ref[i]), axis=0)
         long_ref[i, size_y:] = halo
-        side = wide[:, width - 3 * LANES :]
-        pieces = [side[row : row + SUBLANES] for row in range(0, size_y, SUBLANES)]
-        rest.append(jnp.concatenate(pieces + [halo], axis=1))
-    for at in range(POWERS - 1):
-        low, high = rest[at], rest[size_x - POWERS + 1 + at]
-        rest_refs[0][at] = pick(even_x, high, low)
-        rest_refs[1][at] = pick(even_x, low, high)
+        rest.append(halo)
+    nearest(rest, rest_refs)
 
 
 def contract(left, right):
@@ -145,7 +149,7 @@
     )
 
 
-def prior_body(prior_ref, q_ref, inner_ref):
+def prior_body(prior_ref, q_ref, parts_ref, inner_ref):
     size_x, size_y, width = prior_ref.shape
     size_z = width // BASIS
     lane = lane_of((size_y, LANES))
@@ -163,18 +167,25 @@
                 q_ref[at : at + size_y] = jnp.where(lane < BASIS, rows[r], 0.0)
     rows = q_ref[...]
     inner_ref[...] = contract(rows, rows)[:BASIS]
-
-
-def exact_dot(values, selector):
+    parts_ref[:, :LANES], parts_ref[:, LANES:] = halves(rows)
+
+
+def halves(values):
     high = values.astype(BF16)
-    rest = values - high.astype(F32)
-    middle = rest.astype(BF16)
-    low = (rest - middle.astype(F32)).astype(BF16)
-    dot = functools.partial(jnp.dot, preferred_element_type=F32)
-    return dot(high, selector) + dot(middle, selector) + dot(low, selector)
-
-
-def columns_body(size_z, own_ref, near_ref, far_ref, near_rest_ref, far_rest_ref, q_ref, inner_ref, s_ref, keep_ref, give_ref, joined, coupling, diagonal, levels, sums):
+    return high, (values - high.astype(F32)).astype(BF16)
+
+
+def wide_dot(left_parts, right):
+    high, low = halves(right)
+    stacked = jnp.concatenate(
+        [jnp.concatenate([high, low], axis=1), jnp.concatenate([high, jnp.zeros_like(low)], axis=1)], axis=0
+    )
+    both = jnp.dot(left_parts, stacked, preferred_element_type=F32)
+    count = right.shape[1]
+    return both[:, :count] + both[:, count:]
+
+
+def columns_body(size_z, own_ref, near_ref, far_ref, near_side_ref, far_side_ref, near_rest_ref, far_rest_ref, q_ref, inner_ref, s_ref, keep_ref, give_ref, joined, coupling, diagonal, levels, sums, q_parts, s_parts):
     size_x, rows, width = own_ref.shape
     size_y = rows - 2 * POWERS
     field = width - LANES
@@ -193,29 +204,30 @@
         joined[p, :size_y, own:field] = zero
         joined[p, size_y:] = jnp.zeros((2 * POWERS, width), F32)
     for at in range(POWERS - 1):
-        above, below = sides("gx", near_rest_ref[at], far_rest_ref[at])
-        for p, value in ((size_x + at, above), (size_x + POWERS + 1 + at, below)):
-            for part in range(size_y // SUBLANES):
-                lanes = slice(3 * part * LANES, 3 * (part + 1) * LANES)
-                joined[p, part * SUBLANES : (part + 1) * SUBLANES, own:] = value[:, lanes]
-            joined[p, size_y:] = value[:, 3 * (size_y // SUBLANES) * LANES :]
+        halo = sides("gx", near_rest_ref[at], far_rest_ref[at])
+        side = sides("gx", near_side_ref[at], far_side_ref[at])
+        for up in range(2):
+            p = size_x + at + up * (POWERS + 1)
+            joined[p, :size_y, own:] = side[up]
+            joined[p, size_y:] = halo[up]
 
     weights = joined[:, :, field:].reshape(-1, LANES)
-    source = row_of((LANES, field))
-    position = lane_of((LANES, field)) // BLOCK
+    weights = jnp.concatenate(halves(weights * (1.0 / math.sqrt(DEGREE))), axis=1)
+    source = row_of((2 * LANES, field))
+    position = lane_of((2 * LANES, field)) // BLOCK
     place = jnp.where(
         position < size_z,
         position,
         jnp.where(position < size_z + POWERS, position + 2 * size_z, position + 3 * size_z - 2 * POWERS),
     )
-    unit = 1.0 / math.sqrt(DEGREE)
     for d in range(3):
-        selector = (source == place + d * size_z).astype(F32).astype(BF16)
-        spread = exact_dot(weights, selector) * unit
+        selector = jnp.where(source % LANES == place + d * size_z, 1.0, 0.0).astype(BF16)
+        spread = jnp.dot(weights, selector, preferred_element_type=F32)
         coupling[d] = spread.reshape(planes, rows, field)
     row_last = (row_of((rows, field)) == size_y - 1) & last_on("gy")
     lane_last = (lane_of((rows, field)) // BLOCK == size_z - 1) & last_on("gz")
 
+    distance = lambda p: 0 if p < size_x else min(p - size_x + 1, planes - p)
     near = lambda layers: [p for p in range(planes) if p < size_x + layers or p >= planes - layers]
     for p in near(POWERS - 1):
         x, y, z = (coupling[d, p] for d in range(3))
@@ -239,8 +251,12 @@
             total = total - z * pltpu.roll(value, field - BLOCK, 1) - pltpu.roll(z * value, BLOCK, 1)
             if k > 1:
                 total = total - level(k - 2, p)
-            if k == POWERS:
+            reach = POWERS - k - distance(p)
+            if reach == 0:
                 levels[k - 1, p, :size_y, :own] = total[:size_y, :own]
+            elif reach == 1:
+                levels[k - 1, p, :size_y] = total[:size_y]
+                levels[k - 1, p, size_y:, :own] = total[size_y:, :own]
             else:
                 levels[k - 1, p] = total
 
@@ -252,11 +268,19 @@
             for r in range(4):
                 moved = [pltpu.roll(tiles[m], (32 * (m - r)) % LANES, 1) if m != r else tiles[m] for m in range(POWERS)]
                 at = (i * size_z + 4 * q + r) * size_y
-                s_ref[at : at + size_y] = by_block(block, moved)
-
-    columns = s_ref[...]
-    sums[:BASIS] = contract(q_ref[...], columns)[:BASIS]
-    last = contract(columns[:, WIDE - BLOCK :], columns)
+                row = by_block(block, moved)
+                s_ref[at : at + size_y] = row
+                s_parts[at : at + size_y, :WIDE], s_parts[at : at + size_y, WIDE:] = halves(row)
+                row = jnp.where(lane < BASIS, q_ref[at : at + size_y], row)
+                q_parts[at : at + size_y, :LANES], q_parts[at : at + size_y, LANES:] = halves(row)
+
+    product = lax.dot_general(
+        q_parts[...], s_parts[...], (((0,), (0,)), ((), ())), preferred_element_type=F32
+    )
+    product = product[:LANES] + product[LANES:]
+    product = product[:, :WIDE] + product[:, WIDE:]
+    sums[:BASIS] = product[:BASIS]
+    last = product[BASIS:]
     inner = inner_ref[...]
     block = lane_of((BLOCK, LANES)) // BLOCK
     turned = pltpu.roll(last, 96, 1)
@@ -310,44 +334,50 @@
     return left, right
 
 
-def factor_panel(left, right, column):
-    size, count = left.shape
-    entry = lambda i, j: jnp.broadcast_to(left[i : i + 1, column + j : column + j + 1], (size, count))
-    a = {(i, j): entry(i, j) for i in range(size) for j in range(i, size)}
-    row_a = [jnp.broadcast_to(left[i : i + 1, :], (size, count)) for i in range(size)]
-    row_b = [jnp.broadcast_to(right[i : i + 1, :], (size, count)) for i in range(size)]
-    for k in range(size):
-        inverse = lax.rsqrt(a[k, k])
-        row_a[k] = row_a[k] * inverse
-        row_b[k] = row_b[k] * inverse
-        scaled = {j: a[k, j] * inverse for j in range(k + 1, size)}
-        for i in range(k + 1, size):
-            for j in range(i, size):
-                a[i, j] = a[i, j] - scaled[i] * scaled[j]
-            row_a[i] = row_a[i] - scaled[i] * row_a[k]
-            row_b[i] = row_b[i] - scaled[i] * row_b[k]
-    sub = row_of((size, count))
-    out_a, out_b = row_a[0], row_b[0]
-    for i in range(1, size):
-        out_a, out_b = jnp.where(sub == i, row_a[i], out_a), jnp.where(sub == i, row_b[i], out_b)
-    return out_a, out_b
-
-
 def factor(joined, upper, inverse):
     count = upper.shape[0]
+    shape = (SUBLANES, count)
+    sub, lane = row_of(shape), lane_of(shape)
+    panel = range(SUBLANES)
+    entry = lambda rows, i, j: jnp.broadcast_to(rows[i : i + 1, j : j + 1], shape)
+    spread = lambda rows: [jnp.broadcast_to(rows[i : i + 1], shape) for i in panel]
+
+    def entries(rows, start):
+        return {(i, j): entry(rows[i], 0, start + j) for i in panel for j in panel if j >= i}
+
+    rows_a = spread(joined[:SUBLANES, :count])
+    a = entries(rows_a, 0)
     for start in range(0, count, SUBLANES):
         stop = start + SUBLANES
-        out_a, out_b = factor_panel(joined[start:stop, :count], joined[start:stop, count:], start)
-        shape = (SUBLANES, count)
-        out_a = jnp.where(lane_of(shape) >= row_of(shape) + start, out_a, 0.0)
-        upper[start:stop] = out_a
-        inverse[start:stop] = out_b
-        if stop < count:
-            left, right = split_rows(jnp.concatenate([out_a, out_b], axis=1))
-            update = lax.dot_general(
-                left[:, :count], right, (((0,), (0,)), ((), ())), preferred_element_type=F32
-            )
-            joined[stop:] = joined[stop:] - update[stop:]
+        following = spread(joined[stop : stop + SUBLANES, :count]) if stop < count else None
+        rows_b = spread(joined[start:stop, count:])
+        for k in panel:
+            scale = lax.rsqrt(a[k, k])
+            rows_a[k], rows_b[k] = rows_a[k] * scale, rows_b[k] * scale
+            scaled = {j: a[k, j] * scale for j in panel if j > k}
+            for i in scaled:
+                for j in panel:
+                    if j >= i:
+                        a[i, j] = a[i, j] - scaled[i] * scaled[j]
+                rows_a[i] = rows_a[i] - scaled[i] * rows_a[k]
+                rows_b[i] = rows_b[i] - scaled[i] * rows_b[k]
+        out_a, out_b = rows_a[0], rows_b[0]
+        for i in panel[1:]:
+            out_a, out_b = jnp.where(sub == i, rows_a[i], out_a), jnp.where(sub == i, rows_b[i], out_b)
+        out_a = jnp.where(lane >= sub + start, out_a, 0.0)
+        upper[start:stop], inverse[start:stop] = out_a, out_b
+        if stop == count:
+            break
+        for k in panel:
+            for j in panel:
+                following[j] = following[j] - entry(rows_a[k], 0, stop + j) * rows_a[k]
+        rows_a, a = following, entries(following, stop)
+        left, right = split_rows(jnp.concatenate([out_a, out_b], axis=1))
+        update = lax.dot_general(left[:, :count], right, (((0,), (0,)), ((), ())), preferred_element_type=F32)
+        after = stop + SUBLANES
+        joined[stop:after, count:] = joined[stop:after, count:] - update[stop:after, count:]
+        if after < count:
+            joined[after:] = joined[after:] - update[after:]
 
 
 def basis_change(centre, width):
@@ -425,12 +455,11 @@
     shape = (WIDE, WIDE)
     joined[:, WIDE:] = jnp.where(row_of(shape) == lane_of(shape), 1.0, 0.0)
     padded = jnp.concatenate([moved, jnp.zeros((WIDE - BASIS, WIDE), F32)], axis=0)
-    twice = s_ref[...] - dot(q_ref[...], padded)
+    twice = s_ref[...] - wide_dot(q_ref[...], padded)
+    twice_parts = jnp.concatenate(halves(twice), axis=1)
     factor(joined, upper, inverse)
     triangle_ref[...] = to_powers(upper[...])
-    new_basis = lax.dot_general(
-        twice, inverse[...], (((1,), (1,)), ((), ())), precision=PRECISE, preferred_element_type=F32
-    )
+    new_basis = wide_dot(twice_parts, jnp.transpose(inverse[...]))
     for i in range(size_x):
         for k in range(size_z):
             at = (i * size_z + k) * size_y
@@ -494,17 +523,19 @@
     halos = exchange(faces[0], faces[-1], "gz", "gx") if faces else []
     planes_x = filled(exchange(field, field, "gx", "gz"), field)
     degree_shift = spectral_shift + DEGREE
-    prior_rows, inner = kernel_call(
+    prior_rows, prior_parts, inner = kernel_call(
         prior_body,
-        [(cell_local, LANES), (BASIS, LANES)],
+        [(cell_local, LANES), jax.ShapeDtypeStruct((cell_local, 2 * LANES), BF16), (BASIS, LANES)],
         cost=pl.CostEstimate(flops=6 * 2 * cell_local * LANES * LANES, bytes_accessed=4 * prior_basis.size, transcendentals=0),
     )(prior_basis)
     width = own + 3 * LANES
-    wide, first, second = kernel_call(
-        widen_body, [(size_x, size_y, width)] + [(size_x, POWERS, width)] * 2
+    side = (POWERS - 1, size_y, 3 * LANES)
+    wide, first, second, *side_faces = kernel_call(
+        widen_body, [(size_x, size_y, width)] + [(size_x, POWERS, width)] * 2 + [side] * 2
     )(field, *halos)
     halos = filled(exchange(first, second, "gy", "gx"), first)
-    rest = (POWERS - 1, SUBLANES, 3 * LANES * (size_y // SUBLANES) + width)
+    sides_x = filled(exchange(*side_faces, "gx", "gz"), side_faces[0])
+    rest = (POWERS - 1, 2 * POWERS, width)
     long, first, second = kernel_call(lengthen_body, [(size_x, size_y + 2 * POWERS, width), rest, rest])(wide, *halos)
     rests = filled(exchange(first, second, "gx", "gz"), first)
 
@@ -520,8 +551,10 @@
             pltpu.VMEM((planes, rows, lanes), F32),
             pltpu.VMEM((POWERS, planes, rows, lanes), F32),
             pltpu.VMEM((sum_rows, WIDE), F32),
+            pltpu.VMEM((cell_local, 2 * LANES), BF16),
+            pltpu.VMEM((cell_local, 2 * WIDE), BF16),
         ],
-    )(long, *planes_x, *rests, prior_rows, inner)
+    )(long, *planes_x, *sides_x, *rests, prior_rows, inner)
 
     total = keep + swap(give, "gx", 1)
     for axis in ("gx", "gz", "gy"):
@@ -544,7 +577,7 @@
             pltpu.VMEM((WIDE, WIDE), F32),
         ],
         compiler_params=pltpu.CompilerParams(vmem_limit_bytes=24 * 1024 * 1024),
-    )(degree_shift, prior_rows, columns, total, other)
+    )(degree_shift, prior_parts, columns, total, other)
     return new_basis, projection, triangle
 
 

time: 51.6 us -> 49 us (0.950)
  waiting for transfers between devices: 15.3 us -> 19.5 us
  starting transfers between devices: 19.8 us -> 16.2 us
  Pallas kernels: 15 us -> 11.7 us
    ppermute x7 -> x9, waiting for transfers between devices: 4.79 us -> 7.59 us  [exchange(): lax.ppermute(value, axes, [(place(source), place(target)) for source, tar...]
    pallas_call x1, Pallas kernels: 8.32 us -> 6.25 us  [cycle(): pl.pallas_call(functools.partial(finish_body, 1.0 / cell_count), in_specs...]
    ppermute x6, starting transfers between devices: 10.4 us -> 8.49 us  [swap(): return lax.ppermute(values, axis, [(i, i ^ step) for i in range(count)])]
    ppermute x7 -> x9, starting transfers between devices: 9.33 us -> 7.74 us  [exchange(): lax.ppermute(value, axes, [(place(source), place(target)) for source, tar...]
    ppermute x6, waiting for transfers between devices: 10.5 us -> 11.9 us  [swap(): return lax.ppermute(values, axis, [(i, i ^ step) for i in range(count)])]
    pallas_call x1, Pallas kernels: 4.12 us -> 2.93 us  [cycle(): kernel_call(functools.partial(columns_body, size_z), [(cell_local, WIDE),...]
  transfers between devices with their start and end apart: 13 -> 15, of which waited for: 10 -> 9; matrix products, arithmetic and copies ran while one was open for 0% -> 0% of each run, Pallas kernels for 2% -> 2%
where the time goes in v5:
time: 49 us; the launch traced here: 48.9 us
  waiting for transfers between devices  19.5 us (40%)
  starting transfers between devices  16.2 us (33%)
  Pallas kernels  11.7 us (24%)
  between operations  1.38 us (3%)
    ppermute x6, waiting for transfers between devices, swap(): return lax.ppermute(values, axis, [(i, i ^ step) for i in range(count)])  11.9 us
    ppermute x6, starting transfers between devices, swap(): return lax.ppermute(values, axis, [(i, i ^ step) for i in range(count)])  8.49 us
    ppermute x9, starting transfers between devices, exchange(): lax.ppermute(value, axes, [(place(source), place(target)) for source, tar...  7.74 us
    ppermute x9, waiting for transfers between devices, exchange(): lax.ppermute(value, axes, [(place(source), place(target)) for source, tar...  7.59 us
    pallas_call x1, Pallas kernels, cycle(): pl.pallas_call(functools.partial(finish_body, 1.0 / cell_count), in_specs...  6.25 us
    pallas_call x1, Pallas kernels, cycle(): kernel_call(functools.partial(columns_body, size_z), [(cell_local, WIDE),...  2.93 us
    pallas_call x1, Pallas kernels, cycle(): kernel_call(pack_body, [(size_x, size_y, own + LANES)] + [(size_x, size_y...  1.51 us
  transfers between devices with their start and end apart: 15, of which 9 were waited for; matrix products, arithmetic and copies ran while one was open for 0% of the time, Pallas kernels for 2%

profile of v5, /device:TPU:0, one launch (start us, length us, event | category | flops | bytes accessed | tf_op | source)
XLA Modules:
  0.0 48.9 jit_solution(31232657001484510)
XLA Ops:
  0.6 1.5 %shard_map.59 = (f32[4,16,640]{2,1,0:T(8,128)S(1)}, f32[4,16,256]{2,1,0:T(8,128)S(1)}) custom-call(f32[4,16,1536]{2,1,0:T(8,128)} %prior_hbm.1, f32[3,4,16,16]{3,2,1,0:T(8,128)} %weights_hbm.1), custom_call_target="tpu_custom_call" | custom-call | tf_op jit(solution)/shard_map/pallas_call | solution.py:512
  2.1 0.0 copy-start
  2.2 3.1 %collective-permute-start = (f32[4,16,256]{2,1,0:T(8,128)S(1)}, f32[4,16,256]{2,1,0:T(8,128)S(1)}, u32[]{:S(2)}, u32[]{:S(2)}) collective-permute-start(f32[4,16,256]{2,1,0:T(8,128)S(1)} %get-tuple-element.21), channel_id=1, source_target_pairs={{0,1},{8,9},{16,17},{24,25},{1,0},{9,8},{17,16},{25,24},{2,3},{10,... | collective-permute-start | bytes 196616 | tf_op jit(solution)/shard_map/ppermute | solution.py:488
  5.2 0.0 collective-permute-start.3
  5.2 0.2 collective-permute-start.4
  5.4 2.1 %collective-permute-done.refs_0_ = f32[4,16,256]{2,1,0:T(8,128)S(1)} collective-permute-done((f32[4,16,256]{2,1,0:T(8,128)S(1)}, f32[4,16,256]{2,1,0:T(8,128)S(1)}, u32[]{:S(2)}, u32[]{:S(2)}) %collective-permute-start) | collective-permute-done | bytes 65568 | tf_op jit(solution)/shard_map/ppermute | solution.py:488
  7.5 0.1 shard_map.60
  7.6 0.1 collective-permute-start.5
  7.6 2.1 %collective-permute-start.1 = (f32[4,4,896]{2,1,0:T(4,128)S(1)}, f32[4,4,896]{2,1,0:T(4,128)S(1)}, u32[]{:S(2)}, u32[]{:S(2)}) collective-permute-start(f32[4,4,896]{2,1,0:T(4,128)S(1)} %get-tuple-element.23), channel_id=1, source_target_pairs={{0,2},{8,10},{16,18},{24,26},{2,0},{10,8},{18,16},{26,24},{4,6},{1... | collective-permute-start | bytes 172040 | tf_op jit(solution)/shard_map/ppermute | solution.py:488
  9.8 0.2 collective-permute-start.2
  9.9 2.4 %collective-permute-done.1.first_ref = f32[4,4,896]{2,1,0:T(4,128)S(1)} collective-permute-done((f32[4,4,896]{2,1,0:T(4,128)S(1)}, f32[4,4,896]{2,1,0:T(4,128)S(1)}, u32[]{:S(2)}, u32[]{:S(2)}) %collective-permute-start.1) | collective-permute-done | bytes 57376 | tf_op jit(solution)/shard_map/ppermute | solution.py:488
  12.3 0.0 collective-permute-done.2.second_ref
  12.4 0.1 collective-permute-start.7
  12.4 1.8 %collective-permute-start.8 = (f32[3,8,896]{2,1,0:T(8,128)S(1)}, f32[3,8,896]{2,1,0:T(8,128)S(1)}, u32[]{:S(2)}, u32[]{:S(2)}) collective-permute-start(f32[3,8,896]{2,1,0:T(8,128)S(1)} %get-tuple-element.29), channel_id=1, source_target_pairs={{8,16},{9,17},{16,8},{17,9},{0,1},{1,0},{24,25},{25,24},{10,18},{1... | collective-permute-start | bytes 258056 | tf_op jit(solution)/shard_map/ppermute | solution.py:488
  14.2 0.0 collective-permute-done.5.near_side_ref
  14.2 0.3 collective-permute-start.6
  14.5 0.0 copy-done
  14.5 0.9 %shard_map.58 = (f32[1024,128]{1,0:T(8,128)S(1)}, bf16[1024,256]{1,0:T(8,128)(2,1)S(1)}, f32[96,128]{1,0:T(8,128)S(1)}) custom-call(f32[4,16,1536]{2,1,0:T(8,128)S(1)} %copy-done), custom_call_target="tpu_custom_call" | custom-call | flops 201326592 | bytes 393216 | tf_op jit(solution)/shard_map/pallas_call | solution.py:526
  15.4 3.1 %collective-permute-done.6.far_side_ref = f32[3,16,384]{2,1,0:T(8,128)S(1)} collective-permute-done((f32[3,16,384]{2,1,0:T(8,128)S(1)}, f32[3,16,384]{2,1,0:T(8,128)S(1)}, u32[]{:S(2)}, u32[]{:S(2)}) %collective-permute-start.6) | collective-permute-done | bytes 73760 | tf_op jit(solution)/shard_map/ppermute | solution.py:488
  18.5 0.0 collective-permute-done.3.near_ref
  18.5 0.0 collective-permute-done.4.far_ref
  18.5 0.0 collective-permute-done.7.near_rest_ref
  18.6 0.0 collective-permute-done.8.far_rest_ref
  18.6 2.9 %shard_map.62 = (f32[1024,128]{1,0:T(8,128)S(1)}, f32[88,128]{1,0:T(8,128)S(1)}, f32[88,128]{1,0:T(8,128)S(1)}) custom-call(f32[4,24,896]{2,1,0:T(8,128)S(1)} %get-tuple-element.25.own_ref, f32[4,16,640]{2,1,0:T(8,128)S(1)} %collective-permute-done.3.near_ref, f32[4,16,640]{2,1,0:T(8,128)S(1)} %collective-permute-done.4.far_ref, ...), custom_call_target="tpu_custom_call" | custom-call | tf_op jit(solution)/shard_map/pallas_call | solution.py:545
  21.5 0.1 collective-permute-start.9
  21.6 1.2 %collective-permute-done.9 = f32[88,128]{1,0:T(8,128)S(1)} collective-permute-done((f32[88,128]{1,0:T(8,128)S(1)}, f32[88,128]{1,0:T(8,128)S(1)}, u32[]{:S(2)}, u32[]{:S(2)}) %collective-permute-start.9) | collective-permute-done | bytes 45088 | tf_op jit(solution)/shard_map/ppermute | solution.py:471
  22.8 0.8 %collective-permute-start.10 = (f32[88,128]{1,0:T(8,128)S(1)}, f32[88,128]{1,0:T(8,128)S(1)}, u32[]{:S(2)}, u32[]{:S(2)}) collective-permute-start(f32[88,128]{1,0:T(8,128)S(1)} %add.19), channel_id=1, source_target_pairs={{0,16},{8,24},{16,0},{24,8},{1,17},{9,25},{17,1},{25,9},{2,18},{10... | collective-permute-start | bytes 135176 | tf_op jit(solution)/shard_map/ppermute | solution.py:471
  23.6 3.3 %collective-permute-done.10 = f32[88,128]{1,0:T(8,128)S(1)} collective-permute-done((f32[88,128]{1,0:T(8,128)S(1)}, f32[88,128]{1,0:T(8,128)S(1)}, u32[]{:S(2)}, u32[]{:S(2)}) %collective-permute-start.10) | collective-permute-done | bytes 45088 | tf_op jit(solution)/shard_map/ppermute | solution.py:471
  26.9 1.3 %collective-permute-start.11 = (f32[88,128]{1,0:T(8,128)S(1)}, f32[88,128]{1,0:T(8,128)S(1)}, u32[]{:S(2)}, u32[]{:S(2)}) collective-permute-start(f32[88,128]{1,0:T(8,128)S(1)} %add.20), channel_id=1, source_target_pairs={{0,1},{1,0},{2,3},{3,2},{4,5},{5,4},{6,7},{7,6},{8,9},{9,8},{10,11... | collective-permute-start | bytes 135176 | tf_op jit(solution)/shard_map/ppermute | solution.py:471
  28.3 2.8 %collective-permute-done.11 = f32[88,128]{1,0:T(8,128)S(1)} collective-permute-done((f32[88,128]{1,0:T(8,128)S(1)}, f32[88,128]{1,0:T(8,128)S(1)}, u32[]{:S(2)}, u32[]{:S(2)}) %collective-permute-start.11) | collective-permute-done | bytes 45088 | tf_op jit(solution)/shard_map/ppermute | solution.py:471
  31.0 2.8 %collective-permute-start.12 = (f32[88,128]{1,0:T(8,128)S(1)}, f32[88,128]{1,0:T(8,128)S(1)}, u32[]{:S(2)}, u32[]{:S(2)}) collective-permute-start(f32[88,128]{1,0:T(8,128)S(1)} %add.21), channel_id=1, source_target_pairs={{0,2},{2,0},{4,6},{6,4},{1,3},{3,1},{5,7},{7,5},{8,10},{10,8},{12,... | collective-permute-start | bytes 135176 | tf_op jit(solution)/shard_map/ppermute | solution.py:471
  33.8 2.0 %collective-permute-done.12 = f32[88,128]{1,0:T(8,128)S(1)} collective-permute-done((f32[88,128]{1,0:T(8,128)S(1)}, f32[88,128]{1,0:T(8,128)S(1)}, u32[]{:S(2)}, u32[]{:S(2)}) %collective-permute-start.12) | collective-permute-done | bytes 45088 | tf_op jit(solution)/shard_map/ppermute | solution.py:471
  35.8 3.5 %collective-permute-start.13 = (f32[88,128]{1,0:T(8,128)S(1)}, f32[88,128]{1,0:T(8,128)S(1)}, u32[]{:S(2)}, u32[]{:S(2)}) collective-permute-start(f32[88,128]{1,0:T(8,128)S(1)} %add.22), channel_id=1, source_target_pairs={{0,4},{2,6},{4,0},{6,2},{1,5},{3,7},{5,1},{7,3},{8,12},{10,14},{12... | collective-permute-start | bytes 135176 | tf_op jit(solution)/shard_map/ppermute | solution.py:471
  39.3 2.0 %collective-permute-done.13 = f32[88,128]{1,0:T(8,128)S(1)} collective-permute-done((f32[88,128]{1,0:T(8,128)S(1)}, f32[88,128]{1,0:T(8,128)S(1)}, u32[]{:S(2)}, u32[]{:S(2)}) %collective-permute-start.13) | collective-permute-done | bytes 45088 | tf_op jit(solution)/shard_map/ppermute | solution.py:471
  41.3 0.1 collective-permute-start.14
  42.0 0.6 %collective-permute-done.14.other_ref = f32[88,128]{1,0:T(8,128)S(1)} collective-permute-done((f32[88,128]{1,0:T(8,128)S(1)}, f32[88,128]{1,0:T(8,128)S(1)}, u32[]{:S(2)}, u32[]{:S(2)}) %collective-permute-start.14) | collective-permute-done | bytes 45088 | tf_op jit(solution)/shard_map/ppermute | solution.py:471
  42.6 6.2 %shard_map.63 = (f32[4,16,2048]{2,1,0:T(8,128)}, f32[96,128]{1,0:T(8,128)}, f32[128,128]{1,0:T(8,128)}) custom-call(f32[1]{0:T(128)S(6)} %add.18.shift_ref, bf16[1024,256]{1,0:T(8,128)(2,1)S(1)} %get-tuple-element.19.q_ref, f32[1024,128]{1,0:T(8,128)S(1)} %get-tuple-element.32.s_ref, f32[88,128]{1,0:T(8,128)S(1)} %add.23.mine_ref, ...), custom_call_target="tpu_custom_call" | custom-call | tf_op jit(solution)/shard_map/pallas_call | solution.py:566
  (6 shorter events, 0.1 us)
Async XLA Ops:
  2.1 12.4 %copy-start = (f32[4,16,1536]{2,1,0:T(8,128)S(1)}, f32[4,16,1536]{2,1,0:T(8,128)}, u32[]{:S(2)}) copy-start(f32[4,16,1536]{2,1,0:T(8,128)} %prior_hbm.1) | copy-start | bytes 1179652
  2.2 5.3 %collective-permute-start = (f32[4,16,256]{2,1,0:T(8,128)S(1)}, f32[4,16,256]{2,1,0:T(8,128)S(1)}, u32[]{:S(2)}, u32[]{:S(2)}) collective-permute-start(f32[4,16,256]{2,1,0:T(8,128)S(1)} %get-tuple-element.21), channel_id=1, source_target_pairs={{0,1},{8,9},{16,17},{24,25},{1,0},{9,8},{17,16},{25,24},{2,3},{10,... | collective-permute-start | bytes 196616 | tf_op jit(solution)/shard_map/ppermute | solution.py:488
  5.2 13.3 %collective-permute-start.3 = (f32[4,16,640]{2,1,0:T(8,128)S(1)}, f32[4,16,640]{2,1,0:T(8,128)S(1)}, u32[]{:S(2)}, u32[]{:S(2)}) collective-permute-start(f32[4,16,640]{2,1,0:T(8,128)S(1)} %get-tuple-element.20.field_ref), channel_id=1, source_target_pairs={{0,8},{1,9},{8,0},{9,1},{16,24},{17,25},{24,16},{25,17},{2,10},{3,... | collective-permute-start | bytes 491528 | tf_op jit(solution)/shard_map/ppermute | solution.py:488
  5.2 13.3 %collective-permute-start.4 = (f32[4,16,640]{2,1,0:T(8,128)S(1)}, f32[4,16,640]{2,1,0:T(8,128)S(1)}, u32[]{:S(2)}, u32[]{:S(2)}) collective-permute-start(f32[4,16,640]{2,1,0:T(8,128)S(1)} %get-tuple-element.20.field_ref), channel_id=1, source_target_pairs={{8,16},{9,17},{16,8},{17,9},{0,1},{1,0},{24,25},{25,24},{10,18},{1... | collective-permute-start | bytes 491528 | tf_op jit(solution)/shard_map/ppermute | solution.py:488
  7.6 6.6 %collective-permute-start.5 = (f32[3,16,384]{2,1,0:T(8,128)S(1)}, f32[3,16,384]{2,1,0:T(8,128)S(1)}, u32[]{:S(2)}, u32[]{:S(2)}) collective-permute-start(f32[3,16,384]{2,1,0:T(8,128)S(1)} %get-tuple-element.26), channel_id=1, source_target_pairs={{0,8},{1,9},{8,0},{9,1},{16,24},{17,25},{24,16},{25,17},{2,10},{3,... | collective-permute-start | bytes 221192 | tf_op jit(solution)/shard_map/ppermute | solution.py:488
  7.6 4.7 %collective-permute-start.1 = (f32[4,4,896]{2,1,0:T(4,128)S(1)}, f32[4,4,896]{2,1,0:T(4,128)S(1)}, u32[]{:S(2)}, u32[]{:S(2)}) collective-permute-start(f32[4,4,896]{2,1,0:T(4,128)S(1)} %get-tuple-element.23), channel_id=1, source_target_pairs={{0,2},{8,10},{16,18},{24,26},{2,0},{10,8},{18,16},{26,24},{4,6},{1... | collective-permute-start | bytes 172040 | tf_op jit(solution)/shard_map/ppermute | solution.py:488
  9.8 2.5 %collective-permute-start.2 = (f32[4,4,896]{2,1,0:T(4,128)S(1)}, f32[4,4,896]{2,1,0:T(4,128)S(1)}, u32[]{:S(2)}, u32[]{:S(2)}) collective-permute-start(f32[4,4,896]{2,1,0:T(4,128)S(1)} %get-tuple-element.24), channel_id=1, source_target_pairs={{2,4},{10,12},{18,20},{26,28},{4,2},{12,10},{20,18},{28,26},{0,8},... | collective-permute-start | bytes 172040 | tf_op jit(solution)/shard_map/ppermute | solution.py:488
  12.4 6.2 %collective-permute-start.7 = (f32[3,8,896]{2,1,0:T(8,128)S(1)}, f32[3,8,896]{2,1,0:T(8,128)S(1)}, u32[]{:S(2)}, u32[]{:S(2)}) collective-permute-start(f32[3,8,896]{2,1,0:T(8,128)S(1)} %get-tuple-element.28), channel_id=1, source_target_pairs={{0,8},{1,9},{8,0},{9,1},{16,24},{17,25},{24,16},{25,17},{2,10},{3,... | collective-permute-start | bytes 258056 | tf_op jit(solution)/shard_map/ppermute | solution.py:488
  12.4 6.1 %collective-permute-start.8 = (f32[3,8,896]{2,1,0:T(8,128)S(1)}, f32[3,8,896]{2,1,0:T(8,128)S(1)}, u32[]{:S(2)}, u32[]{:S(2)}) collective-permute-start(f32[3,8,896]{2,1,0:T(8,128)S(1)} %get-tuple-element.29), channel_id=1, source_target_pairs={{8,16},{9,17},{16,8},{17,9},{0,1},{1,0},{24,25},{25,24},{10,18},{1... | collective-permute-start | bytes 258056 | tf_op jit(solution)/shard_map/ppermute | solution.py:488
  14.2 4.4 %collective-permute-start.6 = (f32[3,16,384]{2,1,0:T(8,128)S(1)}, f32[3,16,384]{2,1,0:T(8,128)S(1)}, u32[]{:S(2)}, u32[]{:S(2)}) collective-permute-start(f32[3,16,384]{2,1,0:T(8,128)S(1)} %get-tuple-element.27), channel_id=1, source_target_pairs={{8,16},{9,17},{16,8},{17,9},{0,1},{1,0},{24,25},{25,24},{10,18},{1... | collective-permute-start | bytes 221192 | tf_op jit(solution)/shard_map/ppermute | solution.py:488
  21.5 1.3 %collective-permute-start.9 = (f32[88,128]{1,0:T(8,128)S(1)}, f32[88,128]{1,0:T(8,128)S(1)}, u32[]{:S(2)}, u32[]{:S(2)}) collective-permute-start(f32[88,128]{1,0:T(8,128)S(1)} %get-tuple-element.34), channel_id=1, source_target_pairs={{0,8},{8,0},{16,24},{24,16},{1,9},{9,1},{17,25},{25,17},{2,10},{10... | collective-permute-start | bytes 135176 | tf_op jit(solution)/shard_map/ppermute | solution.py:471
  22.8 4.1 %collective-permute-start.10 = (f32[88,128]{1,0:T(8,128)S(1)}, f32[88,128]{1,0:T(8,128)S(1)}, u32[]{:S(2)}, u32[]{:S(2)}) collective-permute-start(f32[88,128]{1,0:T(8,128)S(1)} %add.19), channel_id=1, source_target_pairs={{0,16},{8,24},{16,0},{24,8},{1,17},{9,25},{17,1},{25,9},{2,18},{10... | collective-permute-start | bytes 135176 | tf_op jit(solution)/shard_map/ppermute | solution.py:471
  26.9 4.1 %collective-permute-start.11 = (f32[88,128]{1,0:T(8,128)S(1)}, f32[88,128]{1,0:T(8,128)S(1)}, u32[]{:S(2)}, u32[]{:S(2)}) collective-permute-start(f32[88,128]{1,0:T(8,128)S(1)} %add.20), channel_id=1, source_target_pairs={{0,1},{1,0},{2,3},{3,2},{4,5},{5,4},{6,7},{7,6},{8,9},{9,8},{10,11... | collective-permute-start | bytes 135176 | tf_op jit(solution)/shard_map/ppermute | solution.py:471
  31.0 4.8 %collective-permute-start.12 = (f32[88,128]{1,0:T(8,128)S(1)}, f32[88,128]{1,0:T(8,128)S(1)}, u32[]{:S(2)}, u32[]{:S(2)}) collective-permute-start(f32[88,128]{1,0:T(8,128)S(1)} %add.21), channel_id=1, source_target_pairs={{0,2},{2,0},{4,6},{6,4},{1,3},{3,1},{5,7},{7,5},{8,10},{10,8},{12,... | collective-permute-start | bytes 135176 | tf_op jit(solution)/shard_map/ppermute | solution.py:471
  35.8 5.5 %collective-permute-start.13 = (f32[88,128]{1,0:T(8,128)S(1)}, f32[88,128]{1,0:T(8,128)S(1)}, u32[]{:S(2)}, u32[]{:S(2)}) collective-permute-start(f32[88,128]{1,0:T(8,128)S(1)} %add.22), channel_id=1, source_target_pairs={{0,4},{2,6},{4,0},{6,2},{1,5},{3,7},{5,1},{7,3},{8,12},{10,14},{12... | collective-permute-start | bytes 135176 | tf_op jit(solution)/shard_map/ppermute | solution.py:471
  41.3 1.3 %collective-permute-start.14 = (f32[88,128]{1,0:T(8,128)S(1)}, f32[88,128]{1,0:T(8,128)S(1)}, u32[]{:S(2)}, u32[]{:S(2)}) collective-permute-start(f32[88,128]{1,0:T(8,128)S(1)} %add.23.mine_ref), channel_id=1, source_target_pairs={{0,8},{8,0},{16,24},{24,16},{1,9},{9,1},{17,25},{25,17},{2,10},{10... | collective-permute-start | bytes 135176 | tf_op jit(solution)/shard_map/ppermute | solution.py:471

commit v6 on v5

--- a/solution.py
+++ b/solution.py
@@ -57,6 +57,15 @@
     above = jnp.where(last_on(axis), 0.0, jnp.where(even, first, second))
     below = jnp.where(lax.axis_index(axis) == 0, 0.0, jnp.where(even, second, first))
     return above, below
+
+
+def bits(axis):
+    return range((lax.axis_size(axis) - 1).bit_length())
+
+
+def owns_first_half():
+    ones = sum((lax.axis_index(axis) >> k) & 1 for axis in AXES for k in bits(axis))
+    return ones % 2 == 0
 
 
 def pick(even, first, second):
@@ -175,14 +184,24 @@
     return high, (values - high.astype(F32)).astype(BF16)
 
 
+def stacked(right):
+    high, low = halves(right)
+    return jnp.concatenate(
+        [jnp.concatenate([high, low], axis=1), jnp.concatenate([high, jnp.zeros_like(low)], axis=1)], axis=0
+    )
+
+
 def wide_dot(left_parts, right):
-    high, low = halves(right)
-    stacked = jnp.concatenate(
-        [jnp.concatenate([high, low], axis=1), jnp.concatenate([high, jnp.zeros_like(low)], axis=1)], axis=0
-    )
-    both = jnp.dot(left_parts, stacked, preferred_element_type=F32)
-    count = right.shape[1]
+    both = jnp.dot(left_parts, right, preferred_element_type=F32)
+    count = right.shape[1] // 2
     return both[:, :count] + both[:, count:]
+
+
+def contract_parts(left, right):
+    product = lax.dot_general(left, right, (((0,), (0,)), ((), ())), preferred_element_type=F32)
+    rows, columns = left.shape[1] // 2, right.shape[1] // 2
+    product = product[:rows] + product[rows:]
+    return product[:, :columns] + product[:, columns:]
 
 
 def columns_body(size_z, own_ref, near_ref, far_ref, near_side_ref, far_side_ref, near_rest_ref, far_rest_ref, q_ref, inner_ref, s_ref, keep_ref, give_ref, joined, coupling, diagonal, levels, sums, q_parts, s_parts):
@@ -274,11 +293,7 @@
                 row = jnp.where(lane < BASIS, q_ref[at : at + size_y], row)
                 q_parts[at : at + size_y, :LANES], q_parts[at : at + size_y, LANES:] = halves(row)
 
-    product = lax.dot_general(
-        q_parts[...], s_parts[...], (((0,), (0,)), ((), ())), preferred_element_type=F32
-    )
-    product = product[:LANES] + product[LANES:]
-    product = product[:, :WIDE] + product[:, WIDE:]
+    product = contract_parts(q_parts[...], s_parts[...])
     sums[:BASIS] = product[:BASIS]
     last = product[BASIS:]
     inner = inner_ref[...]
@@ -292,7 +307,7 @@
         [pltpu.roll(inner[64:80], 64, 1), pltpu.roll(inner[80:96], 96, 1), pltpu.roll(last[:16], 96, 1), last[16:]],
     )
     half = sums.shape[0] // 2
-    even = even_on("gx")
+    even = owns_first_half()
     keep_ref[...] = pick(even, sums[:half], sums[half:])
     give_ref[...] = pick(even, sums[half:], sums[:half])
 
@@ -417,10 +432,9 @@
 def finish_body(scale, shift_ref, q_ref, s_ref, mine_ref, other_ref, basis_ref, projection_ref, triangle_ref, joined, upper, inverse):
     size_x, size_y, width = basis_ref.shape
     size_z = width // WIDE
-    even = even_on("gx")
+    even = owns_first_half()
     mine, other = mine_ref[...] * scale, other_ref[...] * scale
     sums = jnp.concatenate([pick(even, mine, other), pick(even, other, mine)], axis=0)
-    dot = functools.partial(jnp.dot, precision=PRECISE, preferred_element_type=F32)
 
     centre, spread = shift_ref[0] * (1.0 / OPERATOR_SCALE) - 1.0, math.sqrt(DEGREE) / OPERATOR_SCALE
     t, s = basis_change(centre, spread)
@@ -444,31 +458,57 @@
     first = (BASIS - BLOCK) // BLOCK
     copies = [pltpu.roll(defect, ((k - first) * BLOCK) % WIDE, 1) if k != first else defect for k in range(POWERS)]
     start = jnp.where(block < 2, jnp.where(block < 1, copies[0], copies[1]), jnp.where(block < 3, copies[2], copies[3]))
-    start_defect = dot(defect[:, :BASIS], start)
-    both = cross + dot(defect[:, :BASIS], cross)
-    moved = both - start_defect * removed
+    parts = jnp.concatenate(halves(defect), axis=1)
+    pad = lambda values: jnp.concatenate([values, jnp.zeros((LANES - BASIS, WIDE), F32)], axis=0)
+    by_defect = lambda values: wide_dot(parts, stacked(pad(values)))
+    start_removed = start * removed
+    change = by_defect(cross - start_removed)
+    moved = cross + change
+    left = by_defect(start_removed + change)
+    product = contract_parts(
+        jnp.concatenate(halves(jnp.concatenate([cross, moved], axis=0)), axis=1),
+        jnp.concatenate(halves(jnp.concatenate([moved, left], axis=0)), axis=1),
+    )
     start_unit = jnp.where(row - (BASIS - BLOCK) == lane - block * BLOCK, 1.0, 0.0)
-    projection_ref[...] = to_powers(both) + (start_unit - start_defect) * constant
-    left = cross - dot(inner[:, :BASIS], moved)
-    product = contract(jnp.concatenate([cross, moved], axis=0), jnp.concatenate([moved, left], axis=0))
+    both = cross + by_defect(cross)
+    projection_ref[...] = to_powers(both) + (start_unit - by_defect(start)) * constant
     joined[:, :WIDE] = square - product
     shape = (WIDE, WIDE)
     joined[:, WIDE:] = jnp.where(row_of(shape) == lane_of(shape), 1.0, 0.0)
-    padded = jnp.concatenate([moved, jnp.zeros((WIDE - BASIS, WIDE), F32)], axis=0)
-    twice = s_ref[...] - wide_dot(q_ref[...], padded)
+    twice = s_ref[...] - wide_dot(q_ref[...], stacked(pad(moved)))
     twice_parts = jnp.concatenate(halves(twice), axis=1)
     factor(joined, upper, inverse)
     triangle_ref[...] = to_powers(upper[...])
-    new_basis = wide_dot(twice_parts, jnp.transpose(inverse[...]))
+    solve = stacked(jnp.transpose(inverse[...]))
+    new_basis = wide_dot(twice_parts, solve)
     for i in range(size_x):
         for k in range(size_z):
             at = (i * size_z + k) * size_y
             basis_ref[i, :, k * WIDE : (k + 1) * WIDE] = new_basis[at : at + size_y]
 
 
-def swap(values, axis, step):
-    count = lax.axis_size(axis)
-    return lax.ppermute(values, axis, [(i, i ^ step) for i in range(count)])
+def reduced(keep, give):
+    sizes = [lax.axis_size(axis) for axis in AXES]
+    if sizes[0] < 2 or any(size & (size - 1) for size in sizes):
+        even = owns_first_half()
+        whole = jnp.concatenate([pick(even, keep, give), pick(even, give, keep)], axis=0)
+        first, second = jnp.split(lax.psum(whole, AXES), 2)
+        return pick(even, first, second), pick(even, second, first)
+    place = lambda at: (at[0] * sizes[1] + at[1]) * sizes[2] + at[2]
+    devices = [(i, j, k) for i in range(sizes[0]) for j in range(sizes[1]) for k in range(sizes[2])]
+
+    def swap(values, flips):
+        links = [(place(at), place([a ^ b for a, b in zip(at, flips)])) for at in devices]
+        return lax.ppermute(values, AXES, links)
+
+    total = keep + swap(give, (1, 0, 0))
+    for axis in ("gx", "gz", "gy"):
+        for k in bits(axis):
+            if (axis, k) != ("gx", 0):
+                flips = [(1 << k) * (name == axis) for name in AXES]
+                flips[0] ^= 1
+                total = total + swap(total, flips)
+    return total, swap(total, (1, 0, 0))
 
 
 def exchange(first, second, axis, helper):
@@ -491,11 +531,6 @@
 
 def filled(halos, like):
     return halos + [jnp.zeros_like(like)] * (2 - len(halos))
-
-
-def doublings(axis):
-    count = lax.axis_size(axis)
-    return [1 << k for k in range(count.bit_length() - 1)]
 
 
 def cycle(prior_basis, edge_weights, spectral_shift):
@@ -556,12 +591,7 @@
         ],
     )(long, *planes_x, *sides_x, *rests, prior_rows, inner)
 
-    total = keep + swap(give, "gx", 1)
-    for axis in ("gx", "gz", "gy"):
-        for step in doublings(axis):
-            if (axis, step) != ("gx", 1):
-                total = total + swap(total, axis, step)
-    other = swap(total, "gx", 1)
+    total, other = reduced(keep, give)
 
     new_basis, projection, triangle = pl.pallas_call(
         functools.partial(finish_body, 1.0 / cell_count),

time: 49 us -> 47.1 us (0.961)
  waiting for transfers between devices: 19.5 us -> 18 us
    ppermute x6, waiting for transfers between devices: 11.9 us -> 10.4 us  [swap(): return lax.ppermute(values, AXES, links)]
where the time goes in v6:
time: 47.1 us; the launch traced here: 46.9 us
  waiting for transfers between devices  18 us (38%)
  starting transfers between devices  16.1 us (34%)
  Pallas kernels  11.4 us (24%)
  between operations  1.37 us (3%)
    ppermute x6, waiting for transfers between devices, swap(): return lax.ppermute(values, AXES, links)  10.4 us
    ppermute x6, starting transfers between devices, swap(): return lax.ppermute(values, AXES, links)  8.32 us
    ppermute x9, starting transfers between devices, exchange(): lax.ppermute(value, axes, [(place(source), place(target)) for source, tar...  7.74 us
    ppermute x9, waiting for transfers between devices, exchange(): lax.ppermute(value, axes, [(place(source), place(target)) for source, tar...  7.59 us
    pallas_call x1, Pallas kernels, cycle(): pl.pallas_call(functools.partial(finish_body, 1.0 / cell_count), in_specs...  5.98 us
    pallas_call x1, Pallas kernels, cycle(): kernel_call(functools.partial(columns_body, size_z), [(cell_local, WIDE),...  2.94 us
    pallas_call x1, Pallas kernels, cycle(): kernel_call(pack_body, [(size_x, size_y, own + LANES)] + [(size_x, size_y...  1.51 us
  transfers between devices with their start and end apart: 15, of which 9 were waited for; matrix products, arithmetic and copies ran while one was open for 0% of the time, Pallas kernels for 2%

profile of v6, /device:TPU:0, one launch (start us, length us, event | category | flops | bytes accessed | tf_op | source)
XLA Modules:
  0.0 46.9 jit_solution(17307103459105400266)
XLA Ops:
  0.6 1.5 %shard_map.59 = (f32[4,16,640]{2,1,0:T(8,128)S(1)}, f32[4,16,256]{2,1,0:T(8,128)S(1)}) custom-call(f32[4,16,1536]{2,1,0:T(8,128)} %prior_hbm.1, f32[3,4,16,16]{3,2,1,0:T(8,128)} %weights_hbm.1), custom_call_target="tpu_custom_call" | custom-call | tf_op jit(solution)/shard_map/pallas_call | solution.py:547
  2.1 0.0 copy-start
  2.2 3.1 %collective-permute-start = (f32[4,16,256]{2,1,0:T(8,128)S(1)}, f32[4,16,256]{2,1,0:T(8,128)S(1)}, u32[]{:S(2)}, u32[]{:S(2)}) collective-permute-start(f32[4,16,256]{2,1,0:T(8,128)S(1)} %get-tuple-element.21), channel_id=1, source_target_pairs={{0,1},{8,9},{16,17},{24,25},{1,0},{9,8},{17,16},{25,24},{2,3},{10,... | collective-permute-start | bytes 196616 | tf_op jit(solution)/shard_map/ppermute | solution.py:528
  5.2 0.0 collective-permute-start.3
  5.2 0.2 collective-permute-start.4
  5.4 2.1 %collective-permute-done.refs_0_ = f32[4,16,256]{2,1,0:T(8,128)S(1)} collective-permute-done((f32[4,16,256]{2,1,0:T(8,128)S(1)}, f32[4,16,256]{2,1,0:T(8,128)S(1)}, u32[]{:S(2)}, u32[]{:S(2)}) %collective-permute-start) | collective-permute-done | bytes 65568 | tf_op jit(solution)/shard_map/ppermute | solution.py:528
  7.5 0.1 shard_map.60
  7.6 0.1 collective-permute-start.5
  7.6 2.1 %collective-permute-start.1 = (f32[4,4,896]{2,1,0:T(4,128)S(1)}, f32[4,4,896]{2,1,0:T(4,128)S(1)}, u32[]{:S(2)}, u32[]{:S(2)}) collective-permute-start(f32[4,4,896]{2,1,0:T(4,128)S(1)} %get-tuple-element.23), channel_id=1, source_target_pairs={{0,2},{8,10},{16,18},{24,26},{2,0},{10,8},{18,16},{26,24},{4,6},{1... | collective-permute-start | bytes 172040 | tf_op jit(solution)/shard_map/ppermute | solution.py:528
  9.8 0.2 collective-permute-start.2
  9.9 2.4 %collective-permute-done.1.first_ref = f32[4,4,896]{2,1,0:T(4,128)S(1)} collective-permute-done((f32[4,4,896]{2,1,0:T(4,128)S(1)}, f32[4,4,896]{2,1,0:T(4,128)S(1)}, u32[]{:S(2)}, u32[]{:S(2)}) %collective-permute-start.1) | collective-permute-done | bytes 57376 | tf_op jit(solution)/shard_map/ppermute | solution.py:528
  12.3 0.0 collective-permute-done.2.second_ref
  12.4 0.1 collective-permute-start.7
  12.4 1.8 %collective-permute-start.8 = (f32[3,8,896]{2,1,0:T(8,128)S(1)}, f32[3,8,896]{2,1,0:T(8,128)S(1)}, u32[]{:S(2)}, u32[]{:S(2)}) collective-permute-start(f32[3,8,896]{2,1,0:T(8,128)S(1)} %get-tuple-element.29), channel_id=1, source_target_pairs={{8,16},{9,17},{16,8},{17,9},{0,1},{1,0},{24,25},{25,24},{10,18},{1... | collective-permute-start | bytes 258056 | tf_op jit(solution)/shard_map/ppermute | solution.py:528
  14.2 0.0 collective-permute-done.5.near_side_ref
  14.2 0.3 collective-permute-start.6
  14.5 0.0 copy-done
  14.5 0.9 %shard_map.58 = (f32[1024,128]{1,0:T(8,128)S(1)}, bf16[1024,256]{1,0:T(8,128)(2,1)S(1)}, f32[96,128]{1,0:T(8,128)S(1)}) custom-call(f32[4,16,1536]{2,1,0:T(8,128)S(1)} %copy-done), custom_call_target="tpu_custom_call" | custom-call | flops 201326592 | bytes 393216 | tf_op jit(solution)/shard_map/pallas_call | solution.py:561
  15.4 3.1 %collective-permute-done.6.far_side_ref = f32[3,16,384]{2,1,0:T(8,128)S(1)} collective-permute-done((f32[3,16,384]{2,1,0:T(8,128)S(1)}, f32[3,16,384]{2,1,0:T(8,128)S(1)}, u32[]{:S(2)}, u32[]{:S(2)}) %collective-permute-start.6) | collective-permute-done | bytes 73760 | tf_op jit(solution)/shard_map/ppermute | solution.py:528
  18.5 0.0 collective-permute-done.3.near_ref
  18.5 0.0 collective-permute-done.4.far_ref
  18.5 0.0 collective-permute-done.7.near_rest_ref
  18.6 0.0 collective-permute-done.8.far_rest_ref
  18.6 2.9 %shard_map.62 = (f32[1024,128]{1,0:T(8,128)S(1)}, f32[88,128]{1,0:T(8,128)S(1)}, f32[88,128]{1,0:T(8,128)S(1)}) custom-call(f32[4,24,896]{2,1,0:T(8,128)S(1)} %get-tuple-element.25.own_ref, f32[4,16,640]{2,1,0:T(8,128)S(1)} %collective-permute-done.3.near_ref, f32[4,16,640]{2,1,0:T(8,128)S(1)} %collective-permute-done.4.far_ref, ...), custom_call_target="tpu_custom_call" | custom-call | tf_op jit(solution)/shard_map/pallas_call | solution.py:580
  21.5 0.1 collective-permute-start.9
  21.6 1.2 %collective-permute-done.9 = f32[88,128]{1,0:T(8,128)S(1)} collective-permute-done((f32[88,128]{1,0:T(8,128)S(1)}, f32[88,128]{1,0:T(8,128)S(1)}, u32[]{:S(2)}, u32[]{:S(2)}) %collective-permute-start.9) | collective-permute-done | bytes 45088 | tf_op jit(solution)/shard_map/ppermute | solution.py:502
  22.8 0.8 %collective-permute-start.10 = (f32[88,128]{1,0:T(8,128)S(1)}, f32[88,128]{1,0:T(8,128)S(1)}, u32[]{:S(2)}, u32[]{:S(2)}) collective-permute-start(f32[88,128]{1,0:T(8,128)S(1)} %add.19), channel_id=1, source_target_pairs={{0,24},{1,25},{2,26},{3,27},{4,28},{5,29},{6,30},{7,31},{8,16},{9,... | collective-permute-start | bytes 135176 | tf_op jit(solution)/shard_map/ppermute | solution.py:502
  23.6 2.9 %collective-permute-done.10 = f32[88,128]{1,0:T(8,128)S(1)} collective-permute-done((f32[88,128]{1,0:T(8,128)S(1)}, f32[88,128]{1,0:T(8,128)S(1)}, u32[]{:S(2)}, u32[]{:S(2)}) %collective-permute-start.10) | collective-permute-done | bytes 45088 | tf_op jit(solution)/shard_map/ppermute | solution.py:502
  26.5 1.2 %collective-permute-start.11 = (f32[88,128]{1,0:T(8,128)S(1)}, f32[88,128]{1,0:T(8,128)S(1)}, u32[]{:S(2)}, u32[]{:S(2)}) collective-permute-start(f32[88,128]{1,0:T(8,128)S(1)} %add.20), channel_id=1, source_target_pairs={{0,9},{1,8},{2,11},{3,10},{4,13},{5,12},{6,15},{7,14},{8,1},{9,0},... | collective-permute-start | bytes 135176 | tf_op jit(solution)/shard_map/ppermute | solution.py:502
  27.7 2.6 %collective-permute-done.11 = f32[88,128]{1,0:T(8,128)S(1)} collective-permute-done((f32[88,128]{1,0:T(8,128)S(1)}, f32[88,128]{1,0:T(8,128)S(1)}, u32[]{:S(2)}, u32[]{:S(2)}) %collective-permute-start.11) | collective-permute-done | bytes 45088 | tf_op jit(solution)/shard_map/ppermute | solution.py:502
  30.3 2.5 %collective-permute-start.12 = (f32[88,128]{1,0:T(8,128)S(1)}, f32[88,128]{1,0:T(8,128)S(1)}, u32[]{:S(2)}, u32[]{:S(2)}) collective-permute-start(f32[88,128]{1,0:T(8,128)S(1)} %add.21), channel_id=1, source_target_pairs={{0,10},{1,11},{2,8},{3,9},{4,14},{5,15},{6,12},{7,13},{8,2},{9,3},... | collective-permute-start | bytes 135176 | tf_op jit(solution)/shard_map/ppermute | solution.py:502
  32.8 1.8 %collective-permute-done.12 = f32[88,128]{1,0:T(8,128)S(1)} collective-permute-done((f32[88,128]{1,0:T(8,128)S(1)}, f32[88,128]{1,0:T(8,128)S(1)}, u32[]{:S(2)}, u32[]{:S(2)}) %collective-permute-start.12) | collective-permute-done | bytes 45088 | tf_op jit(solution)/shard_map/ppermute | solution.py:502
  34.5 3.4 %collective-permute-start.13 = (f32[88,128]{1,0:T(8,128)S(1)}, f32[88,128]{1,0:T(8,128)S(1)}, u32[]{:S(2)}, u32[]{:S(2)}) collective-permute-start(f32[88,128]{1,0:T(8,128)S(1)} %add.22), channel_id=1, source_target_pairs={{0,12},{1,13},{2,14},{3,15},{4,8},{5,9},{6,10},{7,11},{8,4},{9,5},... | collective-permute-start | bytes 135176 | tf_op jit(solution)/shard_map/ppermute | solution.py:502
  37.9 1.7 %collective-permute-done.13 = f32[88,128]{1,0:T(8,128)S(1)} collective-permute-done((f32[88,128]{1,0:T(8,128)S(1)}, f32[88,128]{1,0:T(8,128)S(1)}, u32[]{:S(2)}, u32[]{:S(2)}) %collective-permute-start.13) | collective-permute-done | bytes 45088 | tf_op jit(solution)/shard_map/ppermute | solution.py:502
  39.6 0.4 collective-permute-start.14
  40.7 0.2 collective-permute-done.14.other_ref
  41.0 6.0 %shard_map.63 = (f32[4,16,2048]{2,1,0:T(8,128)}, f32[96,128]{1,0:T(8,128)}, f32[128,128]{1,0:T(8,128)}) custom-call(f32[1]{0:T(128)S(6)} %add.18.shift_ref, bf16[1024,256]{1,0:T(8,128)(2,1)S(1)} %get-tuple-element.19.q_ref, f32[1024,128]{1,0:T(8,128)S(1)} %get-tuple-element.32.s_ref, f32[88,128]{1,0:T(8,128)S(1)} %add.23.mine_ref, ...), custom_call_target="tpu_custom_call" | custom-call | tf_op jit(solution)/shard_map/pallas_call | solution.py:596
  (6 shorter events, 0.1 us)
Async XLA Ops:
  2.1 12.4 %copy-start = (f32[4,16,1536]{2,1,0:T(8,128)S(1)}, f32[4,16,1536]{2,1,0:T(8,128)}, u32[]{:S(2)}) copy-start(f32[4,16,1536]{2,1,0:T(8,128)} %prior_hbm.1) | copy-start | bytes 1179652
  2.2 5.3 %collective-permute-start = (f32[4,16,256]{2,1,0:T(8,128)S(1)}, f32[4,16,256]{2,1,0:T(8,128)S(1)}, u32[]{:S(2)}, u32[]{:S(2)}) collective-permute-start(f32[4,16,256]{2,1,0:T(8,128)S(1)} %get-tuple-element.21), channel_id=1, source_target_pairs={{0,1},{8,9},{16,17},{24,25},{1,0},{9,8},{17,16},{25,24},{2,3},{10,... | collective-permute-start | bytes 196616 | tf_op jit(solution)/shard_map/ppermute | solution.py:528
  5.2 13.3 %collective-permute-start.3 = (f32[4,16,640]{2,1,0:T(8,128)S(1)}, f32[4,16,640]{2,1,0:T(8,128)S(1)}, u32[]{:S(2)}, u32[]{:S(2)}) collective-permute-start(f32[4,16,640]{2,1,0:T(8,128)S(1)} %get-tuple-element.20.field_ref), channel_id=1, source_target_pairs={{0,8},{1,9},{8,0},{9,1},{16,24},{17,25},{24,16},{25,17},{2,10},{3,... | collective-permute-start | bytes 491528 | tf_op jit(solution)/shard_map/ppermute | solution.py:528
  5.2 13.3 %collective-permute-start.4 = (f32[4,16,640]{2,1,0:T(8,128)S(1)}, f32[4,16,640]{2,1,0:T(8,128)S(1)}, u32[]{:S(2)}, u32[]{:S(2)}) collective-permute-start(f32[4,16,640]{2,1,0:T(8,128)S(1)} %get-tuple-element.20.field_ref), channel_id=1, source_target_pairs={{8,16},{9,17},{16,8},{17,9},{0,1},{1,0},{24,25},{25,24},{10,18},{1... | collective-permute-start | bytes 491528 | tf_op jit(solution)/shard_map/ppermute | solution.py:528
  7.6 6.6 %collective-permute-start.5 = (f32[3,16,384]{2,1,0:T(8,128)S(1)}, f32[3,16,384]{2,1,0:T(8,128)S(1)}, u32[]{:S(2)}, u32[]{:S(2)}) collective-permute-start(f32[3,16,384]{2,1,0:T(8,128)S(1)} %get-tuple-element.26), channel_id=1, source_target_pairs={{0,8},{1,9},{8,0},{9,1},{16,24},{17,25},{24,16},{25,17},{2,10},{3,... | collective-permute-start | bytes 221192 | tf_op jit(solution)/shard_map/ppermute | solution.py:528
  7.6 4.7 %collective-permute-start.1 = (f32[4,4,896]{2,1,0:T(4,128)S(1)}, f32[4,4,896]{2,1,0:T(4,128)S(1)}, u32[]{:S(2)}, u32[]{:S(2)}) collective-permute-start(f32[4,4,896]{2,1,0:T(4,128)S(1)} %get-tuple-element.23), channel_id=1, source_target_pairs={{0,2},{8,10},{16,18},{24,26},{2,0},{10,8},{18,16},{26,24},{4,6},{1... | collective-permute-start | bytes 172040 | tf_op jit(solution)/shard_map/ppermute | solution.py:528
  9.8 2.5 %collective-permute-start.2 = (f32[4,4,896]{2,1,0:T(4,128)S(1)}, f32[4,4,896]{2,1,0:T(4,128)S(1)}, u32[]{:S(2)}, u32[]{:S(2)}) collective-permute-start(f32[4,4,896]{2,1,0:T(4,128)S(1)} %get-tuple-element.24), channel_id=1, source_target_pairs={{2,4},{10,12},{18,20},{26,28},{4,2},{12,10},{20,18},{28,26},{0,8},... | collective-permute-start | bytes 172040 | tf_op jit(solution)/shard_map/ppermute | solution.py:528
  12.4 6.2 %collective-permute-start.7 = (f32[3,8,896]{2,1,0:T(8,128)S(1)}, f32[3,8,896]{2,1,0:T(8,128)S(1)}, u32[]{:S(2)}, u32[]{:S(2)}) collective-permute-start(f32[3,8,896]{2,1,0:T(8,128)S(1)} %get-tuple-element.28), channel_id=1, source_target_pairs={{0,8},{1,9},{8,0},{9,1},{16,24},{17,25},{24,16},{25,17},{2,10},{3,... | collective-permute-start | bytes 258056 | tf_op jit(solution)/shard_map/ppermute | solution.py:528
  12.4 6.1 %collective-permute-start.8 = (f32[3,8,896]{2,1,0:T(8,128)S(1)}, f32[3,8,896]{2,1,0:T(8,128)S(1)}, u32[]{:S(2)}, u32[]{:S(2)}) collective-permute-start(f32[3,8,896]{2,1,0:T(8,128)S(1)} %get-tuple-element.29), channel_id=1, source_target_pairs={{8,16},{9,17},{16,8},{17,9},{0,1},{1,0},{24,25},{25,24},{10,18},{1... | collective-permute-start | bytes 258056 | tf_op jit(solution)/shard_map/ppermute | solution.py:528
  14.2 4.4 %collective-permute-start.6 = (f32[3,16,384]{2,1,0:T(8,128)S(1)}, f32[3,16,384]{2,1,0:T(8,128)S(1)}, u32[]{:S(2)}, u32[]{:S(2)}) collective-permute-start(f32[3,16,384]{2,1,0:T(8,128)S(1)} %get-tuple-element.27), channel_id=1, source_target_pairs={{8,16},{9,17},{16,8},{17,9},{0,1},{1,0},{24,25},{25,24},{10,18},{1... | collective-permute-start | bytes 221192 | tf_op jit(solution)/shard_map/ppermute | solution.py:528
  21.5 1.3 %collective-permute-start.9 = (f32[88,128]{1,0:T(8,128)S(1)}, f32[88,128]{1,0:T(8,128)S(1)}, u32[]{:S(2)}, u32[]{:S(2)}) collective-permute-start(f32[88,128]{1,0:T(8,128)S(1)} %get-tuple-element.34), channel_id=1, source_target_pairs={{0,8},{1,9},{2,10},{3,11},{4,12},{5,13},{6,14},{7,15},{8,0},{9,1},... | collective-permute-start | bytes 135176 | tf_op jit(solution)/shard_map/ppermute | solution.py:502
  22.8 3.7 %collective-permute-start.10 = (f32[88,128]{1,0:T(8,128)S(1)}, f32[88,128]{1,0:T(8,128)S(1)}, u32[]{:S(2)}, u32[]{:S(2)}) collective-permute-start(f32[88,128]{1,0:T(8,128)S(1)} %add.19), channel_id=1, source_target_pairs={{0,24},{1,25},{2,26},{3,27},{4,28},{5,29},{6,30},{7,31},{8,16},{9,... | collective-permute-start | bytes 135176 | tf_op jit(solution)/shard_map/ppermute | solution.py:502
  26.5 3.7 %collective-permute-start.11 = (f32[88,128]{1,0:T(8,128)S(1)}, f32[88,128]{1,0:T(8,128)S(1)}, u32[]{:S(2)}, u32[]{:S(2)}) collective-permute-start(f32[88,128]{1,0:T(8,128)S(1)} %add.20), channel_id=1, source_target_pairs={{0,9},{1,8},{2,11},{3,10},{4,13},{5,12},{6,15},{7,14},{8,1},{9,0},... | collective-permute-start | bytes 135176 | tf_op jit(solution)/shard_map/ppermute | solution.py:502
  30.3 4.2 %collective-permute-start.12 = (f32[88,128]{1,0:T(8,128)S(1)}, f32[88,128]{1,0:T(8,128)S(1)}, u32[]{:S(2)}, u32[]{:S(2)}) collective-permute-start(f32[88,128]{1,0:T(8,128)S(1)} %add.21), channel_id=1, source_target_pairs={{0,10},{1,11},{2,8},{3,9},{4,14},{5,15},{6,12},{7,13},{8,2},{9,3},... | collective-permute-start | bytes 135176 | tf_op jit(solution)/shard_map/ppermute | solution.py:502
  34.5 5.1 %collective-permute-start.13 = (f32[88,128]{1,0:T(8,128)S(1)}, f32[88,128]{1,0:T(8,128)S(1)}, u32[]{:S(2)}, u32[]{:S(2)}) collective-permute-start(f32[88,128]{1,0:T(8,128)S(1)} %add.22), channel_id=1, source_target_pairs={{0,12},{1,13},{2,14},{3,15},{4,8},{5,9},{6,10},{7,11},{8,4},{9,5},... | collective-permute-start | bytes 135176 | tf_op jit(solution)/shard_map/ppermute | solution.py:502
  39.6 1.3 %collective-permute-start.14 = (f32[88,128]{1,0:T(8,128)S(1)}, f32[88,128]{1,0:T(8,128)S(1)}, u32[]{:S(2)}, u32[]{:S(2)}) collective-permute-start(f32[88,128]{1,0:T(8,128)S(1)} %add.23.mine_ref), channel_id=1, source_target_pairs={{0,8},{1,9},{2,10},{3,11},{4,12},{5,13},{6,14},{7,15},{8,0},{9,1},... | collective-permute-start | bytes 135176 | tf_op jit(solution)/shard_map/ppermute | solution.py:502

commit v7 on v6

--- a/solution.py
+++ b/solution.py
@@ -19,6 +19,7 @@
 DEGREE = 6.0
 LANES = 128
 SUBLANES = 8
+EARLY = 4
 F32 = jnp.float32
 BF16 = jnp.bfloat16
 AXES = ("gx", "gy", "gz")
@@ -158,7 +159,7 @@
     )
 
 
-def prior_body(prior_ref, q_ref, parts_ref, inner_ref):
+def prior_body(prior_ref, q_ref, parts_ref, inner_ref, selector_ref):
     size_x, size_y, width = prior_ref.shape
     size_z = width // BASIS
     lane = lane_of((size_y, LANES))
@@ -175,6 +176,16 @@
                 at = (i * size_z + 4 * q + r) * size_y
                 q_ref[at : at + size_y] = jnp.where(lane < BASIS, rows[r], 0.0)
     rows = q_ref[...]
+    field = selector_ref.shape[2]
+    source = row_of((LANES, field))
+    position = lane_of((LANES, field)) // BLOCK
+    place = jnp.where(
+        position < size_z,
+        position,
+        jnp.where(position < size_z + POWERS, position + 2 * size_z, position + 3 * size_z - 2 * POWERS),
+    )
+    for d in range(3):
+        selector_ref[d] = jnp.where(source == place + d * size_z, 1.0, 0.0).astype(BF16)
     inner_ref[...] = contract(rows, rows)[:BASIS]
     parts_ref[:, :LANES], parts_ref[:, LANES:] = halves(rows)
 
@@ -204,7 +215,7 @@
     return product[:, :columns] + product[:, columns:]
 
 
-def columns_body(size_z, own_ref, near_ref, far_ref, near_side_ref, far_side_ref, near_rest_ref, far_rest_ref, q_ref, inner_ref, s_ref, keep_ref, give_ref, joined, coupling, diagonal, levels, sums, q_parts, s_parts):
+def columns_body(size_z, own_ref, near_ref, far_ref, near_side_ref, far_side_ref, near_rest_ref, far_rest_ref, q_ref, inner_ref, selector_ref, s_ref, keep_ref, give_ref, joined, coupling, diagonal, levels, sums, q_parts, s_parts):
     size_x, rows, width = own_ref.shape
     size_y = rows - 2 * POWERS
     field = width - LANES
@@ -232,15 +243,8 @@
 
     weights = joined[:, :, field:].reshape(-1, LANES)
     weights = jnp.concatenate(halves(weights * (1.0 / math.sqrt(DEGREE))), axis=1)
-    source = row_of((2 * LANES, field))
-    position = lane_of((2 * LANES, field)) // BLOCK
-    place = jnp.where(
-        position < size_z,
-        position,
-        jnp.where(position < size_z + POWERS, position + 2 * size_z, position + 3 * size_z - 2 * POWERS),
-    )
     for d in range(3):
-        selector = jnp.where(source % LANES == place + d * size_z, 1.0, 0.0).astype(BF16)
+        selector = jnp.concatenate([selector_ref[d]] * 2, axis=0)
         spread = jnp.dot(weights, selector, preferred_element_type=F32)
         coupling[d] = spread.reshape(planes, rows, field)
     row_last = (row_of((rows, field)) == size_y - 1) & last_on("gy")
@@ -384,9 +388,14 @@
         if stop == count:
             break
         for k in panel:
+            factors = [entry(rows_a[k], 0, stop + j) for j in panel]
             for j in panel:
-                following[j] = following[j] - entry(rows_a[k], 0, stop + j) * rows_a[k]
-        rows_a, a = following, entries(following, stop)
+                following[j] = following[j] - factors[j] * rows_a[k]
+            if k + 1 == EARLY:
+                a = entries(following, stop)
+            elif k + 1 > EARLY:
+                a = {(i, j): value - factors[i] * factors[j] for (i, j), value in a.items()}
+        rows_a = following
         left, right = split_rows(jnp.concatenate([out_a, out_b], axis=1))
         update = lax.dot_general(left[:, :count], right, (((0,), (0,)), ((), ())), preferred_element_type=F32)
         after = stop + SUBLANES
@@ -558,9 +567,14 @@
     halos = exchange(faces[0], faces[-1], "gz", "gx") if faces else []
     planes_x = filled(exchange(field, field, "gx", "gz"), field)
     degree_shift = spectral_shift + DEGREE
-    prior_rows, prior_parts, inner = kernel_call(
+    prior_rows, prior_parts, inner, selector = kernel_call(
         prior_body,
-        [(cell_local, LANES), jax.ShapeDtypeStruct((cell_local, 2 * LANES), BF16), (BASIS, LANES)],
+        [
+            (cell_local, LANES),
+            jax.ShapeDtypeStruct((cell_local, 2 * LANES), BF16),
+            (BASIS, LANES),
+            jax.ShapeDtypeStruct((3, LANES, own + 2 * LANES), BF16),
+        ],
         cost=pl.CostEstimate(flops=6 * 2 * cell_local * LANES * LANES, bytes_accessed=4 * prior_basis.size, transcendentals=0),
     )(prior_basis)
     width = own + 3 * LANES
@@ -589,7 +603,7 @@
             pltpu.VMEM((cell_local, 2 * LANES), BF16),
             pltpu.VMEM((cell_local, 2 * WIDE), BF16),
         ],
-    )(long, *planes_x, *sides_x, *rests, prior_rows, inner)
+    )(long, *planes_x, *sides_x, *rests, prior_rows, inner, selector)
 
     total, other = reduced(keep, give)
 

time: 47.1 us -> 46.8 us (level)
  no operation moved by 1% of the time
where the time goes in v7:
time: 46.8 us; the launch traced here: 46.6 us
  waiting for transfers between devices  17.9 us (38%)
  starting transfers between devices  16.1 us (34%)
  Pallas kernels  11.2 us (24%)
  between operations  1.37 us (3%)
    ppermute x6, waiting for transfers between devices, swap(): return lax.ppermute(values, AXES, links)  10.4 us
    ppermute x6, starting transfers between devices, swap(): return lax.ppermute(values, AXES, links)  8.33 us
    ppermute x9, starting transfers between devices, exchange(): lax.ppermute(value, axes, [(place(source), place(target)) for source, tar...  7.74 us
    ppermute x9, waiting for transfers between devices, exchange(): lax.ppermute(value, axes, [(place(source), place(target)) for source, tar...  7.54 us
    pallas_call x1, Pallas kernels, cycle(): pl.pallas_call(functools.partial(finish_body, 1.0 / cell_count), in_specs...  5.8 us
    pallas_call x1, Pallas kernels, cycle(): kernel_call(functools.partial(columns_body, size_z), [(cell_local, WIDE),...  2.84 us
    pallas_call x1, Pallas kernels, cycle(): kernel_call(pack_body, [(size_x, size_y, own + LANES)] + [(size_x, size_y...  1.51 us
  transfers between devices with their start and end apart: 15, of which 9 were waited for; matrix products, arithmetic and copies ran while one was open for 0% of the time, Pallas kernels for 2%

profile of v7, /device:TPU:0, one launch (start us, length us, event | category | flops | bytes accessed | tf_op | source)
XLA Modules:
  0.0 46.6 jit_solution(16527946188286785397)
XLA Ops:
  0.6 1.5 %shard_map.59 = (f32[4,16,640]{2,1,0:T(8,128)S(1)}, f32[4,16,256]{2,1,0:T(8,128)S(1)}) custom-call(f32[4,16,1536]{2,1,0:T(8,128)} %prior_hbm.1, f32[3,4,16,16]{3,2,1,0:T(8,128)} %weights_hbm.1), custom_call_target="tpu_custom_call" | custom-call | tf_op jit(solution)/shard_map/pallas_call | solution.py:556
  2.1 0.0 copy-start
  2.2 3.1 %collective-permute-start = (f32[4,16,256]{2,1,0:T(8,128)S(1)}, f32[4,16,256]{2,1,0:T(8,128)S(1)}, u32[]{:S(2)}, u32[]{:S(2)}) collective-permute-start(f32[4,16,256]{2,1,0:T(8,128)S(1)} %get-tuple-element.22), channel_id=1, source_target_pairs={{0,1},{8,9},{16,17},{24,25},{1,0},{9,8},{17,16},{25,24},{2,3},{10,... | collective-permute-start | bytes 196616 | tf_op jit(solution)/shard_map/ppermute | solution.py:537
  5.2 0.0 collective-permute-start.3
  5.2 0.2 collective-permute-start.4
  5.4 2.1 %collective-permute-done.refs_0_ = f32[4,16,256]{2,1,0:T(8,128)S(1)} collective-permute-done((f32[4,16,256]{2,1,0:T(8,128)S(1)}, f32[4,16,256]{2,1,0:T(8,128)S(1)}, u32[]{:S(2)}, u32[]{:S(2)}) %collective-permute-start) | collective-permute-done | bytes 65568 | tf_op jit(solution)/shard_map/ppermute | solution.py:537
  7.5 0.1 shard_map.60
  7.6 0.1 collective-permute-start.5
  7.6 2.1 %collective-permute-start.1 = (f32[4,4,896]{2,1,0:T(4,128)S(1)}, f32[4,4,896]{2,1,0:T(4,128)S(1)}, u32[]{:S(2)}, u32[]{:S(2)}) collective-permute-start(f32[4,4,896]{2,1,0:T(4,128)S(1)} %get-tuple-element.24), channel_id=1, source_target_pairs={{0,2},{8,10},{16,18},{24,26},{2,0},{10,8},{18,16},{26,24},{4,6},{1... | collective-permute-start | bytes 172040 | tf_op jit(solution)/shard_map/ppermute | solution.py:537
  9.8 0.2 collective-permute-start.2
  9.9 2.4 %collective-permute-done.1.first_ref = f32[4,4,896]{2,1,0:T(4,128)S(1)} collective-permute-done((f32[4,4,896]{2,1,0:T(4,128)S(1)}, f32[4,4,896]{2,1,0:T(4,128)S(1)}, u32[]{:S(2)}, u32[]{:S(2)}) %collective-permute-start.1) | collective-permute-done | bytes 57376 | tf_op jit(solution)/shard_map/ppermute | solution.py:537
  12.3 0.0 collective-permute-done.2.second_ref
  12.4 0.1 collective-permute-start.7
  12.4 1.8 %collective-permute-start.8 = (f32[3,8,896]{2,1,0:T(8,128)S(1)}, f32[3,8,896]{2,1,0:T(8,128)S(1)}, u32[]{:S(2)}, u32[]{:S(2)}) collective-permute-start(f32[3,8,896]{2,1,0:T(8,128)S(1)} %get-tuple-element.30), channel_id=1, source_target_pairs={{8,16},{9,17},{16,8},{17,9},{0,1},{1,0},{24,25},{25,24},{10,18},{1... | collective-permute-start | bytes 258056 | tf_op jit(solution)/shard_map/ppermute | solution.py:537
  14.2 0.0 collective-permute-done.5.near_side_ref
  14.2 0.3 collective-permute-start.6
  14.5 0.0 copy-done
  14.5 0.9 %shard_map.58 = (f32[1024,128]{1,0:T(8,128)S(1)}, bf16[1024,256]{1,0:T(8,128)(2,1)S(1)}, f32[96,128]{1,0:T(8,128)S(1)}, bf16[3,128,768]{2,1,0:T(8,128)(2,1)S(1)}) custom-call(f32[4,16,1536]{2,1,0:T(8,128)S(1)} %copy-done), custom_call_target="tpu_custom_call" | custom-call | flops 201326592 | bytes 393216 | tf_op jit(solution)/shard_map/pallas_call | solution.py:570
  15.5 3.1 %collective-permute-done.6.far_side_ref = f32[3,16,384]{2,1,0:T(8,128)S(1)} collective-permute-done((f32[3,16,384]{2,1,0:T(8,128)S(1)}, f32[3,16,384]{2,1,0:T(8,128)S(1)}, u32[]{:S(2)}, u32[]{:S(2)}) %collective-permute-start.6) | collective-permute-done | bytes 73760 | tf_op jit(solution)/shard_map/ppermute | solution.py:537
  18.5 0.0 collective-permute-done.3.near_ref
  18.5 0.0 collective-permute-done.4.far_ref
  18.5 0.0 collective-permute-done.7.near_rest_ref
  18.6 0.0 collective-permute-done.8.far_rest_ref
  18.6 2.8 %shard_map.62 = (f32[1024,128]{1,0:T(8,128)S(1)}, f32[88,128]{1,0:T(8,128)S(1)}, f32[88,128]{1,0:T(8,128)S(1)}) custom-call(f32[4,24,896]{2,1,0:T(8,128)S(1)} %get-tuple-element.26.own_ref, f32[4,16,640]{2,1,0:T(8,128)S(1)} %collective-permute-done.3.near_ref, f32[4,16,640]{2,1,0:T(8,128)S(1)} %collective-permute-done.4.far_ref, ...), custom_call_target="tpu_custom_call" | custom-call | tf_op jit(solution)/shard_map/pallas_call | solution.py:594
  21.4 0.1 collective-permute-start.9
  21.5 1.2 %collective-permute-done.9 = f32[88,128]{1,0:T(8,128)S(1)} collective-permute-done((f32[88,128]{1,0:T(8,128)S(1)}, f32[88,128]{1,0:T(8,128)S(1)}, u32[]{:S(2)}, u32[]{:S(2)}) %collective-permute-start.9) | collective-permute-done | bytes 45088 | tf_op jit(solution)/shard_map/ppermute | solution.py:511
  22.7 0.8 %collective-permute-start.10 = (f32[88,128]{1,0:T(8,128)S(1)}, f32[88,128]{1,0:T(8,128)S(1)}, u32[]{:S(2)}, u32[]{:S(2)}) collective-permute-start(f32[88,128]{1,0:T(8,128)S(1)} %add.19), channel_id=1, source_target_pairs={{0,24},{1,25},{2,26},{3,27},{4,28},{5,29},{6,30},{7,31},{8,16},{9,... | collective-permute-start | bytes 135176 | tf_op jit(solution)/shard_map/ppermute | solution.py:511
  23.5 2.9 %collective-permute-done.10 = f32[88,128]{1,0:T(8,128)S(1)} collective-permute-done((f32[88,128]{1,0:T(8,128)S(1)}, f32[88,128]{1,0:T(8,128)S(1)}, u32[]{:S(2)}, u32[]{:S(2)}) %collective-permute-start.10) | collective-permute-done | bytes 45088 | tf_op jit(solution)/shard_map/ppermute | solution.py:511
  26.4 1.2 %collective-permute-start.11 = (f32[88,128]{1,0:T(8,128)S(1)}, f32[88,128]{1,0:T(8,128)S(1)}, u32[]{:S(2)}, u32[]{:S(2)}) collective-permute-start(f32[88,128]{1,0:T(8,128)S(1)} %add.20), channel_id=1, source_target_pairs={{0,9},{1,8},{2,11},{3,10},{4,13},{5,12},{6,15},{7,14},{8,1},{9,0},... | collective-permute-start | bytes 135176 | tf_op jit(solution)/shard_map/ppermute | solution.py:511
  27.6 2.6 %collective-permute-done.11 = f32[88,128]{1,0:T(8,128)S(1)} collective-permute-done((f32[88,128]{1,0:T(8,128)S(1)}, f32[88,128]{1,0:T(8,128)S(1)}, u32[]{:S(2)}, u32[]{:S(2)}) %collective-permute-start.11) | collective-permute-done | bytes 45088 | tf_op jit(solution)/shard_map/ppermute | solution.py:511
  30.2 2.5 %collective-permute-start.12 = (f32[88,128]{1,0:T(8,128)S(1)}, f32[88,128]{1,0:T(8,128)S(1)}, u32[]{:S(2)}, u32[]{:S(2)}) collective-permute-start(f32[88,128]{1,0:T(8,128)S(1)} %add.21), channel_id=1, source_target_pairs={{0,10},{1,11},{2,8},{3,9},{4,14},{5,15},{6,12},{7,13},{8,2},{9,3},... | collective-permute-start | bytes 135176 | tf_op jit(solution)/shard_map/ppermute | solution.py:511
  32.7 1.8 %collective-permute-done.12 = f32[88,128]{1,0:T(8,128)S(1)} collective-permute-done((f32[88,128]{1,0:T(8,128)S(1)}, f32[88,128]{1,0:T(8,128)S(1)}, u32[]{:S(2)}, u32[]{:S(2)}) %collective-permute-start.12) | collective-permute-done | bytes 45088 | tf_op jit(solution)/shard_map/ppermute | solution.py:511
  34.4 3.3 %collective-permute-start.13 = (f32[88,128]{1,0:T(8,128)S(1)}, f32[88,128]{1,0:T(8,128)S(1)}, u32[]{:S(2)}, u32[]{:S(2)}) collective-permute-start(f32[88,128]{1,0:T(8,128)S(1)} %add.22), channel_id=1, source_target_pairs={{0,12},{1,13},{2,14},{3,15},{4,8},{5,9},{6,10},{7,11},{8,4},{9,5},... | collective-permute-start | bytes 135176 | tf_op jit(solution)/shard_map/ppermute | solution.py:511
  37.8 1.7 %collective-permute-done.13 = f32[88,128]{1,0:T(8,128)S(1)} collective-permute-done((f32[88,128]{1,0:T(8,128)S(1)}, f32[88,128]{1,0:T(8,128)S(1)}, u32[]{:S(2)}, u32[]{:S(2)}) %collective-permute-start.13) | collective-permute-done | bytes 45088 | tf_op jit(solution)/shard_map/ppermute | solution.py:511
  39.5 0.4 collective-permute-start.14
  40.6 0.2 collective-permute-done.14.other_ref
  40.8 5.8 %shard_map.63 = (f32[4,16,2048]{2,1,0:T(8,128)}, f32[96,128]{1,0:T(8,128)}, f32[128,128]{1,0:T(8,128)}) custom-call(f32[1]{0:T(128)S(6)} %add.18.shift_ref, bf16[1024,256]{1,0:T(8,128)(2,1)S(1)} %get-tuple-element.20.q_ref, f32[1024,128]{1,0:T(8,128)S(1)} %get-tuple-element.34.s_ref, f32[88,128]{1,0:T(8,128)S(1)} %add.23.mine_ref, ...), custom_call_target="tpu_custom_call" | custom-call | tf_op jit(solution)/shard_map/pallas_call | solution.py:610
  (6 shorter events, 0.1 us)
Async XLA Ops:
  2.1 12.4 %copy-start = (f32[4,16,1536]{2,1,0:T(8,128)S(1)}, f32[4,16,1536]{2,1,0:T(8,128)}, u32[]{:S(2)}) copy-start(f32[4,16,1536]{2,1,0:T(8,128)} %prior_hbm.1) | copy-start | bytes 1179652
  2.2 5.3 %collective-permute-start = (f32[4,16,256]{2,1,0:T(8,128)S(1)}, f32[4,16,256]{2,1,0:T(8,128)S(1)}, u32[]{:S(2)}, u32[]{:S(2)}) collective-permute-start(f32[4,16,256]{2,1,0:T(8,128)S(1)} %get-tuple-element.22), channel_id=1, source_target_pairs={{0,1},{8,9},{16,17},{24,25},{1,0},{9,8},{17,16},{25,24},{2,3},{10,... | collective-permute-start | bytes 196616 | tf_op jit(solution)/shard_map/ppermute | solution.py:537
  5.2 13.3 %collective-permute-start.3 = (f32[4,16,640]{2,1,0:T(8,128)S(1)}, f32[4,16,640]{2,1,0:T(8,128)S(1)}, u32[]{:S(2)}, u32[]{:S(2)}) collective-permute-start(f32[4,16,640]{2,1,0:T(8,128)S(1)} %get-tuple-element.21.field_ref), channel_id=1, source_target_pairs={{0,8},{1,9},{8,0},{9,1},{16,24},{17,25},{24,16},{25,17},{2,10},{3,... | collective-permute-start | bytes 491528 | tf_op jit(solution)/shard_map/ppermute | solution.py:537
  5.2 13.3 %collective-permute-start.4 = (f32[4,16,640]{2,1,0:T(8,128)S(1)}, f32[4,16,640]{2,1,0:T(8,128)S(1)}, u32[]{:S(2)}, u32[]{:S(2)}) collective-permute-start(f32[4,16,640]{2,1,0:T(8,128)S(1)} %get-tuple-element.21.field_ref), channel_id=1, source_target_pairs={{8,16},{9,17},{16,8},{17,9},{0,1},{1,0},{24,25},{25,24},{10,18},{1... | collective-permute-start | bytes 491528 | tf_op jit(solution)/shard_map/ppermute | solution.py:537
  7.6 6.6 %collective-permute-start.5 = (f32[3,16,384]{2,1,0:T(8,128)S(1)}, f32[3,16,384]{2,1,0:T(8,128)S(1)}, u32[]{:S(2)}, u32[]{:S(2)}) collective-permute-start(f32[3,16,384]{2,1,0:T(8,128)S(1)} %get-tuple-element.27), channel_id=1, source_target_pairs={{0,8},{1,9},{8,0},{9,1},{16,24},{17,25},{24,16},{25,17},{2,10},{3,... | collective-permute-start | bytes 221192 | tf_op jit(solution)/shard_map/ppermute | solution.py:537
  7.6 4.7 %collective-permute-start.1 = (f32[4,4,896]{2,1,0:T(4,128)S(1)}, f32[4,4,896]{2,1,0:T(4,128)S(1)}, u32[]{:S(2)}, u32[]{:S(2)}) collective-permute-start(f32[4,4,896]{2,1,0:T(4,128)S(1)} %get-tuple-element.24), channel_id=1, source_target_pairs={{0,2},{8,10},{16,18},{24,26},{2,0},{10,8},{18,16},{26,24},{4,6},{1... | collective-permute-start | bytes 172040 | tf_op jit(solution)/shard_map/ppermute | solution.py:537
  9.8 2.5 %collective-permute-start.2 = (f32[4,4,896]{2,1,0:T(4,128)S(1)}, f32[4,4,896]{2,1,0:T(4,128)S(1)}, u32[]{:S(2)}, u32[]{:S(2)}) collective-permute-start(f32[4,4,896]{2,1,0:T(4,128)S(1)} %get-tuple-element.25), channel_id=1, source_target_pairs={{2,4},{10,12},{18,20},{26,28},{4,2},{12,10},{20,18},{28,26},{0,8},... | collective-permute-start | bytes 172040 | tf_op jit(solution)/shard_map/ppermute | solution.py:537
  12.4 6.2 %collective-permute-start.7 = (f32[3,8,896]{2,1,0:T(8,128)S(1)}, f32[3,8,896]{2,1,0:T(8,128)S(1)}, u32[]{:S(2)}, u32[]{:S(2)}) collective-permute-start(f32[3,8,896]{2,1,0:T(8,128)S(1)} %get-tuple-element.29), channel_id=1, source_target_pairs={{0,8},{1,9},{8,0},{9,1},{16,24},{17,25},{24,16},{25,17},{2,10},{3,... | collective-permute-start | bytes 258056 | tf_op jit(solution)/shard_map/ppermute | solution.py:537
  12.4 6.1 %collective-permute-start.8 = (f32[3,8,896]{2,1,0:T(8,128)S(1)}, f32[3,8,896]{2,1,0:T(8,128)S(1)}, u32[]{:S(2)}, u32[]{:S(2)}) collective-permute-start(f32[3,8,896]{2,1,0:T(8,128)S(1)} %get-tuple-element.30), channel_id=1, source_target_pairs={{8,16},{9,17},{16,8},{17,9},{0,1},{1,0},{24,25},{25,24},{10,18},{1... | collective-permute-start | bytes 258056 | tf_op jit(solution)/shard_map/ppermute | solution.py:537
  14.2 4.4 %collective-permute-start.6 = (f32[3,16,384]{2,1,0:T(8,128)S(1)}, f32[3,16,384]{2,1,0:T(8,128)S(1)}, u32[]{:S(2)}, u32[]{:S(2)}) collective-permute-start(f32[3,16,384]{2,1,0:T(8,128)S(1)} %get-tuple-element.28), channel_id=1, source_target_pairs={{8,16},{9,17},{16,8},{17,9},{0,1},{1,0},{24,25},{25,24},{10,18},{1... | collective-permute-start | bytes 221192 | tf_op jit(solution)/shard_map/ppermute | solution.py:537
  21.4 1.3 %collective-permute-start.9 = (f32[88,128]{1,0:T(8,128)S(1)}, f32[88,128]{1,0:T(8,128)S(1)}, u32[]{:S(2)}, u32[]{:S(2)}) collective-permute-start(f32[88,128]{1,0:T(8,128)S(1)} %get-tuple-element.36), channel_id=1, source_target_pairs={{0,8},{1,9},{2,10},{3,11},{4,12},{5,13},{6,14},{7,15},{8,0},{9,1},... | collective-permute-start | bytes 135176 | tf_op jit(solution)/shard_map/ppermute | solution.py:511
  22.7 3.7 %collective-permute-start.10 = (f32[88,128]{1,0:T(8,128)S(1)}, f32[88,128]{1,0:T(8,128)S(1)}, u32[]{:S(2)}, u32[]{:S(2)}) collective-permute-start(f32[88,128]{1,0:T(8,128)S(1)} %add.19), channel_id=1, source_target_pairs={{0,24},{1,25},{2,26},{3,27},{4,28},{5,29},{6,30},{7,31},{8,16},{9,... | collective-permute-start | bytes 135176 | tf_op jit(solution)/shard_map/ppermute | solution.py:511
  26.4 3.7 %collective-permute-start.11 = (f32[88,128]{1,0:T(8,128)S(1)}, f32[88,128]{1,0:T(8,128)S(1)}, u32[]{:S(2)}, u32[]{:S(2)}) collective-permute-start(f32[88,128]{1,0:T(8,128)S(1)} %add.20), channel_id=1, source_target_pairs={{0,9},{1,8},{2,11},{3,10},{4,13},{5,12},{6,15},{7,14},{8,1},{9,0},... | collective-permute-start | bytes 135176 | tf_op jit(solution)/shard_map/ppermute | solution.py:511
  30.2 4.2 %collective-permute-start.12 = (f32[88,128]{1,0:T(8,128)S(1)}, f32[88,128]{1,0:T(8,128)S(1)}, u32[]{:S(2)}, u32[]{:S(2)}) collective-permute-start(f32[88,128]{1,0:T(8,128)S(1)} %add.21), channel_id=1, source_target_pairs={{0,10},{1,11},{2,8},{3,9},{4,14},{5,15},{6,12},{7,13},{8,2},{9,3},... | collective-permute-start | bytes 135176 | tf_op jit(solution)/shard_map/ppermute | solution.py:511
  34.4 5.1 %collective-permute-start.13 = (f32[88,128]{1,0:T(8,128)S(1)}, f32[88,128]{1,0:T(8,128)S(1)}, u32[]{:S(2)}, u32[]{:S(2)}) collective-permute-start(f32[88,128]{1,0:T(8,128)S(1)} %add.22), channel_id=1, source_target_pairs={{0,12},{1,13},{2,14},{3,15},{4,8},{5,9},{6,10},{7,11},{8,4},{9,5},... | collective-permute-start | bytes 135176 | tf_op jit(solution)/shard_map/ppermute | solution.py:511
  39.5 1.3 %collective-permute-start.14 = (f32[88,128]{1,0:T(8,128)S(1)}, f32[88,128]{1,0:T(8,128)S(1)}, u32[]{:S(2)}, u32[]{:S(2)}) collective-permute-start(f32[88,128]{1,0:T(8,128)S(1)} %add.23.mine_ref), channel_id=1, source_target_pairs={{0,8},{1,9},{2,10},{3,11},{4,12},{5,13},{6,14},{7,15},{8,0},{9,1},... | collective-permute-start | bytes 135176 | tf_op jit(solution)/shard_map/ppermute | solution.py:511
